TPU v7x, 32 devices: a whole 2x2x4 slice. The times are simulated.
32 devices in a mesh: seq: 16 (over z, x, core), tp: 2 (over y).
Axes of the slice: x: 2, y: 2, z: 4, core: 2. Of those that a mesh axis runs over, the one named last changes fastest.
Arguments:
- tokens: bfloat16 [4, 1024, 2048], P(None, 'seq'), may hold values from -6 to 6
- cotangent: bfloat16 [4, 1024, 2048], P(None, 'seq'), may hold values from -6 to 6
- head_groups: int32 [4, 1024], P(None, 'seq'), may hold values from 1 to 4
- ffn_widths: int32 [4, 1024], P(None, 'seq'), may hold values from 1 to 4
- doc_lengths: int32 [4, 6], replicated, may hold values from 1 to 576, 1024 in all within a row
- first_gain: bfloat16 [2048], P('seq'), may hold values from 0.5 to 1.5
- first_shift: bfloat16 [2048], P('seq'), may hold values from -2 to 2
- router_weight: bfloat16 [8, 2048], P(None, 'seq'), may hold values from -0.125 to 0.125
- in_weight: bfloat16 [2048, 3, 16, 128], P('seq', None, 'tp'), may hold values from -0.125 to 0.125
- in_bias: bfloat16 [3, 16, 128], P(None, 'tp', 'seq'), may hold values from -2 to 2
- out_weight: bfloat16 [16, 128, 2048], P('tp', None, 'seq'), may hold values from -1 to 1
- out_bias: bfloat16 [2048], P('seq'), may hold values from -2 to 2
- second_gain: bfloat16 [2048], P('seq'), may hold values from 0.5 to 1.5
- second_shift: bfloat16 [2048], P('seq'), may hold values from -2 to 2
- up_weight: bfloat16 [2048, 8192], P('seq', 'tp'), may hold values from -0.125 to 0.125
- up_bias: bfloat16 [4, 2048], P('tp', 'seq'), may hold values from -3 to 3
- down_weight: bfloat16 [8192, 2048], P('tp', 'seq'), may hold values from -0.0625 to 0.0625
- down_bias: bfloat16 [2048], P('seq'), may hold values from -2 to 2
Outputs:
- block_out: bfloat16 [4, 1024, 2048], P(None, 'seq')
- tokens_grad: float32 [4, 1024, 2048], P(None, 'seq')
- grad_first_gain: float32 [2048], P('seq')
- grad_first_shift: float32 [2048], P('seq')
- grad_router: float32 [8, 2048], P(None, 'seq')
- grad_in_weight: float32 [2048, 3, 16, 128], P('seq', None, 'tp')
- grad_in_bias: float32 [3, 16, 128], P(None, 'tp', 'seq')
- grad_out_weight: float32 [16, 128, 2048], P('tp', None, 'seq')
- grad_out_bias: float32 [2048], P('seq')
- grad_second_gain: float32 [2048], P('seq')
- grad_second_shift: float32 [2048], P('seq')
- grad_up_weight: float32 [2048, 8192], P('seq', 'tp')
- grad_up_bias: float32 [4, 2048], P('tp', 'seq')
- grad_down_weight: float32 [8192, 2048], P('tp', 'seq')
- grad_down_bias: float32 [2048], P('seq')
Inputs may be any that keep to these rules, and one draw needn't show every extreme that they name: `doc_lengths`: each row holds the lengths of the 6 documents of one packed sequence in order; they sum to 1024, and the longest is exactly 576.
All inputs are finite; a program needn't handle non-finite values.
Results may differ from a plain program's by a relative error of at most 0.0095.
The roundings to bfloat16 on the way count: a program that leaves them out, or rounds other values in their place, can miss the bound.
Values may be sent and summed in bfloat16 or wider, within the bound.
No kernel may reach another device: no remote copies, remote signals or barrier semaphores. Data moves between devices by JAX's collectives and lax.ppermute only.
A program may use at most 640 MiB of HBM per device.

v0:
```python
import math

import jax
import jax.numpy as jnp
from jax import lax
from jax.sharding import PartitionSpec as P

HEADS = 16
HEAD_DIM = 128
FF = 8192
GROUPS = 4


EPSILON = 1e-05
HIGHEST = lax.Precision.HIGHEST


def norm_forward(rows, gain, shift):
    center = rows - jnp.mean(rows, axis=-1, keepdims=True)
    inverse = lax.rsqrt(jnp.mean(center * center, axis=-1, keepdims=True) + EPSILON)
    scaled = center * inverse
    return (scaled * gain + shift, scaled, inverse)


def norm_backward(upstream, scaled, inverse, gain):
    through = upstream * gain
    return inverse * (
        through
        - jnp.mean(through, axis=-1, keepdims=True)
        - scaled * jnp.mean(through * scaled, axis=-1, keepdims=True)
    )


def rotary_tables(positions):
    half_dim = HEAD_DIM // 2
    steps_up = jnp.arange(half_dim, dtype=jnp.float32) * (2.0 / HEAD_DIM)
    inverse = jnp.exp(-math.log(10000.0) * steps_up)
    angles = positions.astype(jnp.float32)[:, None] * inverse[None, :]
    angles = jnp.concatenate([angles, angles], axis=1)
    return (jnp.cos(angles), jnp.sin(angles))


def rotate(vectors, cosine, sine):
    half_dim = vectors.shape[-1] // 2
    turned = jnp.concatenate([-vectors[..., half_dim:], vectors[..., :half_dim]], axis=-1)
    return vectors * cosine[:, None, :] + turned * sine[:, None, :]


def rotate_back(grads, cosine, sine):
    half_dim = grads.shape[-1] // 2
    moved = grads * sine[:, None, :]
    turned = jnp.concatenate([moved[..., half_dim:], -moved[..., :half_dim]], axis=-1)
    return grads * cosine[:, None, :] + turned


def doc_index(lengths, positions):
    ends = jnp.cumsum(lengths)
    return jnp.sum((positions[:, None] >= ends[None, :]).astype(jnp.int32), axis=1)


def gate_logit_grad(prob, pick, gate_grad):
    chosen = jnp.sum(prob * pick, axis=-1, keepdims=True)
    return GROUPS * chosen * (pick - prob) * gate_grad[:, None]


def local(
    tokens,
    cotangent,
    head_groups,
    ffn_widths,
    doc_lengths,
    first_gain,
    first_shift,
    router_weight,
    in_weight,
    in_bias,
    out_weight,
    out_bias,
    second_gain,
    second_shift,
    up_weight,
    up_bias,
    down_weight,
    down_bias,
):
    seq_count = lax.axis_size("seq")
    seq_index = lax.axis_index("seq")
    tp_index = lax.axis_index("tp")
    gathered = (
        lax.all_gather(first_gain, "seq", axis=0, tiled=True),
        lax.all_gather(first_shift, "seq", axis=0, tiled=True),
        lax.all_gather(router_weight, "seq", axis=1, tiled=True),
        lax.all_gather(in_weight, "seq", axis=0, tiled=True),
        lax.all_gather(in_bias, "seq", axis=2, tiled=True),
        lax.all_gather(out_weight, "seq", axis=2, tiled=True),
        lax.all_gather(out_bias, "seq", axis=0, tiled=True),
        lax.all_gather(second_gain, "seq", axis=0, tiled=True),
        lax.all_gather(second_shift, "seq", axis=0, tiled=True),
        lax.all_gather(up_weight, "seq", axis=0, tiled=True),
        lax.all_gather(up_bias, "seq", axis=1, tiled=True),
        lax.all_gather(down_weight, "seq", axis=1, tiled=True),
        lax.all_gather(down_bias, "seq", axis=0, tiled=True),
    )
    (
        gain_one,
        shift_one,
        router_full,
        in_full,
        in_bias_full,
        out_full,
        out_bias_full,
        gain_two,
        shift_two,
        up_full,
        up_bias_full,
        down_full,
        down_bias_full,
    ) = gathered
    micro, tok_dev, width = tokens.shape
    local_heads = in_full.shape[2]
    head_dim = in_full.shape[3]
    inner = local_heads * head_dim
    local_units = up_full.shape[1]
    length = tok_dev * seq_count
    scale = HEAD_DIM ** (-0.5)
    gain_one_f = gain_one.astype(jnp.float32)
    shift_one_f = shift_one.astype(jnp.float32)
    gain_two_f = gain_two.astype(jnp.float32)
    shift_two_f = shift_two.astype(jnp.float32)
    out_bias_f = out_bias_full.astype(jnp.float32)
    down_bias_f = down_bias_full.astype(jnp.float32)
    router_wide = router_full.astype(jnp.float32)
    bias_in = in_bias_full.astype(jnp.float32)
    up_bias_vec = up_bias_full.reshape(local_units).astype(jnp.float32)
    in_matrix = in_full.reshape(width, 3 * inner)
    out_matrix = out_full.reshape(inner, width)
    positions_all = jnp.arange(length, dtype=jnp.int32)
    positions_local = seq_index * tok_dev + jnp.arange(tok_dev, dtype=jnp.int32)
    cosine, sine = rotary_tables(positions_local)
    head_ids = tp_index * local_heads + jnp.arange(local_heads, dtype=jnp.int32)
    unit_ids = tp_index * local_units + jnp.arange(local_units, dtype=jnp.int32)
    options = jnp.arange(GROUPS, dtype=jnp.int32)
    grad_gain_one = jnp.zeros((width,), jnp.float32)
    grad_shift_one = jnp.zeros((width,), jnp.float32)
    grad_router = jnp.zeros(router_full.shape, jnp.float32)
    grad_in = jnp.zeros((width, 3 * inner), jnp.float32)
    grad_in_bias = jnp.zeros(in_bias_full.shape, jnp.float32)
    grad_out = jnp.zeros((inner, width), jnp.float32)
    grad_out_bias = jnp.zeros((width,), jnp.float32)
    grad_gain_two = jnp.zeros((width,), jnp.float32)
    grad_shift_two = jnp.zeros((width,), jnp.float32)
    grad_up = jnp.zeros(up_full.shape, jnp.float32)
    grad_up_bias = jnp.zeros((local_units,), jnp.float32)
    grad_down = jnp.zeros(down_full.shape, jnp.float32)
    grad_down_bias = jnp.zeros((width,), jnp.float32)
    outputs = []
    input_grads = []
    for batch in range(micro):
        rows = tokens[batch].astype(jnp.float32)
        doc_all = doc_index(doc_lengths[batch], positions_all)
        doc_local = lax.dynamic_slice_in_dim(doc_all, seq_index * tok_dev, tok_dev, 0)
        allowed = (positions_all[None, :] <= positions_local[:, None]) & (
            doc_all[None, :] == doc_local[:, None]
        )
        head_active = (head_ids[None, :] // (HEADS // GROUPS) < head_groups[batch][:, None]).astype(
            jnp.float32
        )
        unit_active = (unit_ids[None, :] // (FF // GROUPS) < ffn_widths[batch][:, None]).astype(
            jnp.float32
        )
        normed, scaled_one, inverse_one = norm_forward(rows, gain_one_f, shift_one_f)
        normed_low = normed.astype(jnp.bfloat16)
        logits = jnp.dot(normed_low, router_full.T, preferred_element_type=jnp.float32)
        attn_prob = jax.nn.softmax(logits[:, :GROUPS], axis=-1)
        ffn_prob = jax.nn.softmax(logits[:, GROUPS:], axis=-1)
        attn_pick = (options[None, :] == head_groups[batch][:, None] - 1).astype(jnp.float32)
        ffn_pick = (options[None, :] == ffn_widths[batch][:, None] - 1).astype(jnp.float32)
        attn_gate = GROUPS * jnp.sum(attn_prob * attn_pick, axis=-1)
        ffn_gate = GROUPS * jnp.sum(ffn_prob * ffn_pick, axis=-1)
        projected = jnp.dot(normed_low, in_matrix, preferred_element_type=jnp.float32)
        projected = projected.reshape(tok_dev, 3, local_heads, head_dim) + bias_in
        queries = rotate(projected[:, 0], cosine, sine).astype(jnp.bfloat16)
        keys_low = rotate(projected[:, 1], cosine, sine).astype(jnp.bfloat16)
        values_low = projected[:, 2].astype(jnp.bfloat16)
        keys_all, values_all = (
            lax.all_gather(keys_low, "seq", axis=0, tiled=True),
            lax.all_gather(values_low, "seq", axis=0, tiled=True),
        )
        raw_scores = jnp.einsum(
            "qhd,khd->hqk", queries, keys_all, preferred_element_type=jnp.float32
        )
        scores = jnp.where(allowed[None], raw_scores * scale, -jnp.inf)
        row_max = jnp.max(scores, axis=-1, keepdims=True)
        weights = jnp.exp(scores - row_max)
        row_total = jnp.sum(weights, axis=-1, keepdims=True)
        log_total = row_max + jnp.log(row_total)
        probs = weights / row_total
        attended = jnp.einsum(
            "hqk,khd->qhd",
            probs.astype(jnp.bfloat16),
            values_all,
            preferred_element_type=jnp.float32,
        )
        mixed_heads = (attended * head_active[:, :, None]).astype(jnp.bfloat16)
        mixed_flat = mixed_heads.reshape(tok_dev, inner)
        attn_part = jnp.dot(mixed_flat, out_matrix, preferred_element_type=jnp.float32)
        attn_sum = lax.psum(attn_part, "tp")
        attn_branch = attn_sum + out_bias_f
        resid = rows + attn_gate[:, None] * attn_branch
        normed_two, scaled_two, inverse_two = norm_forward(resid, gain_two_f, shift_two_f)
        normed_two_low = normed_two.astype(jnp.bfloat16)
        up_pre = jnp.dot(normed_two_low, up_full, preferred_element_type=jnp.float32) + up_bias_vec
        relu_part = jnp.maximum(up_pre, 0.0)
        hidden = (unit_active * jnp.square(relu_part)).astype(jnp.bfloat16)
        down_part = jnp.dot(hidden, down_full, preferred_element_type=jnp.float32)
        down_sum = lax.psum(down_part.astype(jnp.bfloat16), "tp").astype(jnp.float32)
        ffn_branch = down_sum + down_bias_f
        outputs.append((resid + ffn_gate[:, None] * ffn_branch).astype(jnp.bfloat16))
        upstream = cotangent[batch].astype(jnp.float32)
        ffn_gate_grad = jnp.sum(upstream * ffn_branch, axis=-1)
        gated_up = ffn_gate[:, None] * upstream
        grad_down_bias = grad_down_bias + jnp.sum(gated_up, axis=0)
        down_grad = gated_up.astype(jnp.bfloat16)
        grad_down = grad_down + jnp.einsum(
            "tf,td->fd", hidden, down_grad, preferred_element_type=jnp.float32
        )
        hidden_grad = jnp.einsum(
            "td,fd->tf", down_grad, down_full, preferred_element_type=jnp.float32
        )
        up_grad = (hidden_grad * unit_active * 2.0 * relu_part).astype(jnp.bfloat16)
        grad_up_bias = grad_up_bias + jnp.sum(up_grad.astype(jnp.float32), axis=0)
        grad_up = grad_up + jnp.einsum(
            "td,tf->df", normed_two_low, up_grad, preferred_element_type=jnp.float32
        )
        normed_two_part = jnp.einsum(
            "tf,df->td", up_grad, up_full, preferred_element_type=jnp.float32
        )
        normed_two_grad = lax.psum(normed_two_part, "tp")
        grad_gain_two = grad_gain_two + jnp.sum(normed_two_grad * scaled_two, axis=0)
        grad_shift_two = grad_shift_two + jnp.sum(normed_two_grad, axis=0)
        resid_grad = upstream + norm_backward(normed_two_grad, scaled_two, inverse_two, gain_two_f)
        attn_gate_grad = jnp.sum(resid_grad * attn_branch, axis=-1)
        gated_attn = attn_gate[:, None] * resid_grad
        grad_out_bias = grad_out_bias + jnp.sum(gated_attn, axis=0)
        attn_out_grad = gated_attn.astype(jnp.bfloat16)
        grad_out = grad_out + jnp.einsum(
            "ti,td->id", mixed_flat, attn_out_grad, preferred_element_type=jnp.float32
        )
        mixed_grad = jnp.einsum(
            "td,id->ti", attn_out_grad, out_matrix, preferred_element_type=jnp.float32
        )
        attended_grad = (
            mixed_grad.reshape(tok_dev, local_heads, head_dim) * head_active[:, :, None]
        ).astype(jnp.bfloat16)
        again_raw = jnp.einsum(
            "qhd,khd->hqk", queries, keys_all, preferred_element_type=jnp.float32
        )
        again_scores = jnp.where(allowed[None], again_raw * scale, -jnp.inf)
        probs_again = jnp.exp(again_scores - log_total)
        prob_grad = jnp.einsum(
            "qhd,khd->hqk", attended_grad, values_all, preferred_element_type=jnp.float32
        )
        row_dot = jnp.sum(probs_again * prob_grad, axis=-1, keepdims=True)
        score_grad = (probs_again * (prob_grad - row_dot) * scale).astype(jnp.bfloat16)
        query_rot_grad = jnp.einsum(
            "hqk,khd->qhd", score_grad, keys_all, preferred_element_type=jnp.float32
        )
        probs_low = probs_again.astype(jnp.bfloat16)
        key_part = jnp.einsum(
            "hqk,qhd->khd", score_grad, queries, preferred_element_type=jnp.float32
        )
        value_part = jnp.einsum(
            "hqk,qhd->khd", probs_low, attended_grad, preferred_element_type=jnp.float32
        )
        combined = lax.psum_scatter(
            jnp.concatenate([key_part, value_part], axis=1).reshape(
                lax.axis_size("seq") * tok_dev, 2 * inner
            ),
            "seq",
            scatter_dimension=0,
            tiled=True,
        )
        combined = combined.reshape(tok_dev, 2 * local_heads, head_dim)
        key_rot_grad = combined[:, :local_heads]
        value_grad = combined[:, local_heads:]
        query_grad = rotate_back(query_rot_grad, cosine, sine)
        key_grad = rotate_back(key_rot_grad, cosine, sine)
        proj_grad = jnp.stack([query_grad, key_grad, value_grad], axis=1).astype(jnp.bfloat16)
        grad_in_bias = grad_in_bias + jnp.sum(proj_grad.astype(jnp.float32), axis=0)
        proj_flat = proj_grad.reshape(tok_dev, 3 * inner)
        grad_in = grad_in + jnp.einsum(
            "tw,tc->wc", normed_low, proj_flat, preferred_element_type=jnp.float32
        )
        normed_part = jnp.einsum(
            "tc,wc->tw", proj_flat, in_matrix, preferred_element_type=jnp.float32
        )
        logit_grad = jnp.concatenate(
            [
                gate_logit_grad(attn_prob, attn_pick, attn_gate_grad),
                gate_logit_grad(ffn_prob, ffn_pick, ffn_gate_grad),
            ],
            axis=-1,
        )
        grad_router = grad_router + jnp.dot(
            logit_grad.T, normed_low.astype(jnp.float32), precision=HIGHEST
        )
        router_part = jnp.dot(logit_grad, router_wide, precision=HIGHEST)
        normed_grad = lax.psum(normed_part, "tp") + router_part
        grad_gain_one = grad_gain_one + jnp.sum(normed_grad * scaled_one, axis=0)
        grad_shift_one = grad_shift_one + jnp.sum(normed_grad, axis=0)
        input_grads.append(
            resid_grad + norm_backward(normed_grad, scaled_one, inverse_one, gain_one_f)
        )
    reduced = (
        lax.psum_scatter(grad_gain_one, "seq", scatter_dimension=0, tiled=True),
        lax.psum_scatter(grad_shift_one, "seq", scatter_dimension=0, tiled=True),
        lax.psum_scatter(grad_router, "seq", scatter_dimension=1, tiled=True),
        lax.psum_scatter(
            grad_in.reshape(width, 3, local_heads, head_dim), "seq", scatter_dimension=0, tiled=True
        ),
        lax.psum_scatter(grad_in_bias, "seq", scatter_dimension=2, tiled=True),
        lax.psum_scatter(
            grad_out.reshape(local_heads, head_dim, width), "seq", scatter_dimension=2, tiled=True
        ),
        lax.psum_scatter(grad_out_bias, "seq", scatter_dimension=0, tiled=True),
        lax.psum_scatter(grad_gain_two, "seq", scatter_dimension=0, tiled=True),
        lax.psum_scatter(grad_shift_two, "seq", scatter_dimension=0, tiled=True),
        lax.psum_scatter(grad_up, "seq", scatter_dimension=0, tiled=True),
        lax.psum_scatter(
            grad_up_bias.reshape(up_bias_full.shape), "seq", scatter_dimension=1, tiled=True
        ),
        lax.psum_scatter(grad_down, "seq", scatter_dimension=1, tiled=True),
        lax.psum_scatter(grad_down_bias, "seq", scatter_dimension=0, tiled=True),
    )
    return (
        jnp.stack(outputs),
        jnp.stack(input_grads),
        reduced[0],
        reduced[1],
        reduced[2],
        reduced[3],
        reduced[4],
        reduced[5],
        reduced[6],
        reduced[7],
        reduced[8],
        reduced[9],
        reduced[10],
        reduced[11],
        reduced[12],
    )


def solution(mesh):
    return jax.shard_map(
        local,
        mesh=mesh,
        in_specs=(
            P(None, "seq", None),
            P(None, "seq", None),
            P(None, "seq"),
            P(None, "seq"),
            P(),
            P("seq"),
            P("seq"),
            P(None, "seq"),
            P("seq", None, "tp", None),
            P(None, "tp", "seq"),
            P("tp", None, "seq"),
            P("seq"),
            P("seq"),
            P("seq"),
            P("seq", "tp"),
            P("tp", "seq"),
            P("tp", "seq"),
            P("seq"),
        ),
        out_specs=(
            P(None, "seq", None),
            P(None, "seq", None),
            P("seq"),
            P("seq"),
            P(None, "seq"),
            P("seq", None, "tp", None),
            P(None, "tp", "seq"),
            P("tp", None, "seq"),
            P("seq"),
            P("seq"),
            P("seq"),
            P("seq", "tp"),
            P("tp", "seq"),
            P("tp", "seq"),
            P("seq"),
        ),
        check_vma=False,
    )
```

profile of v0, /device:TPU:0, one launch (start us, length us, event | category | flops | bytes accessed | tf_op | source)
XLA Modules:
  0.0 2787.5 jit_solution(17175263219228133610)
XLA Ops:
  9.6 23.1 all-gather.5
  32.7 17.5 all-gather.4
  50.3 19.8 all_gather.67
  72.4 42.7 %all-gather.23.cloned.1.call-done = bf16[2048,3,8,128]{3,0,2,1:T(8,128)(2,1)} async-done(((bf16[128,3,8,128]{3,0,2,1:T(8,128)(2,1)}), bf16[2048,3,8,128]{3,0,2,1:T(8,128)(2,1)}) %all-gather.23.cloned.1.call-update) | async-done | bytes 12582928 | tf_op jit(solution)/shard_map/all_gather | solution.py:93
  115.1 16.7 copy.105
  173.3 12.5 all-gather.37.cloned.1.call-done
  190.2 38.5 %all-gather.35.cloned.1.call-done = bf16[1024,8,128]{2,0,1:T(8,128)(2,1)} async-done(((bf16[64,8,128]{2,0,1:T(8,128)(2,1)}), bf16[1024,8,128]{2,0,1:T(8,128)(2,1)}) %all-gather.35.cloned.1.call-update) | async-done | bytes 2097168 | tf_op jit(solution)/shard_map/all_gather | solution.py:186
  233.8 37.2 %all-gather.33.cloned.1.call-done = bf16[1024,8,128]{2,0,1:T(8,128)(2,1)} async-done(((bf16[64,8,128]{2,0,1:T(8,128)(2,1)}), bf16[1024,8,128]{2,0,1:T(8,128)(2,1)}) %all-gather.33.cloned.1.call-update) | async-done | bytes 2097168 | tf_op jit(solution)/shard_map/all_gather | solution.py:186
  275.3 38.4 %all-gather.25.cloned.1.call-done = bf16[1024,8,128]{2,0,1:T(8,128)(2,1)} async-done(((bf16[64,8,128]{2,0,1:T(8,128)(2,1)}), bf16[1024,8,128]{2,0,1:T(8,128)(2,1)}) %all-gather.25.cloned.1.call-update) | async-done | bytes 2097168 | tf_op jit(solution)/shard_map/all_gather | solution.py:186
  318.1 38.4 %all-gather.45.cloned.1.call-done = bf16[1024,1,8,128]{3,0,2,1:T(8,128)(2,1)} async-done(((bf16[64,1,8,128]{3,0,2,1:T(8,128)(2,1)}), bf16[1024,1,8,128]{3,0,2,1:T(8,128)(2,1)}) %all-gather.45.cloned.1.call-update) | async-done | bytes 2097168 | tf_op jit(solution)/shard_map/all_gather | solution.py:187
  359.4 51.3 %all-gather.27.cloned.1.call-done = bf16[8,128,2048]{2,1,0:T(8,128)(2,1)} async-done(((bf16[8,128,128]{2,1,0:T(8,128)(2,1)}), bf16[8,128,2048]{2,1,0:T(8,128)(2,1)}) %all-gather.27.cloned.1.call-update) | async-done | bytes 4194320 | tf_op jit(solution)/shard_map/all_gather | solution.py:95
  414.5 37.9 %all-gather.43.cloned.1.call-done = bf16[1024,1,8,128]{3,0,2,1:T(8,128)(2,1)} async-done(((bf16[64,1,8,128]{3,0,2,1:T(8,128)(2,1)}), bf16[1024,1,8,128]{3,0,2,1:T(8,128)(2,1)}) %all-gather.43.cloned.1.call-update) | async-done | bytes 2097168 | tf_op jit(solution)/shard_map/all_gather | solution.py:187
  457.0 37.9 %all-gather.41.cloned.1.call-done = bf16[1024,1,8,128]{3,0,2,1:T(8,128)(2,1)} async-done(((bf16[64,1,8,128]{3,0,2,1:T(8,128)(2,1)}), bf16[1024,1,8,128]{3,0,2,1:T(8,128)(2,1)}) %all-gather.41.cloned.1.call-update) | async-done | bytes 2097168 | tf_op jit(solution)/shard_map/all_gather | solution.py:187
  499.3 37.7 %all-gather.39.cloned.1.call-done = bf16[1024,1,8,128]{3,0,2,1:T(8,128)(2,1)} async-done(((bf16[64,1,8,128]{3,0,2,1:T(8,128)(2,1)}), bf16[1024,1,8,128]{3,0,2,1:T(8,128)(2,1)}) %all-gather.39.cloned.1.call-update) | async-done | bytes 2097168 | tf_op jit(solution)/shard_map/all_gather | solution.py:187
  543.1 19.1 all-gather.6
  562.2 17.3 all_gather.75
  579.5 18.7 all-gather.8
  598.3 17.3 all-gather.7
  615.6 19.6 all_gather.65
  642.9 90.6 %all-gather.29.cloned.1.call-done = bf16[2048,4096]{1,0:T(8,128)(2,1)} async-done(((bf16[128,4096]{1,0:T(8,128)(2,1)}), bf16[2048,4096]{1,0:T(8,128)(2,1)}) %all-gather.29.cloned.1.call-update) | async-done | bytes 16777232 | tf_op jit(solution)/shard_map/all_gather | solution.py:99
  742.4 122.0 %all-gather.31.cloned.1.call-done = bf16[4096,2048]{1,0:T(8,128)(2,1)} async-done(((bf16[4096,128]{1,0:T(8,128)(2,1)}), bf16[4096,2048]{1,0:T(8,128)(2,1)}) %all-gather.31.cloned.1.call-update) | async-done | bytes 16777232 | tf_op jit(solution)/shard_map/all_gather | solution.py:101
  864.4 12.5 convert_reduce_fusion
  876.9 12.1 fusion.480
  899.0 12.7 convert_reduce_fusion.2
  911.7 11.9 fusion.478
  933.5 13.2 convert_reduce_fusion.3
  968.6 12.9 convert_reduce_fusion.1
  1021.7 18.8 all-gather.9
  1040.6 14.7 all-reduce.19.cloned.1.call-done
  1058.0 40.2 %all-reduce.23.cloned.1.call-done = (bf16[64,2048]{1,0:T(8,128)(2,1)}, bf16[64,2048]{1,0:T(8,128)(2,1)}, bf16[64,2048]{1,0:T(8,128)(2,1)}, bf16[64,2048]{1,0:T(8,128)(2,1)}) async-done(((bf16[64,2048]{1,0:T(8,128)(2,1)}, bf16[64,2048]{1,0:T(8,128)(2,1)}, bf16[64,2048]{1,0:T(8,128)(2,1)}, bf16[64,2048]{1,0:T(8,128)(2,1)}), (bf16[64,2048]{1,0:T(8,128)(2,1)}, bf16[64,2048]{1,0:T(8,128)(2,1)}, ...) | async-done | bytes 1048592 | tf_op jit(solution)/shard_map/psum | solution.py:216
  1262.8 86.1 %reduce-scatter.16.cloned.1.call-done = f32[64,2048]{1,0:T(8,128)} async-done(((f32[1024,2048]{1,0:T(8,128)}), f32[64,2048]{1,0:T(8,128)}) %reduce-scatter.16.cloned.1.call-update) | async-done | bytes 524304 | tf_op jit(solution)/shard_map/reduce_scatter | solution.py:275
  1351.5 106.4 %reduce-scatter.14.cloned.1.call-done = f32[64,2048]{1,0:T(8,128)} async-done(((f32[1024,2048]{1,0:T(8,128)}), f32[64,2048]{1,0:T(8,128)}) %reduce-scatter.14.cloned.1.call-update) | async-done | bytes 524304 | tf_op jit(solution)/shard_map/reduce_scatter | solution.py:275
  1460.4 106.5 %reduce-scatter.18.cloned.1.call-done = f32[64,2048]{1,0:T(8,128)} async-done(((f32[1024,2048]{1,0:T(8,128)}), f32[64,2048]{1,0:T(8,128)}) %reduce-scatter.18.cloned.1.call-update) | async-done | bytes 524304 | tf_op jit(solution)/shard_map/reduce_scatter | solution.py:275
  1626.2 12.8 add_add_fusion.2
  1640.2 13.3 fusion.442
  1653.6 13.4 fusion.440
  1667.1 13.4 fusion.441
  1680.5 43.5 %add_add_fusion.1 = f32[2048,4096]{1,0:T(8,128)} fusion(f32[2048,4096]{1,0:T(8,128)} %fusion.442, f32[2048,4096]{1,0:T(8,128)} %fusion.440, f32[2048,4096]{1,0:T(8,128)} %fusion.441, bf16[64,4096]{1,0:T(8,128)(2,1)S(1)} %copy-done.49, f32[64,2048]{1,0:T(8,128)S(1)} %copy-done.10, f32[64]{0:T(128)S(1)} %copy-done.217, f32[64]{0:T(128)S(1)} %copy-done.179, ...), kind=kOutput, calls=%fused_computation.5 | convolution fusion | flops 1099563008 | bytes 135283200 | tf_op jit(solution)/shard_map/td,tf->df/dot_general | solution.py:232
  1725.5 13.2 fusion.368
  1738.8 13.4 fusion.374
  1752.3 15.4 fusion.371
  1767.7 45.7 %add_add_fusion = f32[4096,2048]{1,0:T(8,128)} fusion(f32[4096,2048]{1,0:T(8,128)} %fusion.368, f32[4096,2048]{1,0:T(8,128)} %fusion.374, f32[4096,2048]{1,0:T(8,128)} %fusion.371, f32[64]{0:T(128)S(1)} %copy-done.255, bf16[4,64,2048]{2,1,0:T(8,128)(2,1)S(1)} %copy-done.30, f32[64,4096]{1,0:T(8,128)S(1)} %copy-done.8, s32[4096]{0:T(1024)S(1)} %copy-done.47, ...), kind=kOutput, calls=%fused_computation.4 | convolution fusion | flops 1100349440 | bytes 135545856 | tf_op jit(solution)/shard_map/tf,td->fd/dot_general | solution.py:224
  1847.2 37.8 %add_bitcast_fusion = f32[256,8,24,128]{3,1,2,0:T(8,128)} fusion(f32[2048,3072]{1,0:T(8,128)} %fusion.290, f32[2048,3072]{1,0:T(8,128)} %fusion.296, f32[2048,3072]{1,0:T(8,128)} %fusion.293, bf16[8,8,24,128]{3,2,1,0:T(8,128)(2,1)S(1)} %bitcast.734, f32[64]{0:T(128)S(1)} %copy-done.258, f32[64]{0:T(128)S(1)} %copy-done.220, f32[2048]{0:T(1024)S(1)} %bitcast.743, ...), kind=kOutput, calls=%fused_computation.6 | convolution fusion | flops 824967168 | bytes 101336064 | tf_op jit(solution)/shard_map/tw,tc->wc/dot_general | solution.py:291
  1884.9 23.8 copy.165
  1921.6 64.6 %all-reduce.7 = (f32[2048]{0:T(1024)S(1)}, f32[2048]{0:T(1024)S(1)}, f32[3,8,128]{2,1,0:T(8,128)S(1)}, f32[2048]{0:T(1024)S(1)}, f32[2048]{0:T(1024)S(1)}, /*index=5*/f32[2048]{0:T(1024)S(1)}, f32[2048]{0:T(1024)S(1)}) all-reduce(f32[2048]{0:T(1024)S(1)} %add_add_fusion.10, ...), channel_id=10, replica_groups=mesh['seq'=16,'tp'=2] {'seq'}, use_global_device_ids=true, to_apply=%region_108.109.clone | all-reduce | flops 15360 | bytes 122880
  1993.3 203.5 %reduce-scatter.28.cloned.1.call-done = f32[128,4096]{1,0:T(8,128)} async-done(((f32[2048,4096]{1,0:T(8,128)}), f32[128,4096]{1,0:T(8,128)}) %reduce-scatter.28.cloned.1.call-update) | async-done | bytes 2097168 | tf_op jit(solution)/shard_map/reduce_scatter | solution.py:328
  2196.8 336.6 %reduce-scatter.30.cloned.1.call-done = f32[4096,128]{1,0:T(8,128)} async-done(((f32[4096,2048]{1,0:T(8,128)}), f32[4096,128]{1,0:T(8,128)}) %reduce-scatter.30.cloned.1.call-update) | async-done | bytes 2097168 | tf_op jit(solution)/shard_map/reduce_scatter | solution.py:332
  2533.4 247.3 %reduce-scatter.24.cloned.1.call-done = f32[128,3,8,128]{3,2,1,0:T(8,128)} async-done(((f32[2048,3,8,128]{3,2,1,0:T(8,128)}), f32[128,3,8,128]{3,2,1,0:T(8,128)}) %reduce-scatter.24.cloned.1.call-update) | async-done | bytes 1572880 | tf_op jit(solution)/shard_map/reduce_scatter | solution.py:318
  (949 shorter events, 467.9 us)
Async XLA Ops:
  7.2 107.9 %all-gather.23.cloned.1.call-start = ((), (), s32[]{:S(2)}) async-start(), calls=%async_computation.10 | async-start | bytes 13369344 | tf_op jit(solution)/shard_map/all_gather | solution.py:93
  9.6 176.2 %all-gather.37.cloned.1.call-start = ((), (), s32[]{:S(2)}) async-start(), calls=%async_computation.17 | async-start | bytes 2228224 | tf_op jit(solution)/shard_map/all_gather | solution.py:186
  32.7 602.5 %copy-start.103 = (f32[16,1,128]{2,1,0:T(1,128)}, f32[16,1,128]{2,1,0:T(1,128)S(1)}, u32[]{:S(2)}) copy-start(f32[16,1,128]{2,1,0:T(1,128)S(1)} %convert_element_type.603) | copy-start | bytes 24580
  50.2 584.9 %copy-start.95 = (f32[16,1,128]{2,1,0:T(1,128)}, f32[16,1,128]{2,1,0:T(1,128)S(1)}, u32[]{:S(2)}) copy-start(f32[16,1,128]{2,1,0:T(1,128)S(1)} %convert_element_type.602) | copy-start | bytes 24580
  146.1 82.7 %all-gather.35.cloned.1.call-start = ((), (), s32[]{:S(2)}) async-start(), calls=%async_computation.16 | async-start | bytes 2228224 | tf_op jit(solution)/shard_map/all_gather | solution.py:186
  146.8 124.2 %all-gather.33.cloned.1.call-start = ((), (), s32[]{:S(2)}) async-start(), calls=%async_computation.15 | async-start | bytes 2228224 | tf_op jit(solution)/shard_map/all_gather | solution.py:186
  163.5 150.2 %all-gather.25.cloned.1.call-start = ((), (), s32[]{:S(2)}) async-start(), calls=%async_computation.11 | async-start | bytes 2228224 | tf_op jit(solution)/shard_map/all_gather | solution.py:186
  164.1 192.4 %all-gather.45.cloned.1.call-start = ((), (), s32[]{:S(2)}) async-start(), calls=%async_computation.30 | async-start | bytes 2228224 | tf_op jit(solution)/shard_map/all_gather | solution.py:187
  164.8 245.9 %all-gather.27.cloned.1.call-start = ((), (), s32[]{:S(2)}) async-start(), calls=%async_computation.12 | async-start | bytes 4456448 | tf_op jit(solution)/shard_map/all_gather | solution.py:95
  165.6 286.9 %all-gather.43.cloned.1.call-start = ((), (), s32[]{:S(2)}) async-start(), calls=%async_computation.29 | async-start | bytes 2228224 | tf_op jit(solution)/shard_map/all_gather | solution.py:187
  166.3 328.5 %all-gather.41.cloned.1.call-start = ((), (), s32[]{:S(2)}) async-start(), calls=%async_computation.28 | async-start | bytes 2228224 | tf_op jit(solution)/shard_map/all_gather | solution.py:187
  168.1 369.0 %all-gather.39.cloned.1.call-start = ((), (), s32[]{:S(2)}) async-start(), calls=%async_computation.27 | async-start | bytes 2228224 | tf_op jit(solution)/shard_map/all_gather | solution.py:187
  173.3 466.2 %all-reduce.21.cloned.1.call-start = ((), (), s32[]{:S(2)}) async-start(), calls=%async_computation.34 | async-start | bytes 4194304 | tf_op jit(solution)/shard_map/psum | solution.py:207
  541.7 191.8 %all-gather.29.cloned.1.call-start = ((), (), s32[]{:S(2)}) async-start(), calls=%async_computation.13 | async-start | bytes 17825792 | tf_op jit(solution)/shard_map/all_gather | solution.py:99
  542.3 322.1 %all-gather.31.cloned.1.call-start = ((), (), s32[]{:S(2)}) async-start(), calls=%async_computation.14 | async-start | bytes 17825792 | tf_op jit(solution)/shard_map/all_gather | solution.py:101
  543.1 512.2 %all-reduce.19.cloned.1.call-start = ((), (), s32[]{:S(2)}) async-start(), calls=%async_computation.33 | async-start | bytes 4194304 | tf_op jit(solution)/shard_map/psum | solution.py:238
  636.6 381.1 %copy-start.46 = (s32[4096]{0:T(1024)}, s32[4096]{0:T(1024)S(1)}, u32[]{:S(2)}) copy-start(s32[4096]{0:T(1024)S(1)} %add_select_fusion) | copy-start | bytes 49156
  637.5 466.5 %copy-start.238 = (f32[64]{0:T(128)}, f32[64]{0:T(128)S(1)}, u32[]{:S(2)}) copy-start(f32[64]{0:T(128)S(1)} %broadcast_multiply_fusion.6) | copy-start | bytes 772
  638.1 460.1 %copy-start.240 = (f32[64]{0:T(128)}, f32[64]{0:T(128)S(1)}, u32[]{:S(2)}) copy-start(f32[64]{0:T(128)S(1)} %broadcast_multiply_fusion.8) | copy-start | bytes 772
  638.7 530.5 %copy-start.244 = (f32[64]{0:T(128)}, f32[64]{0:T(128)S(1)}, u32[]{:S(2)}) copy-start(f32[64]{0:T(128)S(1)} %broadcast_multiply_fusion.12) | copy-start | bytes 772
  639.3 499.9 %copy-start.242 = (f32[64]{0:T(128)}, f32[64]{0:T(128)S(1)}, u32[]{:S(2)}) copy-start(f32[64]{0:T(128)S(1)} %broadcast_multiply_fusion.10) | copy-start | bytes 772
  639.4 462.7 %copy-start.253 = (f32[64]{0:T(128)}, f32[64]{0:T(128)S(1)}, u32[]{:S(2)}) copy-start(f32[64]{0:T(128)S(1)} %broadcast_multiply_fusion.5) | copy-start | bytes 772
  639.4 496.5 %copy-start.230 = (f32[64]{0:T(128)}, f32[64]{0:T(128)S(1)}, u32[]{:S(2)}) copy-start(f32[64]{0:T(128)S(1)} %broadcast_multiply_fusion.9) | copy-start | bytes 772
  639.4 529.8 %copy-start.235 = (f32[64]{0:T(128)}, f32[64]{0:T(128)S(1)}, u32[]{:S(2)}) copy-start(f32[64]{0:T(128)S(1)} %broadcast_multiply_fusion.11) | copy-start | bytes 772
  639.4 458.8 %copy-start.233 = (f32[64]{0:T(128)}, f32[64]{0:T(128)S(1)}, u32[]{:S(2)}) copy-start(f32[64]{0:T(128)S(1)} %broadcast_multiply_fusion.7) | copy-start | bytes 772
  639.5 378.3 %copy-start.184 = (s32[64]{0:T(128)}, s32[64]{0:T(128)S(1)}, u32[]{:S(2)}) copy-start(s32[64]{0:T(128)S(1)} %get-tuple-element.265) | copy-start | bytes 772
  641.8 456.4 %copy-start.13 = (f32[64,2048]{1,0:T(8,128)}, f32[64,2048]{1,0:T(8,128)S(1)}, u32[]{:S(2)}) copy-start(f32[64,2048]{1,0:T(8,128)S(1)} %get-tuple-element.164) | copy-start | bytes 1572868
  641.8 460.2 %copy-start.9 = (f32[64,2048]{1,0:T(8,128)}, f32[64,2048]{1,0:T(8,128)S(1)}, u32[]{:S(2)}) copy-start(f32[64,2048]{1,0:T(8,128)S(1)} %get-tuple-element.166) | copy-start | bytes 1572868
  641.8 460.2 %copy-start.178 = (f32[64]{0:T(128)}, f32[64]{0:T(128)S(1)}, u32[]{:S(2)}) copy-start(f32[64]{0:T(128)S(1)} %broadcast_multiply_fusion.29) | copy-start | bytes 772
  642.1 493.8 %copy-start.169 = (f32[64]{0:T(128)}, f32[64]{0:T(128)S(1)}, u32[]{:S(2)}) copy-start(f32[64]{0:T(128)S(1)} %broadcast_multiply_fusion.33) | copy-start | bytes 772
  642.3 526.9 %copy-start.171 = (f32[64]{0:T(128)}, f32[64]{0:T(128)S(1)}, u32[]{:S(2)}) copy-start(f32[64]{0:T(128)S(1)} %broadcast_multiply_fusion.35) | copy-start | bytes 772
  642.6 455.7 %copy-start.173 = (f32[64]{0:T(128)}, f32[64]{0:T(128)S(1)}, u32[]{:S(2)}) copy-start(f32[64]{0:T(128)S(1)} %broadcast_multiply_fusion.31) | copy-start | bytes 772
  642.8 459.3 %copy-start.216 = (f32[64]{0:T(128)}, f32[64]{0:T(128)S(1)}, u32[]{:S(2)}) copy-start(f32[64]{0:T(128)S(1)} %add_rsqrt_fusion) | copy-start | bytes 772
  642.8 493.0 %copy-start.203 = (f32[64]{0:T(128)}, f32[64]{0:T(128)S(1)}, u32[]{:S(2)}) copy-start(f32[64]{0:T(128)S(1)} %add_rsqrt_fusion.4) | copy-start | bytes 772
  642.8 526.4 %copy-start.205 = (f32[64]{0:T(128)}, f32[64]{0:T(128)S(1)}, u32[]{:S(2)}) copy-start(f32[64]{0:T(128)S(1)} %add_rsqrt_fusion.6) | copy-start | bytes 772
  642.9 455.4 %copy-start.207 = (f32[64]{0:T(128)}, f32[64]{0:T(128)S(1)}, u32[]{:S(2)}) copy-start(f32[64]{0:T(128)S(1)} %add_rsqrt_fusion.2) | copy-start | bytes 772
  993.4 104.8 %all-reduce.23.cloned.1.call-start = ((), (), s32[]{:S(2)}) async-start(), calls=%async_computation.35 | async-start | bytes 2097152 | tf_op jit(solution)/shard_map/psum | solution.py:216
  1021.7 239.2 %reduce-scatter.20.cloned.1.call-start = ((), (), s32[]{:S(2)}) async-start(), calls=%async_computation.21 | async-start | bytes 8912896 | tf_op jit(solution)/shard_map/reduce_scatter | solution.py:275
  1135.3 213.7 %reduce-scatter.16.cloned.1.call-start = ((), (), s32[]{:S(2)}) async-start(), calls=%async_computation.19 | async-start | bytes 8912896 | tf_op jit(solution)/shard_map/reduce_scatter | solution.py:275
  1169.1 288.8 %reduce-scatter.14.cloned.1.call-start = ((), (), s32[]{:S(2)}) async-start(), calls=%async_computation.18 | async-start | bytes 8912896 | tf_op jit(solution)/shard_map/reduce_scatter | solution.py:275
  1201.6 365.3 %reduce-scatter.18.cloned.1.call-start = ((), (), s32[]{:S(2)}) async-start(), calls=%async_computation.20 | async-start | bytes 8912896 | tf_op jit(solution)/shard_map/reduce_scatter | solution.py:275
  1231.0 680.3 %reduce-scatter.32.cloned.1.call-start = ((), (), s32[]{:S(2)}) async-start(), calls=%async_computation.31 | async-start | bytes 1114112
  1233.3 680.9 %all-reduce.17.cloned.1.call-start = ((), (), s32[]{:S(2)}) async-start(), calls=%async_computation.32 | async-start | bytes 4194304 | tf_op jit(solution)/shard_map/psum | solution.py:308
  1610.0 383.3 %reduce-scatter.22.cloned.1.call-start = ((), (), s32[]{:S(2)}) async-start(), calls=%async_computation.22 | async-start | bytes 69632 | tf_op jit(solution)/shard_map/reduce_scatter | solution.py:317
  1626.2 367.1 %reduce-scatter.26.cloned.1.call-start = ((), (), s32[]{:S(2)}) async-start(), calls=%async_computation.24 | async-start | bytes 8912896 | tf_op jit(solution)/shard_map/reduce_scatter | solution.py:322
  1639.1 557.7 %reduce-scatter.28.cloned.1.call-start = ((), (), s32[]{:S(2)}) async-start(), calls=%async_computation.25 | async-start | bytes 35651584 | tf_op jit(solution)/shard_map/reduce_scatter | solution.py:328
  1724.1 809.3 %reduce-scatter.30.cloned.1.call-start = ((), (), s32[]{:S(2)}) async-start(), calls=%async_computation.26 | async-start | bytes 35651584 | tf_op jit(solution)/shard_map/reduce_scatter | solution.py:332
  1813.5 967.2 %reduce-scatter.24.cloned.1.call-start = ((), (), s32[]{:S(2)}) async-start(), calls=%async_computation.23 | async-start | bytes 26738688 | tf_op jit(solution)/shard_map/reduce_scatter | solution.py:318
  (289 other events, 7428.2 us)
Sparse Core Ops, SparseCore 0:
  10.8 104.2 all-gather.22
  146.2 39.5 all-gather.36
  188.6 40.1 all-gather.34
  230.8 40.1 all-gather.32
  273.6 40.1 all-gather.24
  316.4 40.1 all-gather.44
  358.7 51.9 all-gather.26
  412.9 39.5 all-gather.42
  454.7 40.1 all-gather.40
  496.9 40.1 all-gather.38
  541.8 62.2 all-reduce.20
  606.4 127.0 all-gather.28
  735.8 128.5 all-gather.30
  993.6 61.6 all-reduce.18
  1057.6 40.6 all-reduce.22
  1135.4 104.5 reduce-scatter.19
  1244.5 104.4 reduce-scatter.15
  1353.4 104.4 reduce-scatter.13
  1462.5 104.3 reduce-scatter.17
  1570.8 57.0 reduce-scatter.31
  1631.0 62.5 all-reduce.16
  1697.9 52.0 reduce-scatter.21
  1754.6 103.8 reduce-scatter.25
  1863.2 333.5 reduce-scatter.27
  2201.6 331.7 reduce-scatter.29
  2537.9 242.7 reduce-scatter.23
where the time goes:
time: 2800 us; the launch traced here: 2790 us
  waiting for transfers between devices  1730 us (62%)
  matrix products  606 us (22%)
  blocking collectives  236 us (8%)
  local copies, waits for them, and re-layouts  126 us (4%)
  other arithmetic  67.3 us (2%)
    reduce_scatter x1, waiting for transfers between devices, local(): lax.psum_scatter(grad_down, 'seq', scatter_dimension=1, tiled=True)  337 us
    reduce_scatter x4, waiting for transfers between devices, local(): lax.psum_scatter(jnp.concatenate([key_part, value_part], axis=1).reshape(...  299 us
    reduce_scatter x1, waiting for transfers between devices, local(): lax.psum_scatter(grad_in.reshape(width, 3, local_heads, head_dim), 'seq',...  247 us
    reduce_scatter x1, waiting for transfers between devices, local(): lax.psum_scatter(grad_up, 'seq', scatter_dimension=0, tiled=True)  203 us
    all_gather x4, waiting for transfers between devices, local(): lax.all_gather(values_low, 'seq', axis=0, tiled=True)  152 us
    all_gather x4, waiting for transfers between devices, local(): lax.all_gather(keys_low, 'seq', axis=0, tiled=True)  127 us
    all_gather x1, waiting for transfers between devices, local(): lax.all_gather(down_weight, 'seq', axis=1, tiled=True)  122 us
    all_gather x1, waiting for transfers between devices, local(): lax.all_gather(up_weight, 'seq', axis=0, tiled=True)  90.6 us
  transfers between devices with their start and end apart: 26, of which 20 were waited for; matrix products, arithmetic and copies ran while one was open for 21% of the time, Pallas kernels for 0%

commit v1 on v0

--- a/solution.py
+++ b/solution.py
@@ -3,6 +3,7 @@
 import jax
 import jax.numpy as jnp
 from jax import lax
+from jax.sharding import Mesh
 from jax.sharding import PartitionSpec as P
 
 HEADS = 16
@@ -351,46 +352,382 @@
     )
 
 
+ROWS = ("zh", "zl", "x", "c")
+GROUP = ("zl", "y", "c")
+PARTS = ("zh", "x")
+LOW = jnp.bfloat16
+WIDE = jnp.float32
+
+
+def swap(value, axis):
+    return lax.ppermute(value, axis, [(0, 1), (1, 0)])
+
+
+def flip_where(bit, value, axis):
+    return jnp.where(bit == 1, jnp.flip(value, axis), value)
+
+
+def to_own_order(value, zh, x):
+    lead, width = value.shape[:-1], value.shape[-1]
+    value = value.reshape(lead + (2, 2, 2, 2, width // 16))
+    value = jnp.swapaxes(value, -4, -3)
+    value = flip_where(zh, value, -5)
+    value = flip_where(x, value, -4)
+    return value.reshape(lead + (width,))
+
+
+def from_own_order(value, zh, x):
+    lead, width = value.shape[:-1], value.shape[-1]
+    value = value.reshape(lead + (2, 2, 2, 2, width // 16))
+    value = flip_where(zh, value, -5)
+    value = flip_where(x, value, -4)
+    value = jnp.swapaxes(value, -4, -3)
+    return value.reshape(lead + (width,))
+
+
+def gather_parts(piece, axis):
+    over_x = swap(piece, "x")
+    over_z = swap(piece, "zh")
+    over_both = swap(over_z, "x")
+    return jnp.concatenate([piece, over_x, over_z, over_both], axis=axis)
+
+
+def scatter_parts(pieces):
+    stay, send = pieces[0], pieces[1]
+    got = [swap(p.astype(LOW), "x") for p in send]
+    first = stay[1] + got[1].astype(WIDE)
+    over_z = swap(first.astype(LOW), "zh")
+    return stay[0] + got[0].astype(WIDE) + over_z.astype(WIDE)
+
+
+def dot_to(left, right, dims):
+    return lax.dot_general(left, right, (dims, ((), ())), preferred_element_type=WIDE)
+
+
+def grouped(
+    tokens,
+    cotangent,
+    head_groups,
+    ffn_widths,
+    doc_lengths,
+    first_gain,
+    first_shift,
+    router_weight,
+    in_weight,
+    in_bias,
+    out_weight,
+    out_bias,
+    second_gain,
+    second_shift,
+    up_weight,
+    up_bias,
+    down_weight,
+    down_bias,
+):
+    zh, zl, x, c, y = (lax.axis_index(a) for a in ("zh", "zl", "x", "c", "y"))
+    micro, tok_dev, width = tokens.shape
+    half = tok_dev // 2
+    own = 4 * half
+    length = 16 * tok_dev
+    block = width // 16
+    tp_heads, head_dim = in_weight.shape[2:]
+    heads = tp_heads // 4
+    inner = heads * head_dim
+    tp_units = up_weight.shape[1]
+    units = tp_units // 4
+    batch = zh * 2 + x
+    part = zl * 2 + c
+    place = (zl * 2 + y) * 2 + c
+    scale = HEAD_DIM ** (-0.5)
+
+    small = jnp.concatenate(
+        [
+            first_gain,
+            first_shift,
+            second_gain,
+            second_shift,
+            out_bias,
+            down_bias,
+            router_weight.reshape(-1),
+            in_bias.reshape(-1),
+            up_bias.reshape(-1),
+            head_groups.astype(LOW).reshape(-1),
+            ffn_widths.astype(LOW).reshape(-1),
+        ]
+    )
+    small_all = lax.all_gather(small, ROWS, axis=0)
+    n_vec = 6 + 2 * GROUPS
+    vectors = small_all[:, : n_vec * block].reshape(16, n_vec, block)
+    vectors = jnp.swapaxes(vectors, 0, 1).reshape(n_vec, width)
+    vectors = to_own_order(vectors, zh, x)
+    vectors_f = vectors.astype(WIDE)
+    gain_one, shift_one, gain_two, shift_two, bias_out, bias_down = (
+        vectors_f[i : i + 1] for i in range(6)
+    )
+    router = vectors[6:]
+    at = n_vec * block
+    size = in_bias.size
+    bias_in = small_all[:, at : at + size].reshape((16,) + in_bias.shape)
+    bias_in = jnp.moveaxis(bias_in, 0, 2).reshape(3, 4, heads, head_dim)
+    bias_in = lax.dynamic_index_in_dim(bias_in, part, 1, keepdims=False).astype(WIDE)
+    at += size
+    size = up_bias.size
+    bias_up = small_all[:, at : at + size].reshape((16,) + up_bias.shape)
+    bias_up = jnp.moveaxis(bias_up, 0, 1).reshape(4, units)
+    bias_up = lax.dynamic_index_in_dim(bias_up, part, 0, keepdims=True).astype(WIDE)
+    at += size
+    widths = small_all[:, at:].reshape(16, 2, micro, tok_dev)
+    widths = lax.dynamic_index_in_dim(widths, batch, 2, keepdims=False).astype(jnp.int32)
+    widths = widths.reshape(2, 2, 2, 2, 2, 2, half)
+    widths = jnp.transpose(widths, (4, 1, 5, 3, 0, 2, 6)).reshape(2, length)
+    heads_row, units_row = widths[0], widths[1]
+
+    index = jnp.arange(length, dtype=jnp.int32).reshape(2, 2, 2, 2, 2, half)
+    positions = jnp.transpose(index, (1, 4, 3, 0, 2, 5)).reshape(length)
+    doc = doc_index(lax.dynamic_index_in_dim(doc_lengths, batch, 0, keepdims=False), positions)
+    cosine, sine = rotary_tables(positions)
+    allowed = (positions[None, :] <= positions[:, None]) & (doc[None, :] == doc[:, None])
+
+    def to_batch(value):
+        mine = lax.dynamic_slice_in_dim(value, y * half, half, 1)
+        got = lax.all_to_all(mine, PARTS, 0, 0, tiled=True)
+        return to_own_order(got.reshape(own, width), zh, x)
+
+    tokens_own = to_batch(tokens)
+    tokens_all = lax.all_gather(tokens_own, GROUP, axis=0, tiled=True)
+    cotangent_own = to_batch(cotangent)
+    cotangent_all = lax.all_gather(cotangent_own, GROUP, axis=0, tiled=True)
+
+    def exchange(value):
+        return lax.all_to_all(value, ("zl", "c"), 0, 0, tiled=True)
+
+    w_in = in_weight.reshape(block, 3, 4, heads, head_dim)
+    w_in = exchange(jnp.moveaxis(w_in, 2, 0)).reshape(4 * block, 3 * inner)
+    w_in = gather_parts(w_in, 0)
+    w_out = exchange(out_weight.reshape(4, inner, block))
+    w_out = gather_parts(jnp.moveaxis(w_out, 0, 1).reshape(inner, 4 * block), 1)
+    w_up = exchange(jnp.moveaxis(up_weight.reshape(block, 4, units), 1, 0))
+    w_up = gather_parts(w_up.reshape(4 * block, units), 0)
+    w_down = exchange(down_weight.reshape(4, units, block))
+    w_down = gather_parts(jnp.moveaxis(w_down, 0, 1).reshape(units, 4 * block), 1)
+
+    normed, _, _ = norm_forward(tokens_all.astype(WIDE), gain_one, shift_one)
+    normed_low = normed.astype(LOW)
+    logits = dot_to(normed_low, router, ((1,), (1,)))
+    options = jnp.arange(GROUPS, dtype=jnp.int32)
+    attn_prob = jax.nn.softmax(logits[:, :GROUPS], axis=-1)
+    ffn_prob = jax.nn.softmax(logits[:, GROUPS:], axis=-1)
+    attn_pick = (options[None, :] == heads_row[:, None] - 1).astype(WIDE)
+    ffn_pick = (options[None, :] == units_row[:, None] - 1).astype(WIDE)
+    attn_gate = GROUPS * jnp.sum(attn_prob * attn_pick, axis=-1, keepdims=True)
+    ffn_gate = GROUPS * jnp.sum(ffn_prob * ffn_pick, axis=-1, keepdims=True)
+
+    def mine(value):
+        return lax.dynamic_slice_in_dim(value, place * own, own, 0)
+
+    rows = tokens_own.astype(WIDE)
+    _, scaled_one, inverse_one = norm_forward(rows, gain_one, shift_one)
+
+    projected = dot_to(normed_low, w_in, ((1,), (0,)))
+    projected = projected.reshape(length, 3, heads, head_dim) + bias_in
+    queries = rotate(projected[:, 0], cosine, sine).astype(LOW)
+    keys = rotate(projected[:, 1], cosine, sine).astype(LOW)
+    values = projected[:, 2].astype(LOW)
+    head_ids = (y * 4 + part) * heads + jnp.arange(heads, dtype=jnp.int32)
+    head_active = (head_ids[None, :] // (HEADS // GROUPS) < heads_row[:, None]).astype(WIDE)
+    unit_ids = (y * 4 + part) * units + jnp.arange(units, dtype=jnp.int32)
+    unit_active = unit_ids[None, :] // (FF // GROUPS) < units_row[:, None]
+    raw = jnp.einsum("qhd,khd->hqk", queries, keys, preferred_element_type=WIDE)
+    scores = jnp.where(allowed[None], raw * scale, -jnp.inf)
+    row_max = jnp.max(scores, axis=-1, keepdims=True)
+    weights = jnp.exp(scores - row_max)
+    row_total = jnp.sum(weights, axis=-1, keepdims=True)
+    probs = weights / row_total
+    probs_low = probs.astype(LOW)
+    attended = jnp.einsum("hqk,khd->qhd", probs_low, values, preferred_element_type=WIDE)
+    mixed = (attended * head_active[:, :, None]).astype(LOW).reshape(length, inner)
+    attn_part = dot_to(mixed, w_out, ((1,), (0,)))
+
+    def group_sum(value):
+        return lax.psum_scatter(
+            value.astype(LOW), GROUP, scatter_dimension=0, tiled=True
+        ).astype(WIDE)
+
+    attn_branch = group_sum(attn_part) + bias_out
+    attn_gate_own = mine(attn_gate)
+    ffn_gate_own = mine(ffn_gate)
+    resid = rows + attn_gate_own * attn_branch
+    normed_two, scaled_two, inverse_two = norm_forward(resid, gain_two, shift_two)
+    normed_two_low = lax.all_gather(normed_two.astype(LOW), GROUP, axis=0, tiled=True)
+
+    up_pre = dot_to(normed_two_low, w_up, ((1,), (0,))) + bias_up
+    relu_part = jnp.where(unit_active, jnp.maximum(up_pre, 0.0), 0.0)
+    hidden = jnp.square(relu_part).astype(LOW)
+    down_grad = (ffn_gate * cotangent_all.astype(WIDE)).astype(LOW)
+    hidden_grad = dot_to(down_grad, w_down, ((1,), (1,)))
+    up_grad = (hidden_grad * 2.0 * relu_part).astype(LOW)
+    normed_two_grad = group_sum(dot_to(up_grad, w_up, ((1,), (1,))))
+    ffn_branch = group_sum(dot_to(hidden, w_down, ((1,), (0,)))) + bias_down
+    grad_up = dot_to(normed_two_low, up_grad, ((0,), (0,)))
+    grad_down = dot_to(hidden, down_grad, ((0,), (0,)))
+    grad_up_bias = jnp.sum(up_grad.astype(WIDE), axis=0)
+
+    upstream = cotangent_own.astype(WIDE)
+    block_out = (resid + ffn_gate_own * ffn_branch).astype(LOW)
+    ffn_gate_grad = jnp.sum(upstream * ffn_branch, axis=-1)
+    grad_down_bias = jnp.sum(ffn_gate_own * upstream, axis=0)
+    grad_gain_two = jnp.sum(normed_two_grad * scaled_two, axis=0)
+    grad_shift_two = jnp.sum(normed_two_grad, axis=0)
+    resid_grad = upstream + norm_backward(normed_two_grad, scaled_two, inverse_two, gain_two)
+    attn_gate_grad = jnp.sum(resid_grad * attn_branch, axis=-1)
+    gated_attn = attn_gate_own * resid_grad
+    grad_out_bias = jnp.sum(gated_attn, axis=0)
+    attn_out_grad = lax.all_gather(gated_attn.astype(LOW), GROUP, axis=0, tiled=True)
+
+    mixed_grad = dot_to(attn_out_grad, w_out, ((1,), (1,)))
+    attended_grad = (
+        mixed_grad.reshape(length, heads, head_dim) * head_active[:, :, None]
+    ).astype(LOW)
+    grad_out = dot_to(mixed, attn_out_grad, ((0,), (0,)))
+    prob_grad = jnp.einsum("qhd,khd->hqk", attended_grad, values, preferred_element_type=WIDE)
+    row_dot = jnp.sum(probs * prob_grad, axis=-1, keepdims=True)
+    score_grad = (probs * (prob_grad - row_dot) * scale).astype(LOW)
+    query_grad = jnp.einsum("hqk,khd->qhd", score_grad, keys, preferred_element_type=WIDE)
+    key_grad = jnp.einsum("hqk,qhd->khd", score_grad, queries, preferred_element_type=WIDE)
+    value_grad = jnp.einsum("hqk,qhd->khd", probs_low, attended_grad, preferred_element_type=WIDE)
+    query_grad = rotate_back(query_grad, cosine, sine)
+    key_grad = rotate_back(key_grad, cosine, sine)
+    proj_grad = jnp.stack([query_grad, key_grad, value_grad], axis=1).astype(LOW)
+    grad_in_bias = jnp.sum(proj_grad.astype(WIDE), axis=0)
+    proj_flat = proj_grad.reshape(length, 3 * inner)
+    normed_part = group_sum(dot_to(proj_flat, w_in, ((1,), (1,))))
+    grad_in = dot_to(normed_low, proj_flat, ((0,), (0,)))
+
+    logit_grad = jnp.concatenate(
+        [
+            gate_logit_grad(mine(attn_prob), mine(attn_pick), attn_gate_grad),
+            gate_logit_grad(mine(ffn_prob), mine(ffn_pick), ffn_gate_grad),
+        ],
+        axis=-1,
+    )
+    normed_own = mine(normed_low)
+    grad_router = jnp.dot(logit_grad.T, normed_own.astype(WIDE), precision=HIGHEST)
+    router_part = jnp.dot(logit_grad, vectors_f[6:], precision=HIGHEST)
+    normed_grad = normed_part + router_part
+    grad_gain_one = jnp.sum(normed_grad * scaled_one, axis=0)
+    grad_shift_one = jnp.sum(normed_grad, axis=0)
+    tokens_grad = resid_grad + norm_backward(normed_grad, scaled_one, inverse_one, gain_one)
+
+    def from_batch(value):
+        value = from_own_order(value, zh, x).astype(LOW).reshape(4, half, width)
+        value = lax.all_to_all(value, PARTS, 0, 0, tiled=True)
+        other = swap(value, "y")
+        return jnp.where(
+            y == 0,
+            jnp.concatenate([value, other], axis=1),
+            jnp.concatenate([other, value], axis=1),
+        )
+
+    def share_rows(grad):
+        total = scatter_parts(jnp.swapaxes(grad.reshape(2, 2, 4 * block, -1), 0, 1))
+        total = exchange(total.astype(LOW).reshape(4, block, -1))
+        return total
+
+    def share_columns(grad):
+        grad = grad.reshape(grad.shape[0], 2, 2, 4 * block)
+        total = scatter_parts(jnp.transpose(grad, (2, 1, 0, 3)))
+        total = total.astype(LOW).reshape(-1, 4, block)
+        return exchange(jnp.swapaxes(total, 0, 1))
+
+    grad_up = jnp.swapaxes(share_rows(grad_up), 0, 1).reshape(block, tp_units)
+    grad_down = share_columns(grad_down).reshape(tp_units, block)
+    grad_out = share_columns(grad_out).reshape(tp_heads, head_dim, block)
+    grad_in = share_rows(grad_in).reshape(4, block, 3, heads, head_dim)
+    grad_in = jnp.transpose(grad_in, (1, 2, 0, 3, 4)).reshape(block, 3, tp_heads, head_dim)
+
+    sums = jnp.stack(
+        [grad_gain_one, grad_shift_one, grad_out_bias, grad_gain_two, grad_shift_two, grad_down_bias]
+    )
+    sums = from_own_order(jnp.concatenate([sums, grad_router], axis=0), zh, x)
+    sums = jnp.swapaxes(sums.reshape(n_vec, 16, block), 0, 1).reshape(16, n_vec * block)
+    chosen = (jnp.arange(4) == part).astype(WIDE)
+    spread_in = (grad_in_bias[:, None] * chosen[None, :, None, None]).reshape(
+        3, tp_heads, 16, head_dim // 16
+    )
+    spread_in = jnp.moveaxis(spread_in, 2, 0).reshape(16, -1)
+    spread_up = (grad_up_bias[None, :] * chosen[:, None]).reshape(up_bias.shape[0], 16, block)
+    spread_up = jnp.moveaxis(spread_up, 1, 0).reshape(16, -1)
+    total = lax.psum_scatter(
+        jnp.concatenate([sums, spread_in, spread_up], axis=1),
+        ROWS,
+        scatter_dimension=0,
+        tiled=True,
+    )[0]
+    shared = lax.psum(total[: n_vec * block], "y").reshape(n_vec, block)
+    at = n_vec * block
+    return (
+        from_batch(block_out),
+        from_batch(tokens_grad).astype(WIDE),
+        shared[0],
+        shared[1],
+        shared[6:],
+        grad_in.astype(WIDE),
+        total[at : at + in_bias.size].reshape(in_bias.shape),
+        grad_out.astype(WIDE),
+        shared[2],
+        shared[3],
+        shared[4],
+        grad_up.astype(WIDE),
+        total[at + in_bias.size :].reshape(up_bias.shape),
+        grad_down.astype(WIDE),
+        shared[5],
+    )
+
+
 def solution(mesh):
+    body, seq, tp = local, "seq", "tp"
+    if mesh.shape["seq"] == 16 and mesh.shape["tp"] == 2:
+        mesh = Mesh(mesh.devices.reshape(2, 2, 2, 2, 2), ROWS + ("y",))
+        body, seq, tp = grouped, ROWS, "y"
     return jax.shard_map(
-        local,
+        body,
         mesh=mesh,
         in_specs=(
-            P(None, "seq", None),
-            P(None, "seq", None),
-            P(None, "seq"),
-            P(None, "seq"),
+            P(None, seq, None),
+            P(None, seq, None),
+            P(None, seq),
+            P(None, seq),
             P(),
-            P("seq"),
-            P("seq"),
-            P(None, "seq"),
-            P("seq", None, "tp", None),
-            P(None, "tp", "seq"),
-            P("tp", None, "seq"),
-            P("seq"),
-            P("seq"),
-            P("seq"),
-            P("seq", "tp"),
-            P("tp", "seq"),
-            P("tp", "seq"),
-            P("seq"),
+            P(seq),
+            P(seq),
+            P(None, seq),
+            P(seq, None, tp, None),
+            P(None, tp, seq),
+            P(tp, None, seq),
+            P(seq),
+            P(seq),
+            P(seq),
+            P(seq, tp),
+            P(tp, seq),
+            P(tp, seq),
+            P(seq),
         ),
         out_specs=(
-            P(None, "seq", None),
-            P(None, "seq", None),
-            P("seq"),
-            P("seq"),
-            P(None, "seq"),
-            P("seq", None, "tp", None),
-            P(None, "tp", "seq"),
-            P("tp", None, "seq"),
-            P("seq"),
-            P("seq"),
-            P("seq"),
-            P("seq", "tp"),
-            P("tp", "seq"),
-            P("tp", "seq"),
-            P("seq"),
+            P(None, seq, None),
+            P(None, seq, None),
+            P(seq),
+            P(seq),
+            P(None, seq),
+            P(seq, None, tp, None),
+            P(None, tp, seq),
+            P(tp, None, seq),
+            P(seq),
+            P(seq),
+            P(seq),
+            P(seq, tp),
+            P(tp, seq),
+            P(tp, seq),
+            P(seq),
         ),
         check_vma=False,
     )

time: 2800 us -> 1090 us (0.39)
  waiting for transfers between devices: 1730 us -> 593 us
  matrix products: 606 us -> 147 us
  blocking collectives: 236 us -> 44.6 us
  starting transfers between devices: 2.74 us -> 81 us
    reduce_scatter x9 -> x4, waiting for transfers between devices: 1090 us -> 117 us  [group_sum(): lax.psum_scatter(value.astype(LOW), GROUP, scatter_dimension=0, tiled=True)]
    all_gather x12 -> x4, waiting for transfers between devices: 585 us -> 14.5 us  [the longest x1 14.5 us: grouped(): lax.all_gather(gated_attn.astype(LOW), GROUP, axis=0, tiled=True)]
    dot_general x84 -> x20, matrix products: 606 us -> 139 us  [the longest x13 88.3 us: dot_to(): lax.dot_general(left, right, (dims, ((), ())), preferred_element_type=WIDE)]
    ppermute x0 -> x26, waiting for transfers between devices: none -> 232 us  [swap(): return lax.ppermute(value, axis, [(0, 1), (1, 0)])]
    all_gather x9 -> x0, blocking collectives: 171 us -> none  [the longest x1 23.1 us: local(): lax.all_gather(first_shift, 'seq', axis=0, tiled=True)]
    unnamed x27 -> x12, waiting for transfers between devices: 3.5 us -> 159 us
    all_to_all x0 -> x10, waiting for transfers between devices: none -> 70.9 us  [the longest x7 54 us: exchange(): return lax.all_to_all(value, ('zl', 'c'), 0, 0, tiled=True)]
    unnamed x1 -> x0, blocking collectives: 64.6 us -> none
  transfers between devices with their start and end apart: 26 -> 46, of which waited for: 20 -> 26; matrix products, arithmetic and copies ran while one was open for 21% -> 27% of each run, Pallas kernels for 0% -> 0%
where the time goes in v1:
time: 1090 us; the launch traced here: 1080 us
  waiting for transfers between devices  593 us (54%)
  matrix products  147 us (13%)
  local copies, waits for them, and re-layouts  122 us (11%)
  starting transfers between devices  81 us (7%)
  other arithmetic  74.4 us (7%)
  blocking collectives  44.6 us (4%)
  between operations  18.1 us (2%)
    ppermute x26, waiting for transfers between devices, swap(): return lax.ppermute(value, axis, [(0, 1), (1, 0)])  232 us
    unnamed x12, waiting for transfers between devices  159 us
    reduce_scatter x4, waiting for transfers between devices, group_sum(): lax.psum_scatter(value.astype(LOW), GROUP, scatter_dimension=0, tiled=True)  117 us
    dot_general x13, matrix products, dot_to(): lax.dot_general(left, right, (dims, ((), ())), preferred_element_type=WIDE)  88.3 us
    all_to_all x7, waiting for transfers between devices, exchange(): return lax.all_to_all(value, ('zl', 'c'), 0, 0, tiled=True)  54 us
    ppermute x26, starting transfers between devices, swap(): return lax.ppermute(value, axis, [(0, 1), (1, 0)])  30.1 us
    all_to_all x7, starting transfers between devices, exchange(): return lax.all_to_all(value, ('zl', 'c'), 0, 0, tiled=True)  25.6 us
    unnamed x153, local copies, waits for them, and re-layouts  24.3 us
  transfers between devices with their start and end apart: 46, of which 26 were waited for; matrix products, arithmetic and copies ran while one was open for 27% of the time, Pallas kernels for 0%

profile of v1, /device:TPU:0, one launch (start us, length us, event | category | flops | bytes accessed | tf_op | source)
XLA Modules:
  0.0 1080.7 jit_solution(16195909397023017350)
XLA Ops:
  10.1 6.2 all-to-all-start
  20.6 5.4 concatenate.74
  45.4 85.9 %all-reduce.5.cloned.1.call-done = bf16[44032]{0:T(1024)(128)(2,1)} async-done(((bf16[44032]{0:T(1024)(128)(2,1)}), bf16[44032]{0:T(1024)(128)(2,1)}) %all-reduce.5.cloned.1.call-update) | async-done | bytes 88080
  143.7 31.9 %collective-permute-done.1 = bf16[512,768]{1,0:T(8,128)(2,1)S(1)} collective-permute-done((bf16[512,768]{1,0:T(8,128)(2,1)S(1)}, bf16[512,768]{1,0:T(8,128)(2,1)S(1)}, u32[]{:S(2)}, u32[]{:S(2)}) %collective-permute-start.1) | collective-permute-done | bytes 786464 | tf_op jit(solution)/shard_map/ppermute | solution.py:363
  182.4 10.5 collective-permute-done.4
  206.9 7.0 fusion.152
  217.4 7.8 fusion.148
  225.2 4.5 fusion.58
  229.8 4.6 convolution_convert_fusion
  234.4 11.0 %all-gather.8.cloned.1.call-start = ((), (), s32[]{:S(2)}) async-start(), calls=%async_computation.18 | async-start | bytes 4718592 | tf_op jit(solution)/shard_map/all_gather | solution.py:561
  249.4 31.3 %reduce-scatter.5.cloned.1.call-done = bf16[128,2048]{1,0:T(8,128)(2,1)} async-done(((bf16[1024,2048]{1,0:T(8,128)(2,1)}), bf16[128,2048]{1,0:T(8,128)(2,1)}) %reduce-scatter.5.cloned.1.call-update) | async-done | bytes 524304 | tf_op jit(solution)/shard_map/reduce_scatter | solution.py:552
  285.9 19.4 %all_to_all.60 = bf16[4,32,2048]{2,1,0:T(8,128)(2,1)S(1)} all-to-all(bf16[4,32,2048]{2,1,0:T(8,128)(2,1)S(1)} %constant_dynamic-slice_fusion.4), channel_id=1, replica_groups=mesh['zh'=2,'zl'=2,'x'=2,'c'=2,'y'=2] {'zh','x'}, dimensions={0} | all-to-all | bytes 1048576 | tf_op jit(solution)/shard_map/all_to_all | solution.py:493
  311.1 20.2 %all_to_all.61 = bf16[4,128,1024]{1,2,0:T(8,128)(2,1)} all-to-all(bf16[4,128,1024]{1,2,0:T(8,128)(2,1)S(1)} %bitcast.287), channel_id=1, replica_groups=mesh['zh'=2,'zl'=2,'x'=2,'c'=2,'y'=2] {'zl','c'}, dimensions={0} | all-to-all | bytes 2097152 | tf_op jit(solution)/shard_map/all_to_all | solution.py:502
  338.9 41.4 %all-to-all-done.4 = bf16[4,1024,128]{2,1,0:T(8,128)(2,1)S(1)} async-done(((bf16[4,1024,128]{2,1,0:T(8,128)(2,1)}), bf16[4,1024,128]{2,1,0:T(8,128)(2,1)S(1)}, u32[]{:S(2)}, u32[]{:S(2)}) %all-to-all-start.4) | async-done | bytes 1048608 | tf_op jit(solution)/shard_map/all_to_all | solution.py:502
  386.6 48.5 %collective-permute-done.10 = bf16[1024,512]{0,1:T(8,128)(2,1)} collective-permute-done((bf16[1024,512]{0,1:T(8,128)(2,1)}, bf16[1024,512]{0,1:T(8,128)(2,1)}, u32[]{:S(2)}, u32[]{:S(2)}) %collective-permute-start.10) | collective-permute-done | bytes 1048608 | tf_op jit(solution)/shard_map/ppermute | solution.py:363
  436.6 9.8 fusion.88
  446.4 6.6 collective-permute-done.9
  453.0 20.2 %collective-permute-done.11 = bf16[1024,512]{0,1:T(8,128)(2,1)} collective-permute-done((bf16[1024,512]{0,1:T(8,128)(2,1)}, bf16[1024,512]{0,1:T(8,128)(2,1)}, u32[]{:S(2)}, u32[]{:S(2)}) %collective-permute-start.11) | collective-permute-done | bytes 1048608 | tf_op jit(solution)/shard_map/ppermute | solution.py:363
  473.2 8.6 convert_reduce_fusion.1
  483.2 8.5 convolution_convert_fusion.2
  492.0 9.6 convolution_convert_fusion.3
  502.3 36.2 %reduce-scatter.9.cloned.1.call-done = bf16[128,2048]{1,0:T(8,128)(2,1)} async-done(((bf16[1024,2048]{1,0:T(8,128)(2,1)}), bf16[128,2048]{1,0:T(8,128)(2,1)}) %reduce-scatter.9.cloned.1.call-update) | async-done | bytes 524304 | tf_op jit(solution)/shard_map/reduce_scatter | solution.py:552
  540.8 49.7 %reduce-scatter.7.cloned.1.call-done = bf16[128,2048]{1,0:T(8,128)(2,1)} async-done(((bf16[1024,2048]{1,0:T(8,128)(2,1)}), bf16[128,2048]{1,0:T(8,128)(2,1)}) %reduce-scatter.7.cloned.1.call-update) | async-done | bytes 524304 | tf_op jit(solution)/shard_map/reduce_scatter | solution.py:552
  596.7 7.4 fusion.153
  610.6 14.5 %all-gather.12.cloned.1.call-done = bf16[1024,2048]{1,0:T(8,128)(2,1)} async-done(((bf16[128,2048]{1,0:T(8,128)(2,1)}), bf16[1024,2048]{1,0:T(8,128)(2,1)}) %all-gather.12.cloned.1.call-update) | async-done | bytes 4194320 | tf_op jit(solution)/shard_map/all_gather | solution.py:585
  628.8 5.7 fusion.49
  634.5 5.7 fusion.102
  640.2 14.8 %fusion.55 = f32[1024,2,128]{0,2,1:T(8,128)} fusion(bf16[1024,2,128]{0,2,1:T(8,128)(2,1)} %get-tuple-element.76, f32[2,1024,1024]{1,2,0:T(8,128)} %fusion.102, f32[2,1024,1024]{1,2,0:T(8,128)} %get-tuple-element.118, f32[2,1024]{1,0:T(2,128)S(1)} %get-tuple-element.117), kind=kOutput, calls=%fused_computation.76 | convolution fusion | flops 551554048 | bytes 18358272 | tf_op jit(solution)/shard_map/hqk,qhd->khd/dot_general | solution.py:596
  655.1 15.6 %broadcast_multiply_fusion.1 = (f32[1024,2,128]{0,2,1:T(8,128)}, f32[1024,2,128]{0,2,1:T(8,128)}, f32[1024,2,128]{0,2,1:T(8,128)}) fusion(f32[1024,128]{0,1:T(8,128)S(1)} %copy-done.18, f32[1024,2,128]{0,2,1:T(8,128)} %fusion.55, bf16[1024,2,128]{0,2,1:T(8,128)(2,1)S(1)} %copy-done.33, f32[2,1024,1024]{1,2,0:T(8,128)} %fusion.102, ...), kind=kOutput, calls=%fused_computation.171 | convolution fusion | flops 552078336 | bytes 22028288 | tf_op jit(solution)/shard_map/hqk,khd->qhd/dot_general | solution.py:595
  675.6 7.1 convolution_convert_fusion.1
  682.8 11.5 %fusion.34 = f32[1024,2048]{1,0:T(8,128)} fusion(bf16[1024,2048]{1,0:T(8,128)(2,1)} %all-gather.10.cloned.1.call-done, f32[1024]{0:T(1024)S(1)} %broadcast_multiply_fusion.4, f32[1024,1024]{1,0:T(8,128)} %fusion.88, f32[1024]{0:T(1024)S(1)} %bitcast.350, s32[1024]{0:T(1024)S(1)} %add_select_fusion, s32[1024]{0:T(1024)S(1)} %broadcast_in_dim_squeeze.9), kind=kOutput, calls=%fused_computation.54 | convolution fusion | flops 4307550208 | bytes 16793600 | tf_op jit(solution)/shard_map/dot_general | solution.py:404
  694.3 11.8 %reshape.970 = f32[1024,2,2,512]{3,2,1,0:T(2,128)} reshape(f32[1024,2048]{1,0:T(8,128)} %fusion.34) | data formatting | bytes 16777216 | tf_op jit(solution)/shard_map/reshape | solution.py:637
  706.0 5.8 copy.369
  729.8 9.2 collective-permute-done.24
  742.7 6.4 copy.336
  749.2 9.3 copy.322
  761.4 37.4 %collective-permute-done.22 = bf16[512,1024]{1,0:T(8,128)(2,1)} collective-permute-done((bf16[512,1024]{1,0:T(8,128)(2,1)}, bf16[512,1024]{1,0:T(8,128)(2,1)}, u32[]{:S(2)}, u32[]{:S(2)}) %collective-permute-start.22) | collective-permute-done | bytes 1048608 | tf_op jit(solution)/shard_map/ppermute | solution.py:363
  806.0 14.5 %collective-permute-done.25 = bf16[1024,512]{1,0:T(8,128)(2,1)} collective-permute-done((bf16[1024,512]{1,0:T(8,128)(2,1)}, bf16[1024,512]{1,0:T(8,128)(2,1)}, u32[]{:S(2)}, u32[]{:S(2)}) %collective-permute-start.25) | collective-permute-done | bytes 1048608 | tf_op jit(solution)/shard_map/ppermute | solution.py:363
  834.4 6.5 copy.338
  847.2 5.9 collective-permute-done.15
  855.8 19.7 %collective-permute-done.18 = bf16[256,512]{1,0:T(8,128)(2,1)S(1)} collective-permute-done((bf16[256,512]{1,0:T(8,128)(2,1)S(1)}, bf16[256,512]{1,0:T(8,128)(2,1)S(1)}, u32[]{:S(2)}, u32[]{:S(2)}) %collective-permute-start.18) | collective-permute-done | bytes 262176 | tf_op jit(solution)/shard_map/ppermute | solution.py:363
  879.9 21.1 %collective-permute-done.19 = bf16[256,512]{1,0:T(8,128)(2,1)} collective-permute-done((bf16[256,512]{1,0:T(8,128)(2,1)}, bf16[256,512]{1,0:T(8,128)(2,1)}, u32[]{:S(2)}, u32[]{:S(2)}) %collective-permute-start.19) | collective-permute-done | bytes 262176 | tf_op jit(solution)/shard_map/ppermute | solution.py:363
  917.2 4.7 all-to-all-done.11
  936.5 13.1 %all-to-all-done.5 = bf16[4,32,2048]{2,1,0:T(8,128)(2,1)S(1)} async-done(((bf16[4,32,2048]{2,1,0:T(8,128)(2,1)}), bf16[4,32,2048]{2,1,0:T(8,128)(2,1)S(1)}, u32[]{:S(2)}, u32[]{:S(2)}) %all-to-all-start.5) | async-done | bytes 524320 | tf_op jit(solution)/shard_map/all_to_all | solution.py:623
  960.4 5.1 all-to-all-done.8
  965.5 4.2 all-to-all-start.7
  978.5 72.6 %all-reduce.7.cloned.1.call-done = f32[16,2240]{1,0:T(8,128)} async-done(((f32[16,2240]{1,0:T(8,128)}), f32[16,2240]{1,0:T(8,128)}) %all-reduce.7.cloned.1.call-update) | async-done | bytes 143376
  1052.5 5.0 psum.7
  (410 shorter events, 242.9 us)
Async XLA Ops:
  10.1 20.7 %all-to-all-start = ((bf16[4,32,2048]{2,1,0:T(8,128)(2,1)}), bf16[4,32,2048]{2,1,0:T(8,128)(2,1)S(1)}, u32[]{:S(2)}, u32[]{:S(2)}) async-start(bf16[4,32,2048]{2,1,0:T(8,128)(2,1)} %constant_dynamic-slice_fusion.8), calls=%async_computation | async-start | bytes 1048576 | tf_op jit(solution)/shard_map/all_to_all | solution.py:493
  16.3 115.0 %all-reduce.5.cloned.1.call-start = ((), (), s32[]{:S(2)}) async-start(), calls=%async_computation.24 | async-start | bytes 176128
  27.1 173.0 %all-gather.6.cloned.1.call-start = ((), (), s32[]{:S(2)}) async-start(), calls=%async_computation.16 | async-start | bytes 4718592 | tf_op jit(solution)/shard_map/all_gather | solution.py:497
  36.3 96.9 %all-to-all-start.1 = ((bf16[4,128,3,2,128]{4,3,2,1,0:T(2,128)(2,1)}), bf16[4,128,3,2,128]{4,3,2,1,0:T(2,128)(2,1)S(1)}, u32[]{:S(2)}, u32[]{:S(2)}) async-start(bf16[4,128,3,2,128]{4,3,2,1,0:T(2,128)(2,1)} %bitcast.271), calls=%async_computation.1 | async-start | bytes 1572864 | tf_op jit(solution)/shard_map/all_to_all | solution.py:502
  43.4 171.3 %copy-start.10 = (f32[1024,128]{0,1:T(8,128)}, f32[1024,128]{0,1:T(8,128)S(1)}, u32[]{:S(2)}) copy-start(f32[1024,128]{0,1:T(8,128)S(1)} %get-tuple-element.97) | copy-start | bytes 1572868
  43.4 171.3 %copy-start.17 = (f32[1024,128]{0,1:T(8,128)}, f32[1024,128]{0,1:T(8,128)S(1)}, u32[]{:S(2)}) copy-start(f32[1024,128]{0,1:T(8,128)S(1)} %get-tuple-element.98) | copy-start | bytes 1572868
  133.3 44.2 %all-to-all-start.2 = ((bf16[4,256,128]{2,1,0:T(8,128)(2,1)}), bf16[4,256,128]{2,1,0:T(8,128)(2,1)S(1)}, u32[]{:S(2)}, u32[]{:S(2)}) async-start(bf16[4,256,128]{2,1,0:T(8,128)(2,1)} %bitcast.24), calls=%async_computation.2 | async-start | bytes 524288 | tf_op jit(solution)/shard_map/all_to_all | solution.py:502
  137.4 143.3 %reduce-scatter.5.cloned.1.call-start = ((), (), s32[]{:S(2)}) async-start(), calls=%async_computation.17 | async-start | bytes 4718592 | tf_op jit(solution)/shard_map/reduce_scatter | solution.py:552
  137.7 37.8 %collective-permute-start.1 = (bf16[512,768]{1,0:T(8,128)(2,1)S(1)}, bf16[512,768]{1,0:T(8,128)(2,1)S(1)}, u32[]{:S(2)}, u32[]{:S(2)}) collective-permute-start(bf16[512,768]{1,0:T(8,128)(2,1)S(1)} %reshape.925), channel_id=1, source_target_pairs={{0,16},{16,0},{1,17},{17,1},{2,18},{18,2},{3,19},{19,3},{4,20},{20... | collective-permute-start | bytes 2359304 | tf_op jit(solution)/shard_map/ppermute | solution.py:363
  142.1 52.8 %collective-permute-start = (bf16[512,768]{1,0:T(8,128)(2,1)S(1)}, bf16[512,768]{1,0:T(8,128)(2,1)}, u32[]{:S(2)}, u32[]{:S(2)}) collective-permute-start(bf16[512,768]{1,0:T(8,128)(2,1)S(1)} %reshape.925), channel_id=1, source_target_pairs={{0,4},{4,0},{1,5},{5,1},{2,6},{6,2},{3,7},{7,3},{8,12},{12,8},{9,1... | collective-permute-start | bytes 2359304 | tf_op jit(solution)/shard_map/ppermute | solution.py:363
  175.6 22.4 %collective-permute-start.2 = (bf16[512,768]{1,0:T(8,128)(2,1)S(1)}, bf16[512,768]{1,0:T(8,128)(2,1)}, u32[]{:S(2)}, u32[]{:S(2)}) collective-permute-start(bf16[512,768]{1,0:T(8,128)(2,1)S(1)} %collective-permute-done.1), channel_id=1, source_target_pairs={{0,4},{4,0},{1,5},{5,1},{2,6},{6,2},{3,7},{7,3},{8,12},{12,8},{9,1... | collective-permute-start | bytes 2359304 | tf_op jit(solution)/shard_map/ppermute | solution.py:363
  178.4 14.6 %collective-permute-start.4 = (bf16[256,512]{0,1:T(8,128)(2,1)}, bf16[256,512]{0,1:T(8,128)(2,1)}, u32[]{:S(2)}, u32[]{:S(2)}) collective-permute-start(bf16[256,512]{0,1:T(8,128)(2,1)} %bitcast.317), channel_id=1, source_target_pairs={{0,16},{16,0},{1,17},{17,1},{2,18},{18,2},{3,19},{19,3},{4,20},{20... | collective-permute-start | bytes 786440 | tf_op jit(solution)/shard_map/ppermute | solution.py:363
  181.3 48.4 %collective-permute-start.3 = (bf16[256,512]{0,1:T(8,128)(2,1)}, bf16[256,512]{0,1:T(8,128)(2,1)}, u32[]{:S(2)}, u32[]{:S(2)}) collective-permute-start(bf16[256,512]{0,1:T(8,128)(2,1)} %bitcast.318), channel_id=1, source_target_pairs={{0,4},{4,0},{1,5},{5,1},{2,6},{6,2},{3,7},{7,3},{8,12},{12,8},{9,1... | collective-permute-start | bytes 786440 | tf_op jit(solution)/shard_map/ppermute | solution.py:363
  193.0 36.8 %collective-permute-start.5 = (bf16[256,512]{0,1:T(8,128)(2,1)}, bf16[256,512]{0,1:T(8,128)(2,1)}, u32[]{:S(2)}, u32[]{:S(2)}) collective-permute-start(bf16[256,512]{0,1:T(8,128)(2,1)} %collective-permute-done.4), channel_id=1, source_target_pairs={{0,4},{4,0},{1,5},{5,1},{2,6},{6,2},{3,7},{7,3},{8,12},{12,8},{9,1... | collective-permute-start | bytes 786440 | tf_op jit(solution)/shard_map/ppermute | solution.py:363
  234.4 202.1 %all-gather.8.cloned.1.call-start = ((), (), s32[]{:S(2)}) async-start(), calls=%async_computation.18 | async-start | bytes 4718592 | tf_op jit(solution)/shard_map/all_gather | solution.py:561
  285.8 187.4 %all-gather.10.cloned.1.call-start = ((), (), s32[]{:S(2)}) async-start(), calls=%async_computation.20 | async-start | bytes 4718592 | tf_op jit(solution)/shard_map/all_gather | solution.py:499
  331.3 49.1 %all-to-all-start.4 = ((bf16[4,1024,128]{2,1,0:T(8,128)(2,1)}), bf16[4,1024,128]{2,1,0:T(8,128)(2,1)S(1)}, u32[]{:S(2)}, u32[]{:S(2)}) async-start(bf16[4,1024,128]{2,1,0:T(8,128)(2,1)} %bitcast.297), calls=%async_computation.5 | async-start | bytes 2097152 | tf_op jit(solution)/shard_map/all_to_all | solution.py:502
  334.8 203.7 %reduce-scatter.9.cloned.1.call-start = ((), (), s32[]{:S(2)}) async-start(), calls=%async_computation.21 | async-start | bytes 4718592 | tf_op jit(solution)/shard_map/reduce_scatter | solution.py:552
  337.1 46.6 %collective-permute-start.7 = (bf16[512,1024]{1,0:T(8,128)(2,1)}, bf16[512,1024]{1,0:T(8,128)(2,1)}, u32[]{:S(2)}, u32[]{:S(2)}) collective-permute-start(bf16[512,1024]{1,0:T(8,128)(2,1)} %bitcast.302), channel_id=1, source_target_pairs={{0,16},{16,0},{1,17},{17,1},{2,18},{18,2},{3,19},{19,3},{4,20},{20... | collective-permute-start | bytes 3145736 | tf_op jit(solution)/shard_map/ppermute | solution.py:363
  381.6 53.4 %collective-permute-start.10 = (bf16[1024,512]{0,1:T(8,128)(2,1)}, bf16[1024,512]{0,1:T(8,128)(2,1)}, u32[]{:S(2)}, u32[]{:S(2)}) collective-permute-start(bf16[1024,512]{0,1:T(8,128)(2,1)} %bitcast.298), channel_id=1, source_target_pairs={{0,16},{16,0},{1,17},{17,1},{2,18},{18,2},{3,19},{19,3},{4,20},{20... | collective-permute-start | bytes 3145736 | tf_op jit(solution)/shard_map/ppermute | solution.py:363
  381.6 54.9 %collective-permute-start.6 = (bf16[512,1024]{1,0:T(8,128)(2,1)}, bf16[512,1024]{1,0:T(8,128)(2,1)}, u32[]{:S(2)}, u32[]{:S(2)}) collective-permute-start(bf16[512,1024]{1,0:T(8,128)(2,1)} %bitcast.303), channel_id=1, source_target_pairs={{0,4},{4,0},{1,5},{5,1},{2,6},{6,2},{3,7},{7,3},{8,12},{12,8},{9,1... | collective-permute-start | bytes 3145736 | tf_op jit(solution)/shard_map/ppermute | solution.py:363
  383.7 52.9 %collective-permute-start.8 = (bf16[512,1024]{1,0:T(8,128)(2,1)}, bf16[512,1024]{1,0:T(8,128)(2,1)}, u32[]{:S(2)}, u32[]{:S(2)}) collective-permute-start(bf16[512,1024]{1,0:T(8,128)(2,1)} %collective-permute-done.7), channel_id=1, source_target_pairs={{0,4},{4,0},{1,5},{5,1},{2,6},{6,2},{3,7},{7,3},{8,12},{12,8},{9,1... | collective-permute-start | bytes 3145736 | tf_op jit(solution)/shard_map/ppermute | solution.py:363
  386.0 67.0 %collective-permute-start.9 = (bf16[1024,512]{0,1:T(8,128)(2,1)}, bf16[1024,512]{0,1:T(8,128)(2,1)}, u32[]{:S(2)}, u32[]{:S(2)}) collective-permute-start(bf16[1024,512]{0,1:T(8,128)(2,1)} %bitcast.299), channel_id=1, source_target_pairs={{0,4},{4,0},{1,5},{5,1},{2,6},{6,2},{3,7},{7,3},{8,12},{12,8},{9,1... | collective-permute-start | bytes 3145736 | tf_op jit(solution)/shard_map/ppermute | solution.py:363
  435.1 38.2 %collective-permute-start.11 = (bf16[1024,512]{0,1:T(8,128)(2,1)}, bf16[1024,512]{0,1:T(8,128)(2,1)}, u32[]{:S(2)}, u32[]{:S(2)}) collective-permute-start(bf16[1024,512]{0,1:T(8,128)(2,1)} %collective-permute-done.10), channel_id=1, source_target_pairs={{0,4},{4,0},{1,5},{5,1},{2,6},{6,2},{3,7},{7,3},{8,12},{12,8},{9,1... | collective-permute-start | bytes 3145736 | tf_op jit(solution)/shard_map/ppermute | solution.py:363
  491.7 98.8 %reduce-scatter.7.cloned.1.call-start = ((), (), s32[]{:S(2)}) async-start(), calls=%async_computation.19 | async-start | bytes 4718592 | tf_op jit(solution)/shard_map/reduce_scatter | solution.py:552
  501.6 123.5 %all-gather.12.cloned.1.call-start = ((), (), s32[]{:S(2)}) async-start(), calls=%async_computation.22 | async-start | bytes 4718592 | tf_op jit(solution)/shard_map/all_gather | solution.py:585
  593.7 316.8 %reduce-scatter.11.cloned.1.call-start = ((), (), s32[]{:S(2)}) async-start(), calls=%async_computation.23 | async-start | bytes 4718592 | tf_op jit(solution)/shard_map/reduce_scatter | solution.py:552
  609.2 115.0 %collective-permute-start.21 = (bf16[512,1024]{1,0:T(8,128)(2,1)}, bf16[512,1024]{1,0:T(8,128)(2,1)}, u32[]{:S(2)}, u32[]{:S(2)}) collective-permute-start(bf16[512,1024]{1,0:T(8,128)(2,1)} %get-tuple-element.74), channel_id=1, source_target_pairs={{0,4},{4,0},{1,5},{5,1},{2,6},{6,2},{3,7},{7,3},{8,12},{12,8},{9,1... | collective-permute-start | bytes 3145736 | tf_op jit(solution)/shard_map/ppermute | solution.py:363
  713.0 26.0 %collective-permute-start.24 = (bf16[1024,512]{1,0:T(8,128)(2,1)S(1)}, bf16[1024,512]{1,0:T(8,128)(2,1)S(1)}, u32[]{:S(2)}, u32[]{:S(2)}) collective-permute-start(bf16[1024,512]{1,0:T(8,128)(2,1)S(1)} %get-tuple-element.72), channel_id=1, source_target_pairs={{0,4},{4,0},{1,5},{5,1},{2,6},{6,2},{3,7},{7,3},{8,12},{12,8},{9,1... | collective-permute-start | bytes 3145736 | tf_op jit(solution)/shard_map/ppermute | solution.py:363
  722.1 39.3 %collective-permute-start.20 = (bf16[512,1024]{1,0:T(8,128)(2,1)}, bf16[512,1024]{1,0:T(8,128)(2,1)S(1)}, u32[]{:S(2)}, u32[]{:S(2)}) collective-permute-start(bf16[512,1024]{1,0:T(8,128)(2,1)} %get-tuple-element.73), channel_id=1, source_target_pairs={{0,4},{4,0},{1,5},{5,1},{2,6},{6,2},{3,7},{7,3},{8,12},{12,8},{9,1... | collective-permute-start | bytes 3145736 | tf_op jit(solution)/shard_map/ppermute | solution.py:363
  723.0 83.0 %collective-permute-start.23 = (bf16[1024,512]{1,0:T(8,128)(2,1)}, bf16[1024,512]{1,0:T(8,128)(2,1)}, u32[]{:S(2)}, u32[]{:S(2)}) collective-permute-start(bf16[1024,512]{1,0:T(8,128)(2,1)} %get-tuple-element.71), channel_id=1, source_target_pairs={{0,4},{4,0},{1,5},{5,1},{2,6},{6,2},{3,7},{7,3},{8,12},{12,8},{9,1... | collective-permute-start | bytes 3145736 | tf_op jit(solution)/shard_map/ppermute | solution.py:363
  727.4 71.4 %collective-permute-start.22 = (bf16[512,1024]{1,0:T(8,128)(2,1)}, bf16[512,1024]{1,0:T(8,128)(2,1)}, u32[]{:S(2)}, u32[]{:S(2)}) collective-permute-start(bf16[512,1024]{1,0:T(8,128)(2,1)} %fusion.25), channel_id=1, source_target_pairs={{0,16},{16,0},{1,17},{17,1},{2,18},{18,2},{3,19},{19,3},{4,20},{20... | collective-permute-start | bytes 3145736 | tf_op jit(solution)/shard_map/ppermute | solution.py:363
  740.3 80.2 %collective-permute-start.25 = (bf16[1024,512]{1,0:T(8,128)(2,1)}, bf16[1024,512]{1,0:T(8,128)(2,1)}, u32[]{:S(2)}, u32[]{:S(2)}) collective-permute-start(bf16[1024,512]{1,0:T(8,128)(2,1)} %fusion.29), channel_id=1, source_target_pairs={{0,16},{16,0},{1,17},{17,1},{2,18},{18,2},{3,19},{19,3},{4,20},{20... | collective-permute-start | bytes 3145736 | tf_op jit(solution)/shard_map/ppermute | solution.py:363
  802.2 100.7 %all-to-all-start.10 = ((bf16[4,128,1024]{2,1,0:T(8,128)(2,1)}), bf16[4,128,1024]{2,1,0:T(8,128)(2,1)S(1)}, u32[]{:S(2)}, u32[]{:S(2)}) async-start(bf16[4,128,1024]{2,1,0:T(8,128)(2,1)} %bitcast.95), calls=%async_computation.14 | async-start | bytes 2097152 | tf_op jit(solution)/shard_map/all_to_all | solution.py:502
  832.3 20.8 %collective-permute-start.15 = (bf16[512,768]{1,0:T(8,128)(2,1)}, bf16[512,768]{1,0:T(8,128)(2,1)}, u32[]{:S(2)}, u32[]{:S(2)}) collective-permute-start(bf16[512,768]{1,0:T(8,128)(2,1)} %get-tuple-element.78), channel_id=1, source_target_pairs={{0,4},{4,0},{1,5},{5,1},{2,6},{6,2},{3,7},{7,3},{8,12},{12,8},{9,1... | collective-permute-start | bytes 2359304 | tf_op jit(solution)/shard_map/ppermute | solution.py:363
  833.5 73.9 %collective-permute-start.14 = (bf16[512,768]{1,0:T(8,128)(2,1)}, bf16[512,768]{1,0:T(8,128)(2,1)}, u32[]{:S(2)}, u32[]{:S(2)}) collective-permute-start(bf16[512,768]{1,0:T(8,128)(2,1)} %get-tuple-element.77), channel_id=1, source_target_pairs={{0,4},{4,0},{1,5},{5,1},{2,6},{6,2},{3,7},{7,3},{8,12},{12,8},{9,1... | collective-permute-start | bytes 2359304 | tf_op jit(solution)/shard_map/ppermute | solution.py:363
  845.2 30.3 %collective-permute-start.18 = (bf16[256,512]{1,0:T(8,128)(2,1)S(1)}, bf16[256,512]{1,0:T(8,128)(2,1)S(1)}, u32[]{:S(2)}, u32[]{:S(2)}) collective-permute-start(bf16[256,512]{1,0:T(8,128)(2,1)S(1)} %get-tuple-element.84), channel_id=1, source_target_pairs={{0,4},{4,0},{1,5},{5,1},{2,6},{6,2},{3,7},{7,3},{8,12},{12,8},{9,1... | collective-permute-start | bytes 786440 | tf_op jit(solution)/shard_map/ppermute | solution.py:363
  846.4 33.5 %collective-permute-start.17 = (bf16[256,512]{1,0:T(8,128)(2,1)}, bf16[256,512]{1,0:T(8,128)(2,1)S(1)}, u32[]{:S(2)}, u32[]{:S(2)}) collective-permute-start(bf16[256,512]{1,0:T(8,128)(2,1)} %get-tuple-element.83), channel_id=1, source_target_pairs={{0,4},{4,0},{1,5},{5,1},{2,6},{6,2},{3,7},{7,3},{8,12},{12,8},{9,1... | collective-permute-start | bytes 786440 | tf_op jit(solution)/shard_map/ppermute | solution.py:363
  855.8 51.7 %collective-permute-start.16 = (bf16[512,768]{1,0:T(8,128)(2,1)}, bf16[512,768]{1,0:T(8,128)(2,1)}, u32[]{:S(2)}, u32[]{:S(2)}) collective-permute-start(bf16[512,768]{1,0:T(8,128)(2,1)} %fusion.36), channel_id=1, source_target_pairs={{0,16},{16,0},{1,17},{17,1},{2,18},{18,2},{3,19},{19,3},{4,20},{20... | collective-permute-start | bytes 2359304 | tf_op jit(solution)/shard_map/ppermute | solution.py:363
  876.3 24.7 %collective-permute-start.19 = (bf16[256,512]{1,0:T(8,128)(2,1)}, bf16[256,512]{1,0:T(8,128)(2,1)}, u32[]{:S(2)}, u32[]{:S(2)}) collective-permute-start(bf16[256,512]{1,0:T(8,128)(2,1)} %fusion.93), channel_id=1, source_target_pairs={{0,16},{16,0},{1,17},{17,1},{2,18},{18,2},{3,19},{19,3},{4,20},{20... | collective-permute-start | bytes 786440 | tf_op jit(solution)/shard_map/ppermute | solution.py:363
  903.9 18.0 %all-to-all-start.11 = ((bf16[4,1024,128]{2,1,0:T(8,128)(2,1)}), bf16[4,1024,128]{2,1,0:T(8,128)(2,1)S(1)}, u32[]{:S(2)}, u32[]{:S(2)}) async-start(bf16[4,1024,128]{2,1,0:T(8,128)(2,1)} %bitcast_bitcast_fusion), calls=%async_computation.15 | async-start | bytes 2097152 | tf_op jit(solution)/shard_map/all_to_all | solution.py:502
  921.9 9.7 all-to-all-start.9
  931.6 18.0 %all-to-all-start.5 = ((bf16[4,32,2048]{2,1,0:T(8,128)(2,1)}), bf16[4,32,2048]{2,1,0:T(8,128)(2,1)S(1)}, u32[]{:S(2)}, u32[]{:S(2)}) async-start(bf16[4,32,2048]{2,1,0:T(8,128)(2,1)} %reshape_reshape.17), calls=%async_computation.7 | async-start | bytes 1048576 | tf_op jit(solution)/shard_map/all_to_all | solution.py:623
  950.4 15.1 %all-to-all-start.8 = ((bf16[4,128,768]{2,1,0:T(8,128)(2,1)}), bf16[4,128,768]{2,1,0:T(8,128)(2,1)S(1)}, u32[]{:S(2)}, u32[]{:S(2)}) async-start(bf16[4,128,768]{2,1,0:T(8,128)(2,1)} %bitcast.74), calls=%async_computation.12 | async-start | bytes 1572864 | tf_op jit(solution)/shard_map/all_to_all | solution.py:502
  953.9 97.2 %all-reduce.7.cloned.1.call-start = ((), (), s32[]{:S(2)}) async-start(), calls=%async_computation.25 | async-start | bytes 294912
  959.4 104.7 %collective-permute-start.12 = (bf16[4,32,2048]{2,1,0:T(8,128)(2,1)}, bf16[4,32,2048]{2,1,0:T(8,128)(2,1)}, u32[]{:S(2)}, u32[]{:S(2)}) collective-permute-start(bf16[4,32,2048]{2,1,0:T(8,128)(2,1)} %copy-done.20), channel_id=1, source_target_pairs={{0,1},{1,0},{2,3},{3,2},{4,5},{5,4},{6,7},{7,6},{8,9},{9,8},{10,11... | collective-permute-start | bytes 1572872 | tf_op jit(solution)/shard_map/ppermute | solution.py:363
  965.5 92.0 %all-to-all-start.7 = ((bf16[4,32,2048]{2,1,0:T(8,128)(2,1)}), bf16[4,32,2048]{2,1,0:T(8,128)(2,1)}, u32[]{:S(2)}, u32[]{:S(2)}) async-start(bf16[4,32,2048]{2,1,0:T(8,128)(2,1)} %convert_element_type.351), calls=%async_computation.11 | async-start | bytes 1048576 | tf_op jit(solution)/shard_map/all_to_all | solution.py:623
  1057.5 12.5 %collective-permute-start.13 = (bf16[4,32,2048]{2,1,0:T(8,128)(2,1)}, bf16[4,32,2048]{2,1,0:T(8,128)(2,1)S(1)}, u32[]{:S(2)}, u32[]{:S(2)}) collective-permute-start(bf16[4,32,2048]{2,1,0:T(8,128)(2,1)} %all-to-all-done.7), channel_id=1, source_target_pairs={{0,1},{1,0},{2,3},{3,2},{4,5},{5,4},{6,7},{7,6},{8,9},{9,8},{10,11... | collective-permute-start | bytes 1572872 | tf_op jit(solution)/shard_map/ppermute | solution.py:363
  (68 other events, 1376.0 us)
Sparse Core Ops, SparseCore 0:
  27.2 104.0 all-reduce.4
  959.5 91.5 all-reduce.6
Sparse Core Ops, SparseCore 1:
  35.0 35.2 all-gather.5
  234.5 46.1 reduce-scatter.4
  285.9 38.3 all-gather.7
  326.6 63.5 all-gather.9
  491.8 46.6 reduce-scatter.8
  540.9 49.6 reduce-scatter.6
  593.8 31.3 all-gather.11
  682.9 47.5 reduce-scatter.10

commit v2 on v1

--- a/solution.py
+++ b/solution.py
@@ -1,8 +1,11 @@
+import functools
 import math
 
 import jax
 import jax.numpy as jnp
 from jax import lax
+from jax.experimental import pallas as pl
+from jax.experimental.pallas import tpu as pltpu
 from jax.sharding import Mesh
 from jax.sharding import PartitionSpec as P
 
@@ -353,7 +356,7 @@
 
 
 ROWS = ("zh", "zl", "x", "c")
-GROUP = ("zl", "y", "c")
+GROUP = ("c", "zl", "y")
 PARTS = ("zh", "x")
 LOW = jnp.bfloat16
 WIDE = jnp.float32
@@ -385,23 +388,360 @@
     return value.reshape(lead + (width,))
 
 
-def gather_parts(piece, axis):
-    over_x = swap(piece, "x")
-    over_z = swap(piece, "zh")
-    over_both = swap(over_z, "x")
-    return jnp.concatenate([piece, over_x, over_z, over_both], axis=axis)
-
-
-def scatter_parts(pieces):
-    stay, send = pieces[0], pieces[1]
-    got = [swap(p.astype(LOW), "x") for p in send]
-    first = stay[1] + got[1].astype(WIDE)
-    over_z = swap(first.astype(LOW), "zh")
-    return stay[0] + got[0].astype(WIDE) + over_z.astype(WIDE)
+def tie(*values):
+    return lax.optimization_barrier(values)
 
 
 def dot_to(left, right, dims):
     return lax.dot_general(left, right, (dims, ((), ())), preferred_element_type=WIDE)
+
+
+def gather_over(value, axes, bits):
+    for axis, bit in zip(axes, bits):
+        other = swap(value, axis)
+        value = jnp.where(
+            bit == 0,
+            jnp.concatenate([value, other], axis=0),
+            jnp.concatenate([other, value], axis=0),
+        )
+    return value
+
+
+def reduce_rows(value, zh, zl, x, c):
+    value = value.reshape(2, 2, 2, 2, -1)
+    for axis, at, bit in (("zh", 0, zh), ("zl", 0, zl), ("x", 0, x), ("c", 0, c)):
+        keep = lax.dynamic_index_in_dim(value, bit, at, keepdims=False)
+        send = lax.dynamic_index_in_dim(value, 1 - bit, at, keepdims=False)
+        value = keep + swap(send, axis)
+    return value
+
+
+BLOCK_Q = 256
+NEVER = -1e30
+
+
+def chunks(bits_ref, width):
+    run = width // 8
+    for at in range(8):
+        zh, x, zl = at // 4, at // 2 % 2, at % 2
+        theirs = ((zh ^ bits_ref[0]) * 2 + zl) * 2 + (x ^ bits_ref[1])
+        yield at * run, pl.multiple_of(theirs * run, run)
+
+
+def norm_kernel(bits_ref, x_ref, gain_ref, shift_ref, router_ref, out_ref, logits_ref):
+    width = x_ref.shape[1]
+    rows = x_ref[...].astype(WIDE)
+    mean = jnp.mean(rows, axis=-1, keepdims=True)
+    center = rows - mean
+    inverse = lax.rsqrt(jnp.mean(center * center, axis=-1, keepdims=True) + EPSILON)
+    logits = None
+    for mine, theirs in chunks(bits_ref, width):
+        at = slice(mine, mine + width // 8)
+        part = (x_ref[:, pl.ds(theirs, width // 8)].astype(WIDE) - mean) * inverse
+        low = (part * gain_ref[:, at] + shift_ref[:, at]).astype(LOW)
+        out_ref[:, at] = low
+        got = dot_to(low, router_ref[:, at], ((1,), (1,)))
+        logits = got if logits is None else logits + got
+    logits_ref[...] = logits
+
+
+def norm_rows(bits, rows, gain, shift, router):
+    length, width = rows.shape
+    n = router.shape[0]
+    return pl.pallas_call(
+        norm_kernel,
+        grid_spec=pltpu.PrefetchScalarGridSpec(
+            num_scalar_prefetch=1,
+            grid=(length // BLOCK_Q,),
+            in_specs=[
+                pl.BlockSpec((BLOCK_Q, width), lambda i, bits: (i, 0)),
+                pl.BlockSpec((1, width), lambda i, bits: (0, 0)),
+                pl.BlockSpec((1, width), lambda i, bits: (0, 0)),
+                pl.BlockSpec((n, width), lambda i, bits: (0, 0)),
+            ],
+            out_specs=[
+                pl.BlockSpec((BLOCK_Q, width), lambda i, bits: (i, 0)),
+                pl.BlockSpec((BLOCK_Q, n), lambda i, bits: (i, 0)),
+            ],
+        ),
+        out_shape=[
+            jax.ShapeDtypeStruct((length, width), LOW),
+            jax.ShapeDtypeStruct((length, n), WIDE),
+        ],
+        name="norm_rows",
+    )(bits, rows, gain, shift, router)
+
+
+def gate_kernel(bits_ref, x_ref, gate_ref, out_ref):
+    width = x_ref.shape[1]
+    gate = gate_ref[...]
+    for mine, theirs in chunks(bits_ref, width):
+        part = x_ref[:, pl.ds(theirs, width // 8)].astype(WIDE) * gate
+        out_ref[:, mine : mine + width // 8] = part.astype(LOW)
+
+
+def gate_rows(bits, rows, gate):
+    length, width = rows.shape
+    return pl.pallas_call(
+        gate_kernel,
+        grid_spec=pltpu.PrefetchScalarGridSpec(
+            num_scalar_prefetch=1,
+            grid=(length // BLOCK_Q,),
+            in_specs=[
+                pl.BlockSpec((BLOCK_Q, width), lambda i, bits: (i, 0)),
+                pl.BlockSpec((BLOCK_Q, 1), lambda i, bits: (i, 0)),
+            ],
+            out_specs=pl.BlockSpec((BLOCK_Q, width), lambda i, bits: (i, 0)),
+        ),
+        out_shape=jax.ShapeDtypeStruct((length, width), LOW),
+        name="gate_rows",
+    )(bits, rows, gate)
+
+
+def add_dots(left_ref, pieces, start=None):
+    at, total = 0, start
+    for piece in pieces:
+        n = piece.shape[0]
+        part = dot_to(left_ref[:, at : at + n], piece[...], ((1,), (0,)))
+        total = part if total is None else total + part
+        at += n
+    return total
+
+
+def by_half(step, away_ref, here_ref, write):
+    half = pl.num_programs(0) // 2
+
+    @pl.when(step < half)
+    def _():
+        write(away_ref)
+
+    @pl.when(step >= half)
+    def _():
+        write(here_ref)
+
+
+def half_specs(steps, rows, width, dtype):
+    half = steps // 2
+    shape = jax.ShapeDtypeStruct((rows * half, width), dtype)
+    return (
+        [
+            pl.BlockSpec((rows, width), lambda i, bit: (jnp.minimum(i, half - 1), 0)),
+            pl.BlockSpec((rows, width), lambda i, bit: (jnp.maximum(i - half, 0), 0)),
+        ],
+        [shape, shape],
+    )
+
+
+def row_spec(steps, rows, width):
+    half = steps // 2
+    return pl.BlockSpec(
+        (rows, width), lambda i, bit: (jnp.where(i < half, i + (1 - bit[0]) * half, i - half + bit[0] * half), 0)
+    )
+
+
+def fixed(value):
+    return pl.BlockSpec(value.shape, lambda *_: (0, 0))
+
+
+def grad_kernel(dz_ref, *refs):
+    pieces, out_ref = refs[:-1], refs[-1]
+    total, at = None, 0
+    for piece in pieces:
+        n = piece.shape[1]
+        part = dot_to(dz_ref[:, at : at + n], piece[...], ((1,), (1,)))
+        total = part if total is None else total + part
+        at += n
+    out_ref[...] = total
+
+
+def hidden_grad_rows(down_grad, downs):
+    length, width = down_grad.shape
+    units = downs[0].shape[0]
+    return pl.pallas_call(
+        grad_kernel,
+        grid=(length // BLOCK_Q,),
+        in_specs=[pl.BlockSpec((BLOCK_Q, width), lambda i: (i, 0))] + [fixed(p) for p in downs],
+        out_specs=pl.BlockSpec((BLOCK_Q, units), lambda i: (i, 0)),
+        out_shape=jax.ShapeDtypeStruct((length, units), WIDE),
+        name="hidden_grad_rows",
+    )(down_grad, *downs)
+
+
+def wide_kernel(bit_ref, left_ref, *refs):
+    pieces, (away_ref, here_ref) = refs[:-2], refs[-2:]
+
+    def write(out_ref):
+        at = 0
+        for piece in pieces:
+            n = piece.shape[1]
+            out_ref[:, at : at + n] = dot_to(left_ref[...], piece[...], ((1,), (0,))).astype(LOW)
+            at += n
+
+    by_half(pl.program_id(0), away_ref, here_ref, write)
+
+
+def wide_rows(bit, left, pieces):
+    length, depth = left.shape
+    rows = BLOCK_Q
+    steps = length // rows
+    width = sum(p.shape[1] for p in pieces)
+    out_specs, out_shape = half_specs(steps, rows, width, LOW)
+    return pl.pallas_call(
+        wide_kernel,
+        grid_spec=pltpu.PrefetchScalarGridSpec(
+            num_scalar_prefetch=1,
+            grid=(steps,),
+            in_specs=[row_spec(steps, rows, depth)] + [fixed(p) for p in pieces],
+            out_specs=out_specs,
+        ),
+        out_shape=out_shape,
+        name="wide_rows",
+    )(bit, left, *pieces)
+
+
+def qkv_kernel(h_ref, *refs):
+    pieces, (bias_ref, cos_ref, sin_ref, out_ref) = refs[:-4], refs[-4:]
+    total = add_dots(h_ref, pieces, bias_ref[...])
+    turned = out_ref.shape[1] // HEAD_DIM * 2 // 3
+    cosine, sine = cos_ref[...], sin_ref[...]
+    for j in range(out_ref.shape[1] // HEAD_DIM):
+        at = slice(j * HEAD_DIM, (j + 1) * HEAD_DIM)
+        part = total[:, at]
+        if j < turned:
+            part = part * cosine + pltpu.roll(part, HEAD_DIM // 2, 1) * sine
+        out_ref[:, at] = part.astype(LOW)
+
+
+def qkv_rows(normed, pieces, bias, cosine, sine):
+    length, width = normed.shape
+    out = bias.shape[1]
+    rows = BLOCK_Q
+    return pl.pallas_call(
+        qkv_kernel,
+        grid=(length // rows,),
+        in_specs=[pl.BlockSpec((rows, width), lambda i: (i, 0))]
+        + [fixed(p) for p in pieces]
+        + [
+            fixed(bias),
+            pl.BlockSpec((rows, HEAD_DIM), lambda i: (i, 0)),
+            pl.BlockSpec((rows, HEAD_DIM), lambda i: (i, 0)),
+        ],
+        out_specs=pl.BlockSpec((rows, out), lambda i: (i, 0)),
+        out_shape=jax.ShapeDtypeStruct((length, out), LOW),
+        name="qkv_rows",
+    )(normed, *pieces, bias, cosine, sine)
+
+
+def attend_kernel(q_ref, k_ref, v_ref, key_ref, span_ref, active_ref, out_ref, lse_ref):
+    scores = dot_to(k_ref[...], q_ref[...], ((1,), (1,))) * (HEAD_DIM**-0.5)
+    key = key_ref[...]
+    allowed = (key >= span_ref[0:1, :]) & (key <= span_ref[1:2, :])
+    scores = jnp.where(allowed, scores, NEVER)
+    top = jnp.max(scores, axis=0, keepdims=True)
+    weights = jnp.exp(scores - top)
+    total = jnp.sum(weights, axis=0, keepdims=True)
+    probs = (weights * (1.0 / total)).astype(LOW)
+    mixed = dot_to(probs, v_ref[...], ((0,), (0,)))
+    out_ref[...] = (mixed * active_ref[0]).astype(LOW)
+    lse_ref[0] = top + jnp.log(total)
+
+
+def turn_back(grad, cosine, sine):
+    lane = lax.broadcasted_iota(jnp.int32, grad.shape, 1)
+    moved = pltpu.roll(grad * sine, HEAD_DIM // 2, 1)
+    return grad * cosine + jnp.where(lane < HEAD_DIM // 2, moved, -moved)
+
+
+def attend_back_kernel(
+    q_ref, k_ref, v_ref, da_ref, w_ref, active_ref, lse_ref,
+    key_ref, span_ref, cos_ref, sin_ref, out_ref, dk_sum, dv_sum,
+):
+    head, step = pl.program_id(0), pl.program_id(1)
+    inner = out_ref.shape[1] // 3
+
+    @pl.when(step == 0)
+    def _():
+        dk_sum[...] = jnp.zeros_like(dk_sum)
+        dv_sum[...] = jnp.zeros_like(dv_sum)
+
+    scale = HEAD_DIM**-0.5
+    query, key = q_ref[...], k_ref[...]
+    grad = dot_to(da_ref[...], w_ref[...], ((1,), (1,)))
+    grad = (grad * active_ref[0]).astype(LOW)
+    scores = dot_to(key, query, ((1,), (1,))) * scale
+    place = key_ref[...]
+    allowed = (place >= span_ref[0:1, :]) & (place <= span_ref[1:2, :])
+    probs = jnp.exp(jnp.where(allowed, scores, NEVER) - lse_ref[0])
+    prob_grad = dot_to(v_ref[...], grad, ((1,), (1,)))
+    delta = jnp.sum(probs * prob_grad, axis=0, keepdims=True)
+    score_grad = (probs * (prob_grad - delta) * scale).astype(LOW)
+    dv_sum[...] += dot_to(probs.astype(LOW), grad, ((1,), (0,)))
+    dk_sum[...] += dot_to(score_grad, query, ((1,), (0,)))
+    dq = dot_to(score_grad, key, ((0,), (0,)))
+    at = pl.ds(pl.multiple_of(step * BLOCK_Q, BLOCK_Q), BLOCK_Q)
+    col = pl.multiple_of(head * HEAD_DIM, HEAD_DIM)
+    dq = turn_back(dq, cos_ref[at, :], sin_ref[at, :])
+    out_ref[at, pl.ds(col, HEAD_DIM)] = dq.astype(LOW)
+
+    @pl.when(step == pl.num_programs(1) - 1)
+    def _():
+        dk = turn_back(dk_sum[...], cos_ref[...], sin_ref[...])
+        out_ref[:, pl.ds(inner + col, HEAD_DIM)] = dk.astype(LOW)
+        out_ref[:, pl.ds(2 * inner + col, HEAD_DIM)] = dv_sum[...].astype(LOW)
+
+
+def attend(qkv, key_place, span, active, heads):
+    length = qkv.shape[0]
+    d = HEAD_DIM
+    n = heads
+    return pl.pallas_call(
+        attend_kernel,
+        grid=(heads, length // BLOCK_Q),
+        in_specs=[
+            pl.BlockSpec((BLOCK_Q, d), lambda h, i: (i, h)),
+            pl.BlockSpec((length, d), lambda h, i: (0, n + h)),
+            pl.BlockSpec((length, d), lambda h, i: (0, 2 * n + h)),
+            pl.BlockSpec((length, 1), lambda h, i: (0, 0)),
+            pl.BlockSpec((2, BLOCK_Q), lambda h, i: (0, i)),
+            pl.BlockSpec((1, BLOCK_Q, 1), lambda h, i: (h, i, 0)),
+        ],
+        out_specs=[
+            pl.BlockSpec((BLOCK_Q, d), lambda h, i: (i, h)),
+            pl.BlockSpec((1, 1, BLOCK_Q), lambda h, i: (h, 0, i)),
+        ],
+        out_shape=[
+            jax.ShapeDtypeStruct((length, heads * d), LOW),
+            jax.ShapeDtypeStruct((heads, 1, length), WIDE),
+        ],
+        name="attend",
+    )(qkv, qkv, qkv, key_place, span, active)
+
+
+def attend_back(qkv, out_grad, w_out, active, lse, key_place, span, cosine, sine, heads):
+    length, width = out_grad.shape
+    d = HEAD_DIM
+    n = heads
+    return pl.pallas_call(
+        attend_back_kernel,
+        grid=(heads, length // BLOCK_Q),
+        in_specs=[
+            pl.BlockSpec((BLOCK_Q, d), lambda h, i: (i, h)),
+            pl.BlockSpec((length, d), lambda h, i: (0, n + h)),
+            pl.BlockSpec((length, d), lambda h, i: (0, 2 * n + h)),
+            pl.BlockSpec((BLOCK_Q, width), lambda h, i: (i, 0)),
+            pl.BlockSpec((d, width), lambda h, i: (h, 0)),
+            pl.BlockSpec((1, BLOCK_Q, 1), lambda h, i: (h, i, 0)),
+            pl.BlockSpec((1, 1, BLOCK_Q), lambda h, i: (h, 0, i)),
+            pl.BlockSpec((length, 1), lambda h, i: (0, 0)),
+            pl.BlockSpec((2, BLOCK_Q), lambda h, i: (0, i)),
+            pl.BlockSpec((length, d), lambda h, i: (0, 0)),
+            pl.BlockSpec((length, d), lambda h, i: (0, 0)),
+        ],
+        out_specs=pl.BlockSpec((length, 3 * heads * d), lambda h, i: (0, 0)),
+        out_shape=jax.ShapeDtypeStruct((length, 3 * heads * d), LOW),
+        scratch_shapes=[pltpu.VMEM((length, d), WIDE), pltpu.VMEM((length, d), WIDE)],
+        name="attend_back",
+    )(qkv, qkv, qkv, out_grad, w_out, active, lse, key_place, span, cosine, sine)
 
 
 def grouped(
@@ -437,9 +777,33 @@
     units = tp_units // 4
     batch = zh * 2 + x
     part = zl * 2 + c
-    place = (zl * 2 + y) * 2 + c
-    scale = HEAD_DIM ** (-0.5)
-
+    place = (c * 2 + zl) * 2 + y
+
+    def exchange(value):
+        return lax.all_to_all(value, ("zl", "c"), 0, 0, tiled=True)
+
+    def keep_and_send(value, bit, at):
+        return (
+            lax.dynamic_index_in_dim(value, bit, at, keepdims=False),
+            lax.dynamic_index_in_dim(value, 1 - bit, at, keepdims=False),
+        )
+
+    def across(pieces):
+        return (
+            pieces[0],
+            swap(pieces[1], "x"),
+            swap(pieces[2], "zh"),
+            lax.ppermute(pieces[3], PARTS, [(i, i ^ 3) for i in range(4)]),
+        )
+
+    def to_batch(value):
+        value = lax.dynamic_slice_in_dim(value, y * half, half, 1)
+        return across(
+            [lax.dynamic_index_in_dim(value, batch ^ k, 0, keepdims=False) for k in range(4)]
+        )
+
+    bits = jnp.stack([zh, x]).astype(jnp.int32)
+    core = c.reshape(1).astype(jnp.int32)
     small = jnp.concatenate(
         [
             first_gain,
@@ -455,65 +819,147 @@
             ffn_widths.astype(LOW).reshape(-1),
         ]
     )
-    small_all = lax.all_gather(small, ROWS, axis=0)
+    count = small.shape[0]
+    small = jnp.pad(small, (0, 24 * 128 - count)).reshape(1, 24, 128)
+    token_pieces = to_batch(tokens)
+    small = gather_over(small, ("zh", "x"), (zh, x))
+    *token_pieces, small, in_weight = tie(*token_pieces, small, in_weight)
+    tokens_own = jnp.concatenate(token_pieces, axis=0)
+    tokens_all = lax.all_gather(tokens_own, GROUP, axis=0, tiled=True)
+    e_in = exchange(jnp.moveaxis(in_weight.reshape(block, 3, 4, heads, head_dim), 2, 0))
+    e_in = e_in.reshape(4 * block, 3 * inner)
+
+    index = jnp.arange(length, dtype=jnp.int32).reshape(2, 2, 2, 2, 2, half)
+
+    def by_place(value):
+        lead = tuple(range(value.ndim - 6))
+        at = value.ndim - 6
+        value = jnp.transpose(value, lead + tuple(at + i for i in (3, 1, 4, 0, 2, 5)))
+        return value.reshape(value.shape[: value.ndim - 6] + (length,))
+
+    e_in, small, cotangent, out_weight, up_weight = tie(
+        e_in, small, cotangent, out_weight, up_weight
+    )
+
+    cut = e_in.shape[0] // 2
+    in_z1 = swap(e_in[:cut], "zh")
+    in_z2 = swap(e_in[cut:], "zh")
+    in_x = swap(e_in, "x")
+    in_zx1 = swap(in_z1, "x")
+    cotangent_own = jnp.concatenate(to_batch(cotangent), axis=0)
+    small = gather_over(small, ("c", "zl"), (c, zl)).reshape(2, 2, 2, 2, -1)
+    small_all = jnp.transpose(small, (3, 0, 2, 1, 4)).reshape(16, 24 * 128)
+    e_out = exchange(out_weight.reshape(4, inner, block))
+    e_out = jnp.moveaxis(e_out, 0, 1).reshape(inner, 4 * block)
+    positions = by_place(index) ^ (zh * (8 * tok_dev) + x * (2 * tok_dev))
+    ends = jnp.cumsum(lax.dynamic_index_in_dim(doc_lengths, batch, 0, keepdims=False))
+    first = jnp.max(jnp.where(ends[:, None] <= positions[None, :], ends[:, None], 0), axis=0)
+    span = jnp.stack([first, positions])
+    key_place = positions[:, None]
+    cosine, sine = rotary_tables(positions)
+    lane = jnp.arange(HEAD_DIM)[None, :]
+    signed = jnp.where(lane < HEAD_DIM // 2, -sine, sine)
     n_vec = 6 + 2 * GROUPS
-    vectors = small_all[:, : n_vec * block].reshape(16, n_vec, block)
-    vectors = jnp.swapaxes(vectors, 0, 1).reshape(n_vec, width)
-    vectors = to_own_order(vectors, zh, x)
-    vectors_f = vectors.astype(WIDE)
-    gain_one, shift_one, gain_two, shift_two, bias_out, bias_down = (
-        vectors_f[i : i + 1] for i in range(6)
-    )
-    router = vectors[6:]
+    rows_of = jnp.arange(16) ^ (zh * 8 + x * 2)
+    pick = (rows_of[:, None] == jnp.arange(16)[None, :]).astype(LOW)
+    small_own = dot_to(pick, small_all, ((1,), (0,)))
+    vectors_f = small_own[:, : n_vec * block].reshape(2, 2, 2, 2, n_vec, block)
+    vectors_f = jnp.transpose(vectors_f, (4, 0, 2, 1, 3, 5)).reshape(n_vec, width)
+    router = vectors_f[6:].astype(LOW)
     at = n_vec * block
     size = in_bias.size
     bias_in = small_all[:, at : at + size].reshape((16,) + in_bias.shape)
     bias_in = jnp.moveaxis(bias_in, 0, 2).reshape(3, 4, heads, head_dim)
     bias_in = lax.dynamic_index_in_dim(bias_in, part, 1, keepdims=False).astype(WIDE)
+    bias_in = bias_in.reshape(1, 3 * inner)
     at += size
     size = up_bias.size
     bias_up = small_all[:, at : at + size].reshape((16,) + up_bias.shape)
     bias_up = jnp.moveaxis(bias_up, 0, 1).reshape(4, units)
     bias_up = lax.dynamic_index_in_dim(bias_up, part, 0, keepdims=True).astype(WIDE)
     at += size
-    widths = small_all[:, at:].reshape(16, 2, micro, tok_dev)
+    widths = small_own[:, at:count].reshape(16, 2, micro, tok_dev)
     widths = lax.dynamic_index_in_dim(widths, batch, 2, keepdims=False).astype(jnp.int32)
-    widths = widths.reshape(2, 2, 2, 2, 2, 2, half)
-    widths = jnp.transpose(widths, (4, 1, 5, 3, 0, 2, 6)).reshape(2, length)
-    heads_row, units_row = widths[0], widths[1]
-
-    index = jnp.arange(length, dtype=jnp.int32).reshape(2, 2, 2, 2, 2, half)
-    positions = jnp.transpose(index, (1, 4, 3, 0, 2, 5)).reshape(length)
-    doc = doc_index(lax.dynamic_index_in_dim(doc_lengths, batch, 0, keepdims=False), positions)
-    cosine, sine = rotary_tables(positions)
-    allowed = (positions[None, :] <= positions[:, None]) & (doc[None, :] == doc[:, None])
-
-    def to_batch(value):
-        mine = lax.dynamic_slice_in_dim(value, y * half, half, 1)
-        got = lax.all_to_all(mine, PARTS, 0, 0, tiled=True)
-        return to_own_order(got.reshape(own, width), zh, x)
-
-    tokens_own = to_batch(tokens)
-    tokens_all = lax.all_gather(tokens_own, GROUP, axis=0, tiled=True)
-    cotangent_own = to_batch(cotangent)
+    widths = jnp.swapaxes(widths, 0, 1).reshape(2, 2, 2, 2, 2, 2, half)
+    heads_row, units_row = by_place(widths)
+    head_ids = (y * 4 + part) * heads + jnp.arange(heads, dtype=jnp.int32)
+    head_active = (head_ids[:, None] // (HEADS // GROUPS) < heads_row[None, :]).astype(WIDE)
+    head_active = head_active[:, :, None]
+    unit_group = (y * 4 + part) * units // (FF // GROUPS)
+    unit_active = (unit_group < units_row).astype(WIDE)[:, None]
+    (
+        tokens_all, in_x, in_z1, in_z2, in_zx1, e_out, cotangent_own, up_weight, down_weight,
+        vectors_f, router, bias_in, bias_up, head_active, unit_active,
+        cosine, sine, signed, span, key_place,
+    ) = tie(
+        tokens_all, in_x, in_z1, in_z2, in_zx1, e_out, cotangent_own, up_weight, down_weight,
+        vectors_f, router, bias_in, bias_up, head_active, unit_active,
+        cosine, sine, signed, span, key_place,
+    )
+    gain_one, shift_one, gain_two, shift_two, bias_out, bias_down = (
+        vectors_f[i : i + 1] for i in range(6)
+    )
+
+    in_zx2 = swap(in_z2, "x")
+    out_z = swap(e_out, "zh")
+    out_x = swap(e_out, "x")
+    e_up = exchange(jnp.moveaxis(up_weight.reshape(block, 4, units), 1, 0))
+    e_up = e_up.reshape(4 * block, units)
     cotangent_all = lax.all_gather(cotangent_own, GROUP, axis=0, tiled=True)
-
-    def exchange(value):
-        return lax.all_to_all(value, ("zl", "c"), 0, 0, tiled=True)
-
-    w_in = in_weight.reshape(block, 3, 4, heads, head_dim)
-    w_in = exchange(jnp.moveaxis(w_in, 2, 0)).reshape(4 * block, 3 * inner)
-    w_in = gather_parts(w_in, 0)
-    w_out = exchange(out_weight.reshape(4, inner, block))
-    w_out = gather_parts(jnp.moveaxis(w_out, 0, 1).reshape(inner, 4 * block), 1)
-    w_up = exchange(jnp.moveaxis(up_weight.reshape(block, 4, units), 1, 0))
-    w_up = gather_parts(w_up.reshape(4 * block, units), 0)
-    w_down = exchange(down_weight.reshape(4, units, block))
-    w_down = gather_parts(jnp.moveaxis(w_down, 0, 1).reshape(units, 4 * block), 1)
-
-    normed, _, _ = norm_forward(tokens_all.astype(WIDE), gain_one, shift_one)
-    normed_low = normed.astype(LOW)
-    logits = dot_to(normed_low, router, ((1,), (1,)))
+    normed_low, logits = norm_rows(bits, tokens_all, gain_one, shift_one, router)
+    normed_low, in_zx2, out_z, out_x, e_up, down_weight, logits = tie(
+        normed_low, in_zx2, out_z, out_x, e_up, down_weight, logits
+    )
+
+    def mine(value):
+        return lax.dynamic_slice_in_dim(value, place * own, own, 0)
+
+    up_cut = e_up.shape[0] // 2
+    out_zx = swap(out_z, "x")
+    up_x1 = swap(e_up[:up_cut], "x")
+    up_z1 = swap(e_up[:up_cut], "zh")
+    e_down = exchange(down_weight.reshape(4, units, block))
+    e_down = jnp.moveaxis(e_down, 0, 1).reshape(units, 4 * block)
+    w_in = (e_in, in_x, in_z1, in_z2, in_zx1, in_zx2)
+    qkv = qkv_rows(normed_low, w_in, bias_in, cosine, signed)
+    mixed, lse = attend(qkv, key_place, span, head_active, heads)
+    w_out = jnp.concatenate([e_out, out_x, out_z, out_zx], axis=1)
+    mixed, w_out, e_up, e_down, up_x1, up_z1, cotangent_own, tokens_own, logits, w_in = tie(
+        mixed, w_out, e_up, e_down, up_x1, up_z1, cotangent_own, tokens_own, logits, w_in
+    )
+
+    part_own = own // 2
+
+    def halves(value):
+        return (
+            lax.dynamic_slice_in_dim(value, c * (length // 2), length // 2, 0),
+            lax.dynamic_slice_in_dim(value, (1 - c) * (length // 2), length // 2, 0),
+        )
+
+    def group_second(total):
+        total = total.reshape(2, 2, own, width)
+        a_keep, a_send = keep_and_send(total[:, :, :part_own], zl, 0)
+        b_keep, b_send = keep_and_send(total[:, :, part_own:], y, 1)
+        a_got = swap(a_send.astype(LOW), "zl")
+        b_got = swap(b_send.astype(LOW), "y")
+        return a_keep, b_keep, a_got, b_got
+
+    def group_third(a_keep, b_keep, a_got, b_got):
+        a_keep, a_send = keep_and_send(a_keep + a_got.astype(WIDE), y, 0)
+        b_keep, b_send = keep_and_send(b_keep + b_got.astype(WIDE), zl, 0)
+        a_got = swap(a_send.astype(LOW), "y")
+        b_got = swap(b_send.astype(LOW), "zl")
+        return jnp.concatenate([a_keep + a_got.astype(WIDE), b_keep + b_got.astype(WIDE)], axis=0)
+
+    attn_here, attn_away = halves(mixed)
+    attn_away = dot_to(attn_away, w_out, ((1,), (0,))).astype(LOW)
+    attn_away, attn_here, tokens_own, cotangent_own, logits = tie(
+        attn_away, attn_here, tokens_own, cotangent_own, logits
+    )
+    attn_got = swap(attn_away, "c")
+    up_x2 = swap(e_up[up_cut:], "x")
+    up_z2 = swap(e_up[up_cut:], "zh")
+    up_zx1 = swap(up_z1, "x")
     options = jnp.arange(GROUPS, dtype=jnp.int32)
     attn_prob = jax.nn.softmax(logits[:, :GROUPS], axis=-1)
     ffn_prob = jax.nn.softmax(logits[:, GROUPS:], axis=-1)
@@ -521,88 +967,151 @@
     ffn_pick = (options[None, :] == units_row[:, None] - 1).astype(WIDE)
     attn_gate = GROUPS * jnp.sum(attn_prob * attn_pick, axis=-1, keepdims=True)
     ffn_gate = GROUPS * jnp.sum(ffn_prob * ffn_pick, axis=-1, keepdims=True)
-
-    def mine(value):
-        return lax.dynamic_slice_in_dim(value, place * own, own, 0)
-
-    rows = tokens_own.astype(WIDE)
-    _, scaled_one, inverse_one = norm_forward(rows, gain_one, shift_one)
-
-    projected = dot_to(normed_low, w_in, ((1,), (0,)))
-    projected = projected.reshape(length, 3, heads, head_dim) + bias_in
-    queries = rotate(projected[:, 0], cosine, sine).astype(LOW)
-    keys = rotate(projected[:, 1], cosine, sine).astype(LOW)
-    values = projected[:, 2].astype(LOW)
-    head_ids = (y * 4 + part) * heads + jnp.arange(heads, dtype=jnp.int32)
-    head_active = (head_ids[None, :] // (HEADS // GROUPS) < heads_row[:, None]).astype(WIDE)
-    unit_ids = (y * 4 + part) * units + jnp.arange(units, dtype=jnp.int32)
-    unit_active = unit_ids[None, :] // (FF // GROUPS) < units_row[:, None]
-    raw = jnp.einsum("qhd,khd->hqk", queries, keys, preferred_element_type=WIDE)
-    scores = jnp.where(allowed[None], raw * scale, -jnp.inf)
-    row_max = jnp.max(scores, axis=-1, keepdims=True)
-    weights = jnp.exp(scores - row_max)
-    row_total = jnp.sum(weights, axis=-1, keepdims=True)
-    probs = weights / row_total
-    probs_low = probs.astype(LOW)
-    attended = jnp.einsum("hqk,khd->qhd", probs_low, values, preferred_element_type=WIDE)
-    mixed = (attended * head_active[:, :, None]).astype(LOW).reshape(length, inner)
-    attn_part = dot_to(mixed, w_out, ((1,), (0,)))
-
-    def group_sum(value):
-        return lax.psum_scatter(
-            value.astype(LOW), GROUP, scatter_dimension=0, tiled=True
-        ).astype(WIDE)
-
-    attn_branch = group_sum(attn_part) + bias_out
+    attn_total = dot_to(attn_here, w_out, ((1,), (0,))) + attn_got.astype(WIDE)
+    attn_total, attn_gate, ffn_gate, tokens_own, cotangent_own = tie(
+        attn_total, attn_gate, ffn_gate, tokens_own, cotangent_own
+    )
+    attn_parts = group_second(attn_total)
+    rows = to_own_order(tokens_own, zh, x).astype(WIDE)
+    upstream = to_own_order(cotangent_own, zh, x).astype(WIDE)
+    *attn_parts, rows, upstream, up_x2 = tie(*attn_parts, rows, upstream, up_x2)
+    attn_sum = group_third(*attn_parts)
+    down_cut = e_down.shape[1] // 2
+    down_x1 = swap(e_down[:, :down_cut], "x")
+    attn_sum, cotangent_all, up_z2, up_zx1, down_x1, e_down = tie(
+        attn_sum, cotangent_all, up_z2, up_zx1, down_x1, e_down
+    )
+
+    attn_branch = attn_sum + bias_out
     attn_gate_own = mine(attn_gate)
     ffn_gate_own = mine(ffn_gate)
     resid = rows + attn_gate_own * attn_branch
     normed_two, scaled_two, inverse_two = norm_forward(resid, gain_two, shift_two)
-    normed_two_low = lax.all_gather(normed_two.astype(LOW), GROUP, axis=0, tiled=True)
-
+    normed_two_low = normed_two.astype(LOW)
+    normed_two_low, e_down, cotangent_all, w_in, up_z2 = tie(
+        normed_two_low, e_down, cotangent_all, w_in, up_z2
+    )
+    normed_two_low = lax.all_gather(normed_two_low, GROUP, axis=0, tiled=True)
+    down_z1 = swap(e_down[:, :down_cut], "zh")
+    up_zx2 = swap(up_z2, "x")
+    down_x2 = swap(e_down[:, down_cut:], "x")
+    down_grad = gate_rows(bits, cotangent_all, ffn_gate)
+    w_in = jnp.concatenate(w_in, axis=0)
+    down_grad, down_z1, up_zx2, down_x2, w_in, e_down = tie(
+        down_grad, down_z1, up_zx2, down_x2, w_in, e_down
+    )
+    down_z2 = swap(e_down[:, down_cut:], "zh")
+    down_zx1 = swap(down_z1, "x")
+    hidden_grad = hidden_grad_rows(down_grad, (e_down, down_x1, down_x2, down_z1))
+    w_up = jnp.concatenate([e_up, up_x1, up_x2, up_z1, up_z2, up_zx1, up_zx2], axis=0)
+    normed_two_low, hidden_grad, w_up, down_z2, down_zx1 = tie(
+        normed_two_low, hidden_grad, w_up, down_z2, down_zx1
+    )
+
+    def columns(value, k):
+        return value[:, k * 4 * block : (k + 1) * 4 * block]
+
+    down_zx2 = swap(down_z2, "x")
     up_pre = dot_to(normed_two_low, w_up, ((1,), (0,))) + bias_up
-    relu_part = jnp.where(unit_active, jnp.maximum(up_pre, 0.0), 0.0)
+    relu_part = jnp.maximum(up_pre, 0.0) * unit_active
+    relu_part, down_zx2, hidden_grad, w_up = tie(relu_part, down_zx2, hidden_grad, w_up)
+    late = jnp.concatenate([down_z2, down_zx1, down_zx2], axis=1)
+    late_at = width - late.shape[1]
+    hidden_grad = hidden_grad + dot_to(down_grad[:, late_at:], late, ((1,), (1,)))
+    up_grad = (hidden_grad * 2.0 * relu_part).astype(LOW)
+    w_down = (e_down, down_x1, down_x2, down_z1, down_z2, down_zx1, down_zx2)
+    two_here, two_away = halves(up_grad)
+    two_away = dot_to(two_away, w_up, ((1,), (1,))).astype(LOW)
+    two_away, two_here, relu_part, down_grad, up_grad = tie(
+        two_away, two_here, relu_part, down_grad, up_grad
+    )
+    two_got = swap(two_away, "c")
     hidden = jnp.square(relu_part).astype(LOW)
-    down_grad = (ffn_gate * cotangent_all.astype(WIDE)).astype(LOW)
-    hidden_grad = dot_to(down_grad, w_down, ((1,), (1,)))
-    up_grad = (hidden_grad * 2.0 * relu_part).astype(LOW)
-    normed_two_grad = group_sum(dot_to(up_grad, w_up, ((1,), (1,))))
-    ffn_branch = group_sum(dot_to(hidden, w_down, ((1,), (0,)))) + bias_down
-    grad_up = dot_to(normed_two_low, up_grad, ((0,), (0,)))
-    grad_down = dot_to(hidden, down_grad, ((0,), (0,)))
-    grad_up_bias = jnp.sum(up_grad.astype(WIDE), axis=0)
-
-    upstream = cotangent_own.astype(WIDE)
+
+    def down_piece(k):
+        return dot_to(hidden, columns(down_grad, k), ((0,), (0,)))
+
+    def up_piece(k):
+        return dot_to(columns(normed_two_low, k), up_grad, ((0,), (0,)))
+
+    down_send3 = down_piece(3).astype(LOW)
+    down_got3 = swap(down_send3, "x")
+    two_total = dot_to(two_here, w_up, ((1,), (1,))) + two_got.astype(WIDE)
+    two_total, hidden, up_grad, down_send3 = tie(two_total, hidden, up_grad, down_send3)
+    two_parts = group_second(two_total)
+    up_send3 = up_piece(3).astype(LOW)
+    down_send1 = down_piece(1).astype(LOW)
+    *two_parts, down_got3, down_send1, up_send3, up_grad = tie(
+        *two_parts, down_got3, down_send1, up_send3, up_grad
+    )
+    normed_two_grad = group_third(*two_parts)
+    up_got3 = swap(up_send3, "x")
+    down_send2 = (down_piece(2) + down_got3.astype(WIDE)).astype(LOW)
+    normed_two_grad, down_send2, hidden, down_grad, up_grad = tie(
+        normed_two_grad, down_send2, hidden, down_grad, up_grad
+    )
+
+    resid_grad = upstream + norm_backward(normed_two_grad, scaled_two, inverse_two, gain_two)
+    gated_attn = attn_gate_own * resid_grad
+    gated_low = gated_attn.astype(LOW)
+    gated_low, hidden, down_grad, up_grad, normed_two_grad, resid_grad, down_send2 = tie(
+        gated_low, hidden, down_grad, up_grad, normed_two_grad, resid_grad, down_send2
+    )
+    attn_out_grad = lax.all_gather(gated_low, GROUP, axis=0, tiled=True)
+    down_far = swap(down_send2, "zh")
+    down_got1 = swap(down_send1, "x")
+    ffn_away, ffn_here = wide_rows(core, hidden, w_down)
+    ffn_got = swap(ffn_away, "c")
+    ffn_total = ffn_here.astype(WIDE) + ffn_got.astype(WIDE)
+    grad_gain_two = jnp.sum(normed_two_grad * scaled_two, axis=0)
+    grad_shift_two = jnp.sum(normed_two_grad, axis=0)
+    attn_gate_grad = jnp.sum(resid_grad * attn_branch, axis=-1)
+    grad_out_bias = jnp.sum(attn_gate_own * resid_grad, axis=0)
+    up_send1 = up_piece(1).astype(LOW)
+    up_send2 = (up_piece(2) + up_got3.astype(WIDE)).astype(LOW)
+    attn_out_grad, ffn_total, up_send1, up_send2, grad_out_bias, grad_gain_two, down_far = tie(
+        attn_out_grad, ffn_total, up_send1, up_send2, grad_out_bias, grad_gain_two, down_far
+    )
+
+    up_rows = up_send2.shape[0] // 2
+    up_far1 = swap(up_send2[:up_rows], "zh")
+    ffn_parts = group_second(ffn_total)
+    proj_grad = attend_back(
+        qkv, attn_out_grad, w_out, head_active, lse, key_place, span, cosine, sine, heads
+    )
+    proj_grad, *ffn_parts, attn_out_grad, down_got1, up_far1, hidden, up_send1, up_send2 = tie(
+        proj_grad, *ffn_parts, attn_out_grad, down_got1, up_far1, hidden, up_send1, up_send2
+    )
+
+    def in_piece(k):
+        return dot_to(columns(normed_low, k), proj_grad, ((0,), (0,)))
+
+    def out_piece(k):
+        return dot_to(mixed, columns(attn_out_grad, k), ((0,), (0,)))
+
+    one_here, one_away = halves(proj_grad)
+    one_away = dot_to(one_away, w_in, ((1,), (1,))).astype(LOW)
+    one_away, one_here, proj_grad, attn_out_grad, *ffn_parts, hidden = tie(
+        one_away, one_here, proj_grad, attn_out_grad, *ffn_parts, hidden
+    )
+    one_got = swap(one_away, "c")
+    up_far2 = swap(up_send2[up_rows:], "zh")
+    in_send3 = in_piece(3).astype(LOW)
+    in_got3 = swap(in_send3, "x")
+    ffn_sum = group_third(*ffn_parts)
+    one_total = dot_to(one_here, w_in, ((1,), (1,))) + one_got.astype(WIDE)
+    one_total, proj_grad, attn_out_grad, ffn_sum, in_send3 = tie(
+        one_total, proj_grad, attn_out_grad, ffn_sum, in_send3
+    )
+    one_parts = group_second(one_total)
+    in_send1 = in_piece(1).astype(LOW)
+    out_send = jnp.stack([out_piece(1), out_piece(3)]).astype(LOW)
+    ffn_branch = ffn_sum + bias_down
     block_out = (resid + ffn_gate_own * ffn_branch).astype(LOW)
     ffn_gate_grad = jnp.sum(upstream * ffn_branch, axis=-1)
     grad_down_bias = jnp.sum(ffn_gate_own * upstream, axis=0)
-    grad_gain_two = jnp.sum(normed_two_grad * scaled_two, axis=0)
-    grad_shift_two = jnp.sum(normed_two_grad, axis=0)
-    resid_grad = upstream + norm_backward(normed_two_grad, scaled_two, inverse_two, gain_two)
-    attn_gate_grad = jnp.sum(resid_grad * attn_branch, axis=-1)
-    gated_attn = attn_gate_own * resid_grad
-    grad_out_bias = jnp.sum(gated_attn, axis=0)
-    attn_out_grad = lax.all_gather(gated_attn.astype(LOW), GROUP, axis=0, tiled=True)
-
-    mixed_grad = dot_to(attn_out_grad, w_out, ((1,), (1,)))
-    attended_grad = (
-        mixed_grad.reshape(length, heads, head_dim) * head_active[:, :, None]
-    ).astype(LOW)
-    grad_out = dot_to(mixed, attn_out_grad, ((0,), (0,)))
-    prob_grad = jnp.einsum("qhd,khd->hqk", attended_grad, values, preferred_element_type=WIDE)
-    row_dot = jnp.sum(probs * prob_grad, axis=-1, keepdims=True)
-    score_grad = (probs * (prob_grad - row_dot) * scale).astype(LOW)
-    query_grad = jnp.einsum("hqk,khd->qhd", score_grad, keys, preferred_element_type=WIDE)
-    key_grad = jnp.einsum("hqk,qhd->khd", score_grad, queries, preferred_element_type=WIDE)
-    value_grad = jnp.einsum("hqk,qhd->khd", probs_low, attended_grad, preferred_element_type=WIDE)
-    query_grad = rotate_back(query_grad, cosine, sine)
-    key_grad = rotate_back(key_grad, cosine, sine)
-    proj_grad = jnp.stack([query_grad, key_grad, value_grad], axis=1).astype(LOW)
-    grad_in_bias = jnp.sum(proj_grad.astype(WIDE), axis=0)
-    proj_flat = proj_grad.reshape(length, 3 * inner)
-    normed_part = group_sum(dot_to(proj_flat, w_in, ((1,), (1,))))
-    grad_in = dot_to(normed_low, proj_flat, ((0,), (0,)))
-
+    grad_up_bias = jnp.sum(up_grad.astype(WIDE), axis=0)
+    grad_in_bias = jnp.sum(proj_grad.astype(WIDE), axis=0).reshape(3, heads, head_dim)
     logit_grad = jnp.concatenate(
         [
             gate_logit_grad(mine(attn_prob), mine(attn_pick), attn_gate_grad),
@@ -613,43 +1122,25 @@
     normed_own = mine(normed_low)
     grad_router = jnp.dot(logit_grad.T, normed_own.astype(WIDE), precision=HIGHEST)
     router_part = jnp.dot(logit_grad, vectors_f[6:], precision=HIGHEST)
-    normed_grad = normed_part + router_part
-    grad_gain_one = jnp.sum(normed_grad * scaled_one, axis=0)
-    grad_shift_one = jnp.sum(normed_grad, axis=0)
-    tokens_grad = resid_grad + norm_backward(normed_grad, scaled_one, inverse_one, gain_one)
-
-    def from_batch(value):
-        value = from_own_order(value, zh, x).astype(LOW).reshape(4, half, width)
-        value = lax.all_to_all(value, PARTS, 0, 0, tiled=True)
-        other = swap(value, "y")
+
+    def both_halves(value, other):
+        def batches(v):
+            v = v.reshape(2, 2, half, width)
+            return flip_where(x, flip_where(zh, v, 0), 1).reshape(4, half, width)
+
+        value, other = batches(value), batches(other)
         return jnp.where(
             y == 0,
             jnp.concatenate([value, other], axis=1),
             jnp.concatenate([other, value], axis=1),
         )
 
-    def share_rows(grad):
-        total = scatter_parts(jnp.swapaxes(grad.reshape(2, 2, 4 * block, -1), 0, 1))
-        total = exchange(total.astype(LOW).reshape(4, block, -1))
-        return total
-
-    def share_columns(grad):
-        grad = grad.reshape(grad.shape[0], 2, 2, 4 * block)
-        total = scatter_parts(jnp.transpose(grad, (2, 1, 0, 3)))
-        total = total.astype(LOW).reshape(-1, 4, block)
-        return exchange(jnp.swapaxes(total, 0, 1))
-
-    grad_up = jnp.swapaxes(share_rows(grad_up), 0, 1).reshape(block, tp_units)
-    grad_down = share_columns(grad_down).reshape(tp_units, block)
-    grad_out = share_columns(grad_out).reshape(tp_heads, head_dim, block)
-    grad_in = share_rows(grad_in).reshape(4, block, 3, heads, head_dim)
-    grad_in = jnp.transpose(grad_in, (1, 2, 0, 3, 4)).reshape(block, 3, tp_heads, head_dim)
-
-    sums = jnp.stack(
-        [grad_gain_one, grad_shift_one, grad_out_bias, grad_gain_two, grad_shift_two, grad_down_bias]
-    )
-    sums = from_own_order(jnp.concatenate([sums, grad_router], axis=0), zh, x)
-    sums = jnp.swapaxes(sums.reshape(n_vec, 16, block), 0, 1).reshape(16, n_vec * block)
+    def spread(rows, cut):
+        rows = from_own_order(rows, zh, x)
+        return jnp.swapaxes(rows.reshape(cut, 16, block), 0, 1).reshape(16, cut * block)
+
+    sums = jnp.stack([grad_out_bias, grad_gain_two, grad_shift_two, grad_down_bias])
+    sums = spread(jnp.concatenate([sums, grad_router], axis=0), n_vec - 2)
     chosen = (jnp.arange(4) == part).astype(WIDE)
     spread_in = (grad_in_bias[:, None] * chosen[None, :, None, None]).reshape(
         3, tp_heads, 16, head_dim // 16
@@ -657,29 +1148,76 @@
     spread_in = jnp.moveaxis(spread_in, 2, 0).reshape(16, -1)
     spread_up = (grad_up_bias[None, :] * chosen[:, None]).reshape(up_bias.shape[0], 16, block)
     spread_up = jnp.moveaxis(spread_up, 1, 0).reshape(16, -1)
-    total = lax.psum_scatter(
-        jnp.concatenate([sums, spread_in, spread_up], axis=1),
-        ROWS,
-        scatter_dimension=0,
-        tiled=True,
-    )[0]
-    shared = lax.psum(total[: n_vec * block], "y").reshape(n_vec, block)
+    early = jnp.concatenate([sums, spread_in, spread_up], axis=1)
+    _, scaled_one, inverse_one = norm_forward(rows, gain_one, shift_one)
+    block_low = from_own_order(block_out, zh, x).reshape(4, half, width)
+    (
+        *one_parts, in_send1, out_send, block_low, early, router_part, scaled_one, inverse_one,
+        in_got3,
+    ) = tie(
+        *one_parts, in_send1, out_send, block_low, early, router_part, scaled_one, inverse_one,
+        in_got3,
+    )
+    normed_sum = group_third(*one_parts)
+    in_got1 = swap(in_send1, "x")
+    up_got1 = swap(up_send1, "x")
+    in_send2 = (in_piece(2) + in_got3.astype(WIDE)).astype(LOW)
+    down_home = (down_piece(0) + down_got1.astype(WIDE) + down_far.astype(WIDE)).astype(LOW)
+    normed_sum, in_send2, block_low, early, out_send, up_grad, up_far2, in_got1, down_home = tie(
+        normed_sum, in_send2, block_low, early, out_send, up_grad, up_far2, in_got1, down_home
+    )
+
+    in_far = swap(in_send2, "zh")
+    down_home = exchange(jnp.moveaxis(down_home.reshape(units, 4, block), 1, 0))
+    normed_grad = normed_sum + router_part
+    tokens_grad = resid_grad + norm_backward(normed_grad, scaled_one, inverse_one, gain_one)
+    tokens_low = from_own_order(tokens_grad.astype(LOW), zh, x).reshape(4, half, width)
+    tokens_low, normed_grad, block_low, out_send, up_grad, early = tie(
+        tokens_low, normed_grad, block_low, out_send, up_grad, early
+    )
+    tokens_pieces = across([tokens_low[k] for k in range(4)])
+    grad_gain_one = jnp.sum(normed_grad * scaled_one, axis=0)
+    grad_shift_one = jnp.sum(normed_grad, axis=0)
+    last = spread(jnp.stack([grad_gain_one, grad_shift_one]), 2)
+    up_far = jnp.concatenate([up_far1, up_far2], axis=0)
+    up_home = (up_piece(0) + up_got1.astype(WIDE) + up_far.astype(WIDE)).astype(LOW)
+    out_got = swap(out_send, "x")
+    *tokens_pieces, last, early, block_low, out_got, in_far, up_home, down_home = tie(
+        *tokens_pieces, last, early, block_low, out_got, in_far, up_home, down_home
+    )
+    tokens_grad = jnp.stack(tokens_pieces)
+    tokens_other = swap(tokens_grad, "y")
+    in_home = (in_piece(0) + in_got1.astype(WIDE) + in_far.astype(WIDE)).astype(LOW)
+    out_far = swap((out_piece(2) + out_got[1].astype(WIDE)).astype(LOW), "zh")
+    block_out = jnp.stack(across([block_low[k] for k in range(4)]))
+    total = reduce_rows(jnp.concatenate([last, early], axis=1), zh, zl, x, c)
+    up_home = exchange(up_home.reshape(4, block, units))
+    tokens_other, block_out, out_far, in_home, up_home, total = tie(
+        tokens_other, block_out, out_far, in_home, up_home, total
+    )
+    block_other = swap(block_out, "y")
+    in_home = exchange(in_home.reshape(4, block, 3 * inner)).reshape(4, block, 3, heads, head_dim)
+    out_home = (out_piece(0) + out_got[0].astype(WIDE) + out_far.astype(WIDE)).astype(LOW)
+    out_home = exchange(jnp.moveaxis(out_home.reshape(inner, 4, block), 1, 0))
     at = n_vec * block
+    shared = total[:at]
+    shared = (shared + swap(shared, "y")).reshape(n_vec, block)
+    early = total[at:]
     return (
-        from_batch(block_out),
-        from_batch(tokens_grad).astype(WIDE),
+        both_halves(block_out, block_other),
+        both_halves(tokens_grad, tokens_other).astype(WIDE),
         shared[0],
         shared[1],
         shared[6:],
-        grad_in.astype(WIDE),
-        total[at : at + in_bias.size].reshape(in_bias.shape),
-        grad_out.astype(WIDE),
+        jnp.transpose(in_home, (1, 2, 0, 3, 4)).reshape(in_weight.shape).astype(WIDE),
+        early[: in_bias.size].reshape(in_bias.shape),
+        out_home.reshape(out_weight.shape).astype(WIDE),
         shared[2],
         shared[3],
         shared[4],
-        grad_up.astype(WIDE),
-        total[at + in_bias.size :].reshape(up_bias.shape),
-        grad_down.astype(WIDE),
+        jnp.swapaxes(up_home, 0, 1).reshape(up_weight.shape).astype(WIDE),
+        early[in_bias.size :].reshape(up_bias.shape),
+        down_home.reshape(down_weight.shape).astype(WIDE),
         shared[5],
     )
 

time: 1090 us -> 713 us (0.65)
  waiting for transfers between devices: 593 us -> 240 us
  matrix products: 147 us -> 74.6 us
  Pallas kernels: 0 us -> 70.1 us
  starting transfers between devices: 81 us -> 126 us
  blocking collectives: 44.6 us -> 0 us
  local copies, waits for them, and re-layouts: 122 us -> 110 us
    unnamed x12 -> x4, waiting for transfers between devices: 159 us -> 0.07 us
    reduce_scatter x4 -> x0, waiting for transfers between devices: 117 us -> none  [group_sum(): lax.psum_scatter(value.astype(LOW), GROUP, scatter_dimension=0, tiled=True)]
    pallas_call x0 -> x7, Pallas kernels: none -> 70.1 us  [the longest x1 21.1 us: attend_back(): pl.pallas_call(attend_back_kernel, grid=(heads, length // BLOCK_Q), in_sp...]
    ppermute x26 -> x71, starting transfers between devices: 30.1 us -> 81.3 us  [swap(): return lax.ppermute(value, axis, [(0, 1), (1, 0)])]
    dot_general x5 -> x0, matrix products: 46.4 us -> none  [the longest x1 15.6 us: grouped(): jnp.einsum('hqk,khd->qhd', score_grad, keys, preferred_element_type=WIDE)]
    ppermute x26 -> x71, waiting for transfers between devices: 232 us -> 187 us  [swap(): return lax.ppermute(value, axis, [(0, 1), (1, 0)])]
    all_to_all x2 -> x0, blocking collectives: 39.6 us -> none  [the longest x1 20.2 us: exchange(): return lax.all_to_all(value, ('zl', 'c'), 0, 0, tiled=True)]
    all_to_all x7 -> x8, waiting for transfers between devices: 54 us -> 31.8 us  [exchange(): return lax.all_to_all(value, ('zl', 'c'), 0, 0, tiled=True)]
  transfers between devices with their start and end apart: 46 -> 87, of which waited for: 26 -> 38; matrix products, arithmetic and copies ran while one was open for 27% -> 29% of each run, Pallas kernels for 0% -> 10%
where the time goes in v2:
time: 713 us; the launch traced here: 701 us
  waiting for transfers between devices  240 us (34%)
  starting transfers between devices  126 us (18%)
  local copies, waits for them, and re-layouts  110 us (15%)
  matrix products  74.6 us (10%)
  Pallas kernels  70.1 us (10%)
  other arithmetic  64.4 us (9%)
  between operations  16.1 us (2%)
    ppermute x71, waiting for transfers between devices, swap(): return lax.ppermute(value, axis, [(0, 1), (1, 0)])  187 us
    ppermute x71, starting transfers between devices, swap(): return lax.ppermute(value, axis, [(0, 1), (1, 0)])  81.3 us
    dot_general x25, matrix products, dot_to(): lax.dot_general(left, right, (dims, ((), ())), preferred_element_type=WIDE)  72.3 us
    all_to_all x8, waiting for transfers between devices, exchange(): return lax.all_to_all(value, ('zl', 'c'), 0, 0, tiled=True)  31.8 us
    all_to_all x8, starting transfers between devices, exchange(): return lax.all_to_all(value, ('zl', 'c'), 0, 0, tiled=True)  28.8 us
    unnamed x205, local copies, waits for them, and re-layouts  25.2 us
    ppermute x4, waiting for transfers between devices, across(): lax.ppermute(pieces[3], PARTS, [(i, i ^ 3) for i in range(4)])  21.2 us
    pallas_call x1, Pallas kernels, attend_back(): pl.pallas_call(attend_back_kernel, grid=(heads, length // BLOCK_Q), in_sp...  21.1 us
  transfers between devices with their start and end apart: 87, of which 38 were waited for; matrix products, arithmetic and copies ran while one was open for 29% of the time, Pallas kernels for 10%

profile of v2, /device:TPU:0, one launch (start us, length us, event | category | flops | bytes accessed | tf_op | source)
XLA Modules:
  0.0 701.4 jit_solution(991923785051969862)
XLA Ops:
  9.6 5.4 concatenate.99
  15.1 4.1 collective-permute-start.3
  28.7 5.4 collective-permute-done.2
  46.1 15.6 %all-to-all-done = bf16[4,128,3,2,128]{4,3,2,1,0:T(2,128)(2,1)S(1)} async-done(((bf16[4,128,3,2,128]{4,3,2,1,0:T(2,128)(2,1)}), bf16[4,128,3,2,128]{4,3,2,1,0:T(2,128)(2,1)S(1)}, u32[]{:S(2)}, u32[]{:S(2)}) %all-to-all-start) | async-done | bytes 786464 | tf_op jit(solution)/shard_map/all_to_all | solution.py:783
  70.6 4.4 collective-permute-start.10
  81.4 10.2 %collective-permute-done.11 = bf16[32,2048]{1,0:T(8,128)(2,1)S(1)} collective-permute-done((bf16[32,2048]{1,0:T(8,128)(2,1)S(1)}, bf16[32,2048]{1,0:T(8,128)(2,1)S(1)}, u32[]{:S(2)}, u32[]{:S(2)}) %collective-permute-start.11) | collective-permute-done | bytes 131104 | tf_op jit(solution)/shard_map/ppermute | solution.py:796
  92.3 19.6 %collective-permute-done.6.refs_2_ = bf16[256,768]{1,0:T(8,128)(2,1)S(1)} collective-permute-done((bf16[256,768]{1,0:T(8,128)(2,1)}, bf16[256,768]{1,0:T(8,128)(2,1)S(1)}, u32[]{:S(2)}, u32[]{:S(2)}) %collective-permute-start.6) | collective-permute-done | bytes 393248 | tf_op jit(solution)/shard_map/ppermute | solution.py:366
  114.0 6.2 collective-permute-done.7.refs_3_
  125.5 3.5 all-to-all-start.2
  132.4 7.8 %norm_rows.1 = (bf16[1024,2048]{1,0:T(8,128)(2,1)}, f32[1024,8]{1,0:T(8,128)}) custom-call(s32[2]{0:T(128)} %pad_add_fusion.1.bits_ref, bf16[1024,2048]{1,0:T(8,128)(2,1)} %all-gather.5.cloned.1.call-done.x_ref, f32[1,2048]{1,0:T(1,128)} %get-tuple-element.506.gain_ref, f32[1,2048]{1,0:T(1,128)} %get-tuple-element.505.shift_ref, bf16[8,2048]{1,0:T(8,128)(2,1)} %bitcast.372), custom_call_target="tpu_custom_call" | custom-call | tf_op jit(solution)/shard_map/norm_rows/pallas_call | solution.py:451
  140.2 8.9 %all-to-all-done.2 = bf16[4,128,1024]{1,2,0:T(8,128)(2,1)S(1)} async-done(((bf16[4,128,1024]{1,2,0:T(8,128)(2,1)}), bf16[4,128,1024]{1,2,0:T(8,128)(2,1)S(1)}, u32[]{:S(2)}, u32[]{:S(2)}) %all-to-all-start.2) | async-done | bytes 1048608 | tf_op jit(solution)/shard_map/all_to_all | solution.py:783
  150.4 3.5 all-to-all-start.3
  158.1 7.8 %qkv_rows.1.q_ref.k_ref.v_ref = bf16[1024,768]{1,0:T(8,128)(2,1)} custom-call(bf16[1024,2048]{1,0:T(8,128)(2,1)} %get-tuple-element.245.h_ref, bf16[512,768]{1,0:T(8,128)(2,1)} %copy-done.10, bf16[512,768]{1,0:T(8,128)(2,1)} %copy-done.37, bf16[256,768]{1,0:T(8,128)(2,1)} %copy-done.47, bf16[256,768]{1,0:T(8,128)(2,1)} %copy-done.49, ...), custom_call_target="tpu_custom_call" | custom-call | tf_op jit(solution)/shard_map/qkv_rows/pallas_call | solution.py:619
  165.9 11.1 %attend.1 = (bf16[1024,256]{1,0:T(8,128)(2,1)}, f32[2,1,1024]{2,1,0:T(1,128)}) custom-call(bf16[1024,768]{1,0:T(8,128)(2,1)} %qkv_rows.1.q_ref.k_ref.v_ref, bf16[1024,768]{1,0:T(8,128)(2,1)} %qkv_rows.1.q_ref.k_ref.v_ref, bf16[1024,768]{1,0:T(8,128)(2,1)} %qkv_rows.1.q_ref.k_ref.v_ref, s32[1024,1]{1,0:T(8,128)} %copy.229.key_ref, ...), custom_call_target="tpu_custom_call" | custom-call | tf_op jit(solution)/shard_map/attend/pallas_call | solution.py:697
  178.4 4.2 collective-permute-done.19
  184.8 10.3 %all-gather.9.cloned.1.call-start = ((), (), s32[]{:S(2)}) async-start(), calls=%async_computation.10 | async-start | bytes 4718592 | tf_op jit(solution)/shard_map/all_gather | solution.py:994
  203.4 4.4 convert_add_fusion.3
  230.2 3.8 collective-permute-done.21
  241.3 4.1 collective-permute-done.24
  265.0 6.0 gate_rows.1.dz_ref
  274.3 7.3 %collective-permute-done.31.refs_2_ = bf16[1024,256]{1,0:T(8,128)(2,1)} collective-permute-done((bf16[1024,256]{1,0:T(8,128)(2,1)}, bf16[1024,256]{1,0:T(8,128)(2,1)}, u32[]{:S(2)}, u32[]{:S(2)}) %collective-permute-start.31) | collective-permute-done | bytes 524320 | tf_op jit(solution)/shard_map/ppermute | solution.py:366
  281.7 4.3 collective-permute-done.29.refs_3_
  298.5 7.3 %hidden_grad_rows.1 = f32[1024,1024]{1,0:T(8,128)} custom-call(bf16[1024,2048]{1,0:T(8,128)(2,1)} %gate_rows.1.dz_ref, bf16[1024,512]{1,0:T(8,128)(2,1)} %copy-done.2, bf16[1024,256]{1,0:T(8,128)(2,1)} %collective-permute-done.28.refs_1_, bf16[1024,256]{1,0:T(8,128)(2,1)} %collective-permute-done.31.refs_2_, bf16[1024,256]{1,0:T(8,128)(2,1)} %collective-permute-done.29.refs_3_), custom_call_target="tpu_custom_call" | custom-call | tf_op jit(solution)/shard_map/hidden_grad_rows/pallas_call | solution.py:560
  311.4 8.1 %maximum_multiply_fusion = f32[1024,1024]{1,0:T(8,128)S(1)} fusion(f32[1024]{0:T(1024)S(1)} %bitcast.396, f32[1024]{0:T(1024)S(1)} %bitcast.398, bf16[1024,2048]{1,0:T(8,128)(2,1)} %all-gather.9.cloned.1.call-done, bf16[2048,1024]{1,0:T(8,128)(2,1)} %constant_dynamic-update-slice_fusion.10), kind=kOutput, calls=%fused_computation.6 | convolution fusion | flops 4298113024 | bytes 12591104 | tf_op jit(solution)/shard_map/dot_general | solution.py:396
  327.3 4.6 convolution_convert_fusion
  336.1 4.6 convert_add_fusion.2
  341.6 3.5 convolution_convert_fusion.4
  349.0 10.5 %collective-permute-done.38 = bf16[1024,512]{1,0:T(8,128)(2,1)S(1)} collective-permute-done((bf16[1024,512]{1,0:T(8,128)(2,1)S(1)}, bf16[1024,512]{1,0:T(8,128)(2,1)S(1)}, u32[]{:S(2)}, u32[]{:S(2)}) %collective-permute-start.38) | collective-permute-done | bytes 1048608 | tf_op jit(solution)/shard_map/ppermute | solution.py:366
  361.3 6.3 collective-permute-done.39
  373.3 8.9 %wide_rows.1 = (bf16[512,2048]{1,0:T(8,128)(2,1)}, bf16[512,2048]{1,0:T(8,128)(2,1)}) custom-call(s32[1]{0:T(128)} %bitcast.63.bit_ref, bf16[1024,1024]{1,0:T(8,128)(2,1)} %copy-done.23, bf16[1024,512]{1,0:T(8,128)(2,1)} %copy-done.2, bf16[1024,256]{1,0:T(8,128)(2,1)} %collective-permute-done.28.refs_1_, bf16[1024,256]{1,0:T(8,128)(2,1)} %collective-permute-done.31.refs_2_, ...), custom_call_target="tpu_custom_call" | custom-call | tf_op jit(solution)/shard_map/wide_rows/pallas_call | solution.py:589
  389.7 19.6 %collective-permute-done.42 = bf16[512,1024]{1,0:T(8,128)(2,1)S(1)} collective-permute-done((bf16[512,1024]{1,0:T(8,128)(2,1)}, bf16[512,1024]{1,0:T(8,128)(2,1)S(1)}, u32[]{:S(2)}, u32[]{:S(2)}) %collective-permute-start.42) | collective-permute-done | bytes 1048608 | tf_op jit(solution)/shard_map/ppermute | solution.py:366
  415.6 18.6 %collective-permute-done.43 = bf16[1024,512]{1,0:T(8,128)(2,1)} collective-permute-done((bf16[1024,512]{1,0:T(8,128)(2,1)}, bf16[1024,512]{1,0:T(8,128)(2,1)}, u32[]{:S(2)}, u32[]{:S(2)}) %collective-permute-start.43) | collective-permute-done | bytes 1048608 | tf_op jit(solution)/shard_map/ppermute | solution.py:366
  442.4 21.1 %attend_back.1 = bf16[1024,768]{1,0:T(8,128)(2,1)} custom-call(bf16[1024,768]{1,0:T(8,128)(2,1)} %qkv_rows.1.q_ref.k_ref.v_ref, bf16[1024,768]{1,0:T(8,128)(2,1)} %qkv_rows.1.q_ref.k_ref.v_ref, bf16[1024,768]{1,0:T(8,128)(2,1)} %qkv_rows.1.q_ref.k_ref.v_ref, bf16[1024,2048]{1,0:T(8,128)(2,1)} %all-gather.11.cloned.1.call-done.da_ref, ...), custom_call_target="tpu_custom_call" | custom-call | tf_op jit(solution)/shard_map/attend_back/pallas_call | solution.py:724
  470.2 3.8 convolution_convert_fusion.2
  487.6 9.1 %collective-permute-done.50 = bf16[64,2048]{1,0:T(8,128)(2,1)S(1)} collective-permute-done((bf16[64,2048]{1,0:T(8,128)(2,1)S(1)}, bf16[64,2048]{1,0:T(8,128)(2,1)S(1)}, u32[]{:S(2)}, u32[]{:S(2)}) %collective-permute-start.50) | collective-permute-done | bytes 262176 | tf_op jit(solution)/shard_map/ppermute | solution.py:366
  496.9 3.9 convert_add_fusion
  528.0 4.8 collective-permute-done.51
  542.6 9.0 %collective-permute-done.57 = bf16[512,768]{1,0:T(8,128)(2,1)S(1)} collective-permute-done((bf16[512,768]{1,0:T(8,128)(2,1)S(1)}, bf16[512,768]{1,0:T(8,128)(2,1)S(1)}, u32[]{:S(2)}, u32[]{:S(2)}) %collective-permute-start.57) | collective-permute-done | bytes 786464 | tf_op jit(solution)/shard_map/ppermute | solution.py:366
  564.1 4.3 all-to-all-start.4
  569.5 4.2 collective-permute-start.60
  578.7 4.2 add_convert_fusion
  586.5 5.5 collective-permute-done.61
  592.1 27.5 %collective-permute-done.62 = bf16[512,768]{1,0:T(8,128)(2,1)} collective-permute-done((bf16[512,768]{1,0:T(8,128)(2,1)}, bf16[512,768]{1,0:T(8,128)(2,1)}, u32[]{:S(2)}, u32[]{:S(2)}) %collective-permute-start.62) | collective-permute-done | bytes 786464 | tf_op jit(solution)/shard_map/ppermute | solution.py:366
  619.6 3.5 all-to-all-start.5
  637.3 5.3 collective-permute-start.70
  651.0 5.0 collective-permute-done.67
  677.0 3.6 all-to-all-start.6
  684.9 7.3 %all-to-all-done.6 = bf16[4,128,768]{2,1,0:T(8,128)(2,1)S(1)} async-done(((bf16[4,128,768]{2,1,0:T(8,128)(2,1)}), bf16[4,128,768]{2,1,0:T(8,128)(2,1)S(1)}, u32[]{:S(2)}, u32[]{:S(2)}) %all-to-all-start.6) | async-done | bytes 786464 | tf_op jit(solution)/shard_map/all_to_all | solution.py:783
  (636 shorter events, 313.4 us)
Async XLA Ops:
  7.2 115.6 %all-gather.5.cloned.1.call-start = ((), (), s32[]{:S(2)}) async-start(), calls=%async_computation.8 | async-start | bytes 4718592 | tf_op jit(solution)/shard_map/all_gather | solution.py:828
  38.1 23.5 %all-to-all-start = ((bf16[4,128,3,2,128]{4,3,2,1,0:T(2,128)(2,1)}), bf16[4,128,3,2,128]{4,3,2,1,0:T(2,128)(2,1)S(1)}, u32[]{:S(2)}, u32[]{:S(2)}) async-start(bf16[4,128,3,2,128]{4,3,2,1,0:T(2,128)(2,1)} %bitcast.328), calls=%async_computation | async-start | bytes 1572864 | tf_op jit(solution)/shard_map/all_to_all | solution.py:783
  63.2 59.7 %collective-permute-start.5 = (bf16[512,768]{1,0:T(8,128)(2,1)S(1)}, bf16[512,768]{1,0:T(8,128)(2,1)S(1)}, u32[]{:S(2)}, u32[]{:S(2)}) collective-permute-start(bf16[512,768]{1,0:T(8,128)(2,1)S(1)} %reshape.887.refs_0_), channel_id=1, source_target_pairs={{0,4},{4,0},{1,5},{5,1},{2,6},{6,2},{3,7},{7,3},{8,12},{12,8},{9,1... | collective-permute-start | bytes 2359304 | tf_op jit(solution)/shard_map/ppermute | solution.py:366
  63.2 50.8 %all-to-all-start.1 = ((bf16[4,256,128]{2,1,0:T(8,128)(2,1)}), bf16[4,256,128]{2,1,0:T(8,128)(2,1)S(1)}, u32[]{:S(2)}, u32[]{:S(2)}) async-start(bf16[4,256,128]{2,1,0:T(8,128)(2,1)} %bitcast.11), calls=%async_computation.1 | async-start | bytes 524288 | tf_op jit(solution)/shard_map/all_to_all | solution.py:783
  70.6 21.0 %collective-permute-start.11 = (bf16[32,2048]{1,0:T(8,128)(2,1)S(1)}, bf16[32,2048]{1,0:T(8,128)(2,1)S(1)}, u32[]{:S(2)}, u32[]{:S(2)}) collective-permute-start(bf16[32,2048]{1,0:T(8,128)(2,1)S(1)} %get-tuple-element.475), channel_id=1, source_target_pairs={{0,20},{4,16},{16,4},{20,0},{1,21},{5,17},{17,5},{21,1},{2,22},{6,... | collective-permute-start | bytes 393224 | tf_op jit(solution)/shard_map/ppermute | solution.py:796
  70.6 41.2 %collective-permute-start.10 = (bf16[32,2048]{1,0:T(8,128)(2,1)}, bf16[32,2048]{1,0:T(8,128)(2,1)}, u32[]{:S(2)}, u32[]{:S(2)}) collective-permute-start(bf16[32,2048]{1,0:T(8,128)(2,1)} %get-tuple-element.476), channel_id=1, source_target_pairs={{0,16},{16,0},{1,17},{17,1},{2,18},{18,2},{3,19},{19,3},{4,20},{20... | collective-permute-start | bytes 393224 | tf_op jit(solution)/shard_map/ppermute | solution.py:366
  75.0 36.9 %collective-permute-start.9 = (bf16[32,2048]{1,0:T(8,128)(2,1)}, bf16[32,2048]{1,0:T(8,128)(2,1)}, u32[]{:S(2)}, u32[]{:S(2)}) collective-permute-start(bf16[32,2048]{1,0:T(8,128)(2,1)} %get-tuple-element.477), channel_id=1, source_target_pairs={{0,4},{4,0},{1,5},{5,1},{2,6},{6,2},{3,7},{7,3},{8,12},{12,8},{9,1... | collective-permute-start | bytes 393224 | tf_op jit(solution)/shard_map/ppermute | solution.py:366
  75.0 36.8 %collective-permute-start.6 = (bf16[256,768]{1,0:T(8,128)(2,1)}, bf16[256,768]{1,0:T(8,128)(2,1)S(1)}, u32[]{:S(2)}, u32[]{:S(2)}) collective-permute-start(bf16[256,768]{1,0:T(8,128)(2,1)} %get-tuple-element.483), channel_id=1, source_target_pairs={{0,16},{16,0},{1,17},{17,1},{2,18},{18,2},{3,19},{19,3},{4,20},{20... | collective-permute-start | bytes 1179656 | tf_op jit(solution)/shard_map/ppermute | solution.py:366
  91.6 28.6 %collective-permute-start.7 = (bf16[256,768]{1,0:T(8,128)(2,1)}, bf16[256,768]{1,0:T(8,128)(2,1)S(1)}, u32[]{:S(2)}, u32[]{:S(2)}) collective-permute-start(bf16[256,768]{1,0:T(8,128)(2,1)} %get-tuple-element.482), channel_id=1, source_target_pairs={{0,16},{16,0},{1,17},{17,1},{2,18},{18,2},{3,19},{19,3},{4,20},{20... | collective-permute-start | bytes 1179656 | tf_op jit(solution)/shard_map/ppermute | solution.py:366
  125.5 23.6 %all-to-all-start.2 = ((bf16[4,128,1024]{1,2,0:T(8,128)(2,1)}), bf16[4,128,1024]{1,2,0:T(8,128)(2,1)S(1)}, u32[]{:S(2)}, u32[]{:S(2)}) async-start(bf16[4,128,1024]{1,2,0:T(8,128)(2,1)} %bitcast.31), calls=%async_computation.2 | async-start | bytes 2097152 | tf_op jit(solution)/shard_map/all_to_all | solution.py:783
  129.6 20.0 %collective-permute-start.16 = (bf16[256,512]{1,0:T(8,128)(2,1)S(1)}, bf16[256,512]{1,0:T(8,128)(2,1)S(1)}, u32[]{:S(2)}, u32[]{:S(2)}) collective-permute-start(bf16[256,512]{1,0:T(8,128)(2,1)S(1)} %copy_bitcast_fusion.4), channel_id=1, source_target_pairs={{0,4},{4,0},{1,5},{5,1},{2,6},{6,2},{3,7},{7,3},{8,12},{12,8},{9,1... | collective-permute-start | bytes 786440 | tf_op jit(solution)/shard_map/ppermute | solution.py:366
  129.9 19.7 %collective-permute-start.15 = (bf16[256,512]{1,0:T(8,128)(2,1)S(1)}, bf16[256,512]{1,0:T(8,128)(2,1)}, u32[]{:S(2)}, u32[]{:S(2)}) collective-permute-start(bf16[256,512]{1,0:T(8,128)(2,1)S(1)} %copy_bitcast_fusion.4), channel_id=1, source_target_pairs={{0,16},{16,0},{1,17},{17,1},{2,18},{18,2},{3,19},{19,3},{4,20},{20... | collective-permute-start | bytes 786440 | tf_op jit(solution)/shard_map/ppermute | solution.py:366
  129.9 19.7 %collective-permute-start.14 = (bf16[256,768]{1,0:T(8,128)(2,1)S(1)}, bf16[256,768]{1,0:T(8,128)(2,1)S(1)}, u32[]{:S(2)}, u32[]{:S(2)}) collective-permute-start(bf16[256,768]{1,0:T(8,128)(2,1)S(1)} %collective-permute-done.7.refs_3_), channel_id=1, source_target_pairs={{0,4},{4,0},{1,5},{5,1},{2,6},{6,2},{3,7},{7,3},{8,12},{12,8},{9,1... | collective-permute-start | bytes 1179656 | tf_op jit(solution)/shard_map/ppermute | solution.py:366
  150.4 27.8 %all-to-all-start.3 = ((bf16[4,1024,128]{2,1,0:T(8,128)(2,1)}), bf16[4,1024,128]{2,1,0:T(8,128)(2,1)S(1)}, u32[]{:S(2)}, u32[]{:S(2)}) async-start(bf16[4,1024,128]{2,1,0:T(8,128)(2,1)} %bitcast.353), calls=%async_computation.3 | async-start | bytes 2097152 | tf_op jit(solution)/shard_map/all_to_all | solution.py:783
  153.9 95.6 %all-gather.7.cloned.1.call-start = ((), (), s32[]{:S(2)}) async-start(), calls=%async_computation.9 | async-start | bytes 4718592 | tf_op jit(solution)/shard_map/all_gather | solution.py:908
  154.0 23.0 %collective-permute-start.17 = (bf16[256,512]{1,0:T(8,128)(2,1)}, bf16[256,512]{1,0:T(8,128)(2,1)}, u32[]{:S(2)}, u32[]{:S(2)}) collective-permute-start(bf16[256,512]{1,0:T(8,128)(2,1)} %collective-permute-done.15), channel_id=1, source_target_pairs={{0,4},{4,0},{1,5},{5,1},{2,6},{6,2},{3,7},{7,3},{8,12},{12,8},{9,1... | collective-permute-start | bytes 786440 | tf_op jit(solution)/shard_map/ppermute | solution.py:366
  156.2 26.4 %collective-permute-start.19 = (bf16[256,1024]{1,0:T(8,128)(2,1)}, bf16[256,1024]{1,0:T(8,128)(2,1)}, u32[]{:S(2)}, u32[]{:S(2)}) collective-permute-start(bf16[256,1024]{1,0:T(8,128)(2,1)} %slice.250), channel_id=1, source_target_pairs={{0,16},{16,0},{1,17},{17,1},{2,18},{18,2},{3,19},{19,3},{4,20},{20... | collective-permute-start | bytes 1572872 | tf_op jit(solution)/shard_map/ppermute | solution.py:366
  156.3 26.3 %collective-permute-start.18 = (bf16[256,1024]{1,0:T(8,128)(2,1)}, bf16[256,1024]{1,0:T(8,128)(2,1)}, u32[]{:S(2)}, u32[]{:S(2)}) collective-permute-start(bf16[256,1024]{1,0:T(8,128)(2,1)} %slice.250), channel_id=1, source_target_pairs={{0,4},{4,0},{1,5},{5,1},{2,6},{6,2},{3,7},{7,3},{8,12},{12,8},{9,1... | collective-permute-start | bytes 1572872 | tf_op jit(solution)/shard_map/ppermute | solution.py:366
  184.7 18.7 %collective-permute-start.20 = (bf16[512,2048]{1,0:T(8,128)(2,1)}, bf16[512,2048]{1,0:T(8,128)(2,1)}, u32[]{:S(2)}, u32[]{:S(2)}) collective-permute-start(bf16[512,2048]{1,0:T(8,128)(2,1)} %convolution_convert_fusion.1), channel_id=1, source_target_pairs={{0,2},{2,0},{1,3},{3,1},{4,6},{6,4},{5,7},{7,5},{8,10},{10,8},{9,1... | collective-permute-start | bytes 6291464 | tf_op jit(solution)/shard_map/ppermute | solution.py:366
  184.8 125.0 %all-gather.9.cloned.1.call-start = ((), (), s32[]{:S(2)}) async-start(), calls=%async_computation.10 | async-start | bytes 4718592 | tf_op jit(solution)/shard_map/all_gather | solution.py:994
  197.0 52.4 %collective-permute-start.26 = (bf16[256,1024]{1,0:T(8,128)(2,1)}, bf16[256,1024]{1,0:T(8,128)(2,1)}, u32[]{:S(2)}, u32[]{:S(2)}) collective-permute-start(bf16[256,1024]{1,0:T(8,128)(2,1)} %slice.255), channel_id=1, source_target_pairs={{0,16},{16,0},{1,17},{17,1},{2,18},{18,2},{3,19},{19,3},{4,20},{20... | collective-permute-start | bytes 1572872 | tf_op jit(solution)/shard_map/ppermute | solution.py:366
  197.1 31.4 %collective-permute-start.23 = (bf16[256,1024]{1,0:T(8,128)(2,1)}, bf16[256,1024]{1,0:T(8,128)(2,1)}, u32[]{:S(2)}, u32[]{:S(2)}) collective-permute-start(bf16[256,1024]{1,0:T(8,128)(2,1)} %slice.255), channel_id=1, source_target_pairs={{0,4},{4,0},{1,5},{5,1},{2,6},{6,2},{3,7},{7,3},{8,12},{12,8},{9,1... | collective-permute-start | bytes 1572872 | tf_op jit(solution)/shard_map/ppermute | solution.py:366
  199.6 49.8 %collective-permute-start.28 = (bf16[1024,256]{1,0:T(8,128)(2,1)}, bf16[1024,256]{1,0:T(8,128)(2,1)}, u32[]{:S(2)}, u32[]{:S(2)}) collective-permute-start(bf16[1024,256]{1,0:T(8,128)(2,1)} %slice.256), channel_id=1, source_target_pairs={{0,4},{4,0},{1,5},{5,1},{2,6},{6,2},{3,7},{7,3},{8,12},{12,8},{9,1... | collective-permute-start | bytes 1572872 | tf_op jit(solution)/shard_map/ppermute | solution.py:366
  212.9 21.1 %collective-permute-start.21 = (bf16[2,64,2048]{2,1,0:T(8,128)(2,1)}, bf16[2,64,2048]{2,1,0:T(8,128)(2,1)}, u32[]{:S(2)}, u32[]{:S(2)}) collective-permute-start(bf16[2,64,2048]{2,1,0:T(8,128)(2,1)} %fusion.42), channel_id=1, source_target_pairs={{0,8},{8,0},{1,9},{9,1},{2,10},{10,2},{3,11},{11,3},{4,12},{12,4},... | collective-permute-start | bytes 1572872 | tf_op jit(solution)/shard_map/ppermute | solution.py:366
  228.4 21.0 %collective-permute-start.27 = (bf16[256,1024]{1,0:T(8,128)(2,1)}, bf16[256,1024]{1,0:T(8,128)(2,1)}, u32[]{:S(2)}, u32[]{:S(2)}) collective-permute-start(bf16[256,1024]{1,0:T(8,128)(2,1)} %collective-permute-done.19), channel_id=1, source_target_pairs={{0,4},{4,0},{1,5},{5,1},{2,6},{6,2},{3,7},{7,3},{8,12},{12,8},{9,1... | collective-permute-start | bytes 1572872 | tf_op jit(solution)/shard_map/ppermute | solution.py:366
  253.4 180.8 %all-gather.11.cloned.1.call-start = ((), (), s32[]{:S(2)}) async-start(), calls=%async_computation.11 | async-start | bytes 4718592 | tf_op jit(solution)/shard_map/all_gather | solution.py:1060
  260.1 21.6 %collective-permute-start.31 = (bf16[1024,256]{1,0:T(8,128)(2,1)}, bf16[1024,256]{1,0:T(8,128)(2,1)}, u32[]{:S(2)}, u32[]{:S(2)}) collective-permute-start(bf16[1024,256]{1,0:T(8,128)(2,1)} %get-tuple-element.472), channel_id=1, source_target_pairs={{0,4},{4,0},{1,5},{5,1},{2,6},{6,2},{3,7},{7,3},{8,12},{12,8},{9,1... | collective-permute-start | bytes 1572872 | tf_op jit(solution)/shard_map/ppermute | solution.py:366
  260.6 25.3 %collective-permute-start.29 = (bf16[1024,256]{1,0:T(8,128)(2,1)}, bf16[1024,256]{1,0:T(8,128)(2,1)}, u32[]{:S(2)}, u32[]{:S(2)}) collective-permute-start(bf16[1024,256]{1,0:T(8,128)(2,1)} %get-tuple-element.473), channel_id=1, source_target_pairs={{0,16},{16,0},{1,17},{17,1},{2,18},{18,2},{3,19},{19,3},{4,20},{20... | collective-permute-start | bytes 1572872 | tf_op jit(solution)/shard_map/ppermute | solution.py:366
  286.0 23.8 %collective-permute-start.32 = (bf16[1024,256]{1,0:T(8,128)(2,1)S(1)}, bf16[1024,256]{1,0:T(8,128)(2,1)S(1)}, u32[]{:S(2)}, u32[]{:S(2)}) collective-permute-start(bf16[1024,256]{1,0:T(8,128)(2,1)S(1)} %slice.262), channel_id=1, source_target_pairs={{0,16},{16,0},{1,17},{17,1},{2,18},{18,2},{3,19},{19,3},{4,20},{20... | collective-permute-start | bytes 1572872 | tf_op jit(solution)/shard_map/ppermute | solution.py:366
  289.4 20.3 %collective-permute-start.33 = (bf16[1024,256]{1,0:T(8,128)(2,1)}, bf16[1024,256]{1,0:T(8,128)(2,1)S(1)}, u32[]{:S(2)}, u32[]{:S(2)}) collective-permute-start(bf16[1024,256]{1,0:T(8,128)(2,1)} %collective-permute-done.29.refs_3_), channel_id=1, source_target_pairs={{0,4},{4,0},{1,5},{5,1},{2,6},{6,2},{3,7},{7,3},{8,12},{12,8},{9,1... | collective-permute-start | bytes 1572872 | tf_op jit(solution)/shard_map/ppermute | solution.py:366
  333.9 25.6 %collective-permute-start.38 = (bf16[1024,512]{1,0:T(8,128)(2,1)S(1)}, bf16[1024,512]{1,0:T(8,128)(2,1)S(1)}, u32[]{:S(2)}, u32[]{:S(2)}) collective-permute-start(bf16[1024,512]{1,0:T(8,128)(2,1)S(1)} %convolution_convert_fusion.6), channel_id=1, source_target_pairs={{0,4},{4,0},{1,5},{5,1},{2,6},{6,2},{3,7},{7,3},{8,12},{12,8},{9,1... | collective-permute-start | bytes 3145736 | tf_op jit(solution)/shard_map/ppermute | solution.py:366
  382.3 30.5 %collective-permute-start.41 = (bf16[512,2048]{1,0:T(8,128)(2,1)}, bf16[512,2048]{1,0:T(8,128)(2,1)S(1)}, u32[]{:S(2)}, u32[]{:S(2)}) collective-permute-start(bf16[512,2048]{1,0:T(8,128)(2,1)} %get-tuple-element.350), channel_id=1, source_target_pairs={{0,2},{2,0},{1,3},{3,1},{4,6},{6,4},{5,7},{7,5},{8,10},{10,8},{9,1... | collective-permute-start | bytes 6291464 | tf_op jit(solution)/shard_map/ppermute | solution.py:366
  383.1 26.2 %collective-permute-start.42 = (bf16[512,1024]{1,0:T(8,128)(2,1)}, bf16[512,1024]{1,0:T(8,128)(2,1)S(1)}, u32[]{:S(2)}, u32[]{:S(2)}) collective-permute-start(bf16[512,1024]{1,0:T(8,128)(2,1)} %convolution_convert_fusion.4), channel_id=1, source_target_pairs={{0,4},{4,0},{1,5},{5,1},{2,6},{6,2},{3,7},{7,3},{8,12},{12,8},{9,1... | collective-permute-start | bytes 3145736 | tf_op jit(solution)/shard_map/ppermute | solution.py:366
  384.6 80.9 %collective-permute-start.46 = (bf16[1024,512]{1,0:T(8,128)(2,1)}, bf16[1024,512]{1,0:T(8,128)(2,1)}, u32[]{:S(2)}, u32[]{:S(2)}) collective-permute-start(bf16[1024,512]{1,0:T(8,128)(2,1)} %convolution_convert_fusion.5), channel_id=1, source_target_pairs={{0,4},{4,0},{1,5},{5,1},{2,6},{6,2},{3,7},{7,3},{8,12},{12,8},{9,1... | collective-permute-start | bytes 3145736 | tf_op jit(solution)/shard_map/ppermute | solution.py:366
  385.6 48.6 %collective-permute-start.43 = (bf16[1024,512]{1,0:T(8,128)(2,1)}, bf16[1024,512]{1,0:T(8,128)(2,1)}, u32[]{:S(2)}, u32[]{:S(2)}) collective-permute-start(bf16[1024,512]{1,0:T(8,128)(2,1)} %add_convert_fusion.3), channel_id=1, source_target_pairs={{0,16},{16,0},{1,17},{17,1},{2,18},{18,2},{3,19},{19,3},{4,20},{20... | collective-permute-start | bytes 3145736 | tf_op jit(solution)/shard_map/ppermute | solution.py:366
  439.9 25.6 %collective-permute-start.47 = (bf16[256,1024]{1,0:T(8,128)(2,1)}, bf16[256,1024]{1,0:T(8,128)(2,1)}, u32[]{:S(2)}, u32[]{:S(2)}) collective-permute-start(bf16[256,1024]{1,0:T(8,128)(2,1)} %slice.274), channel_id=1, source_target_pairs={{0,16},{16,0},{1,17},{17,1},{2,18},{18,2},{3,19},{19,3},{4,20},{20... | collective-permute-start | bytes 1572872 | tf_op jit(solution)/shard_map/ppermute | solution.py:366
  439.9 25.6 %collective-permute-start.44 = (bf16[2,64,2048]{2,1,0:T(8,128)(2,1)}, bf16[2,64,2048]{2,1,0:T(8,128)(2,1)}, u32[]{:S(2)}, u32[]{:S(2)}) collective-permute-start(bf16[2,64,2048]{2,1,0:T(8,128)(2,1)} %fusion.44), channel_id=1, source_target_pairs={{0,8},{8,0},{1,9},{9,1},{2,10},{10,2},{3,11},{11,3},{4,12},{12,4},... | collective-permute-start | bytes 1572872 | tf_op jit(solution)/shard_map/ppermute | solution.py:366
  440.6 24.9 %collective-permute-start.45 = (bf16[2,64,2048]{2,1,0:T(8,128)(2,1)}, bf16[2,64,2048]{2,1,0:T(8,128)(2,1)}, u32[]{:S(2)}, u32[]{:S(2)}) collective-permute-start(bf16[2,64,2048]{2,1,0:T(8,128)(2,1)} %fusion.48), channel_id=1, source_target_pairs={{0,1},{1,0},{2,3},{3,2},{4,5},{5,4},{6,7},{7,6},{8,9},{9,8},{10,11... | collective-permute-start | bytes 1572872 | tf_op jit(solution)/shard_map/ppermute | solution.py:366
  466.5 76.1 %collective-permute-start.56 = (bf16[256,1024]{1,0:T(8,128)(2,1)}, bf16[256,1024]{1,0:T(8,128)(2,1)}, u32[]{:S(2)}, u32[]{:S(2)}) collective-permute-start(bf16[256,1024]{1,0:T(8,128)(2,1)} %slice.284), channel_id=1, source_target_pairs={{0,16},{16,0},{1,17},{17,1},{2,18},{18,2},{3,19},{19,3},{4,20},{20... | collective-permute-start | bytes 1572872 | tf_op jit(solution)/shard_map/ppermute | solution.py:366
  468.7 107.1 %collective-permute-start.63 = (bf16[512,1024]{1,0:T(8,128)(2,1)}, bf16[512,1024]{1,0:T(8,128)(2,1)}, u32[]{:S(2)}, u32[]{:S(2)}) collective-permute-start(bf16[512,1024]{1,0:T(8,128)(2,1)} %convolution_convert_fusion.3), channel_id=1, source_target_pairs={{0,4},{4,0},{1,5},{5,1},{2,6},{6,2},{3,7},{7,3},{8,12},{12,8},{9,1... | collective-permute-start | bytes 3145736 | tf_op jit(solution)/shard_map/ppermute | solution.py:366
  476.0 52.1 %collective-permute-start.53 = (bf16[512,768]{1,0:T(8,128)(2,1)}, bf16[512,768]{1,0:T(8,128)(2,1)}, u32[]{:S(2)}, u32[]{:S(2)}) collective-permute-start(bf16[512,768]{1,0:T(8,128)(2,1)} %convolution_convert_fusion.8), channel_id=1, source_target_pairs={{0,4},{4,0},{1,5},{5,1},{2,6},{6,2},{3,7},{7,3},{8,12},{12,8},{9,1... | collective-permute-start | bytes 2359304 | tf_op jit(solution)/shard_map/ppermute | solution.py:366
  478.5 18.4 %collective-permute-start.48 = (bf16[512,2048]{1,0:T(8,128)(2,1)S(1)}, bf16[512,2048]{1,0:T(8,128)(2,1)S(1)}, u32[]{:S(2)}, u32[]{:S(2)}) collective-permute-start(bf16[512,2048]{1,0:T(8,128)(2,1)S(1)} %convolution_convert_fusion.2), channel_id=1, source_target_pairs={{0,2},{2,0},{1,3},{3,1},{4,6},{6,4},{5,7},{7,5},{8,10},{10,8},{9,1... | collective-permute-start | bytes 6291464 | tf_op jit(solution)/shard_map/ppermute | solution.py:366
  532.8 18.8 %collective-permute-start.57 = (bf16[512,768]{1,0:T(8,128)(2,1)S(1)}, bf16[512,768]{1,0:T(8,128)(2,1)S(1)}, u32[]{:S(2)}, u32[]{:S(2)}) collective-permute-start(bf16[512,768]{1,0:T(8,128)(2,1)S(1)} %copy-done.91), channel_id=1, source_target_pairs={{0,4},{4,0},{1,5},{5,1},{2,6},{6,2},{3,7},{7,3},{8,12},{12,8},{9,1... | collective-permute-start | bytes 2359304 | tf_op jit(solution)/shard_map/ppermute | solution.py:366
  564.1 55.5 %all-to-all-start.4 = ((bf16[4,1024,128]{2,1,0:T(8,128)(2,1)}), bf16[4,1024,128]{2,1,0:T(8,128)(2,1)}, u32[]{:S(2)}, u32[]{:S(2)}) async-start(bf16[4,1024,128]{2,1,0:T(8,128)(2,1)} %bitcast_bitcast_fusion), calls=%async_computation.4 | async-start | bytes 2097152 | tf_op jit(solution)/shard_map/all_to_all | solution.py:783
  575.7 43.9 %collective-permute-start.62 = (bf16[512,768]{1,0:T(8,128)(2,1)}, bf16[512,768]{1,0:T(8,128)(2,1)}, u32[]{:S(2)}, u32[]{:S(2)}) collective-permute-start(bf16[512,768]{1,0:T(8,128)(2,1)} %add_convert_fusion.5), channel_id=1, source_target_pairs={{0,16},{16,0},{1,17},{17,1},{2,18},{18,2},{3,19},{19,3},{4,20},{20... | collective-permute-start | bytes 2359304 | tf_op jit(solution)/shard_map/ppermute | solution.py:366
  619.6 40.1 %all-to-all-start.5 = ((bf16[4,128,1024]{2,1,0:T(8,128)(2,1)}), bf16[4,128,1024]{2,1,0:T(8,128)(2,1)S(1)}, u32[]{:S(2)}, u32[]{:S(2)}) async-start(bf16[4,128,1024]{2,1,0:T(8,128)(2,1)} %bitcast.125), calls=%async_computation.5 | async-start | bytes 2097152 | tf_op jit(solution)/shard_map/all_to_all | solution.py:783
  627.6 31.3 %collective-permute-start.68 = (bf16[256,512]{1,0:T(8,128)(2,1)S(1)}, bf16[256,512]{1,0:T(8,128)(2,1)S(1)}, u32[]{:S(2)}, u32[]{:S(2)}) collective-permute-start(bf16[256,512]{1,0:T(8,128)(2,1)S(1)} %fusion.8), channel_id=1, source_target_pairs={{0,16},{16,0},{1,17},{17,1},{2,18},{18,2},{3,19},{19,3},{4,20},{20... | collective-permute-start | bytes 786440 | tf_op jit(solution)/shard_map/ppermute | solution.py:366
  629.1 30.6 %collective-permute-start.64 = (bf16[4,32,2048]{2,1,0:T(8,128)(2,1)S(1)}, bf16[4,32,2048]{2,1,0:T(8,128)(2,1)S(1)}, u32[]{:S(2)}, u32[]{:S(2)}) collective-permute-start(bf16[4,32,2048]{2,1,0:T(8,128)(2,1)S(1)} %pad_maximum_fusion.8), channel_id=1, source_target_pairs={{0,1},{1,0},{2,3},{3,2},{4,5},{5,4},{6,7},{7,6},{8,9},{9,8},{10,11... | collective-permute-start | bytes 1572872 | tf_op jit(solution)/shard_map/ppermute | solution.py:366
  (132 other events, 1315.5 us)
Sparse Core Ops, SparseCore 0:
  36.8 35.1 all-gather.4
  184.9 42.4 all-gather.6
  253.6 41.8 all-gather.8
  371.5 35.4 all-gather.10

commit v3 on v2

--- a/solution.py
+++ b/solution.py
@@ -508,95 +508,215 @@
     return total
 
 
-def by_half(step, away_ref, here_ref, write):
-    half = pl.num_programs(0) // 2
-
-    @pl.when(step < half)
-    def _():
-        write(away_ref)
-
-    @pl.when(step >= half)
-    def _():
-        write(here_ref)
-
-
-def half_specs(steps, rows, width, dtype):
-    half = steps // 2
-    shape = jax.ShapeDtypeStruct((rows * half, width), dtype)
-    return (
-        [
-            pl.BlockSpec((rows, width), lambda i, bit: (jnp.minimum(i, half - 1), 0)),
-            pl.BlockSpec((rows, width), lambda i, bit: (jnp.maximum(i - half, 0), 0)),
-        ],
-        [shape, shape],
-    )
-
-
 def row_spec(steps, rows, width):
     half = steps // 2
-    return pl.BlockSpec(
-        (rows, width), lambda i, bit: (jnp.where(i < half, i + (1 - bit[0]) * half, i - half + bit[0] * half), 0)
-    )
+    return pl.BlockSpec((rows, width), lambda i, bit: ((i + (1 - bit[0]) * half) % steps, 0))
 
 
 def fixed(value):
     return pl.BlockSpec(value.shape, lambda *_: (0, 0))
 
 
-def grad_kernel(dz_ref, *refs):
-    pieces, out_ref = refs[:-1], refs[-1]
-    total, at = None, 0
-    for piece in pieces:
-        n = piece.shape[1]
-        part = dot_to(dz_ref[:, at : at + n], piece[...], ((1,), (1,)))
-        total = part if total is None else total + part
-        at += n
-    out_ref[...] = total
-
-
-def hidden_grad_rows(down_grad, downs):
+def hidden_kernel(cuts, h_ref, active_ref, bias_ref, *refs):
+    pieces, (relu_ref, hidden_ref) = refs[:-2], refs[-2:]
+    at, used = 0, 0
+    for n in cuts:
+        group = pieces[used : used + n]
+        used += n
+        width = group[0].shape[1]
+        total = add_dots(h_ref, group, bias_ref[:, at : at + width])
+        relu = jnp.maximum(total, 0.0) * active_ref[...]
+        relu_ref[:, at : at + width] = relu
+        hidden_ref[:, at : at + width] = (relu * relu).astype(LOW)
+        at += width
+
+
+def hidden_rows(normed, active, bias, groups):
+    length, width = normed.shape
+    units = bias.shape[1]
+    rows = BLOCK_Q
+    pieces = [p for group in groups for p in group]
+    return pl.pallas_call(
+        functools.partial(hidden_kernel, tuple(len(g) for g in groups)),
+        grid=(length // rows,),
+        in_specs=[
+            pl.BlockSpec((rows, width), lambda i: (i, 0)),
+            pl.BlockSpec((rows, 1), lambda i: (i, 0)),
+            fixed(bias),
+        ]
+        + [fixed(p) for p in pieces],
+        out_specs=[pl.BlockSpec((rows, units), lambda i: (i, 0))] * 2,
+        out_shape=[
+            jax.ShapeDtypeStruct((length, units), WIDE),
+            jax.ShapeDtypeStruct((length, units), LOW),
+        ],
+        name="hidden_rows",
+    )(normed, active, bias, *pieces)
+
+
+def ffn_kernel(cuts_down, cuts_up, bit_ref, dz_ref, relu_ref, *refs):
+    du_ref, dh_ref = refs[-2:]
+    n_down = sum(cuts_down)
+    downs, ups = refs[:n_down], refs[n_down:-2]
+    at, used = 0, 0
+    parts = []
+    for n in cuts_down:
+        group = downs[used : used + n]
+        used += n
+        grad, col = None, 0
+        for piece in group:
+            k = piece.shape[1]
+            part = dot_to(dz_ref[:, col : col + k], piece[...], ((1,), (1,)))
+            grad = part if grad is None else grad + part
+            col += k
+        m = grad.shape[1]
+        du = (grad * 2.0 * relu_ref[:, at : at + m]).astype(LOW)
+        du_ref[:, at : at + m] = du
+        parts.append((at, m, du))
+        at += m
+    for j in range(cuts_up[0]):
+        total, used = None, 0
+        for g, n in enumerate(cuts_up):
+            piece = ups[used + j]
+            used += n
+            part = dot_to(parts[g][2], piece[...], ((1,), (1,)))
+            total = part if total is None else total + part
+        k = total.shape[1]
+        dh_ref[:, j * k : (j + 1) * k] = total.astype(LOW)
+
+
+def ffn_rows(bit, down_grad, relu, down_groups, up_groups):
     length, width = down_grad.shape
-    units = downs[0].shape[0]
-    return pl.pallas_call(
-        grad_kernel,
-        grid=(length // BLOCK_Q,),
-        in_specs=[pl.BlockSpec((BLOCK_Q, width), lambda i: (i, 0))] + [fixed(p) for p in downs],
-        out_specs=pl.BlockSpec((BLOCK_Q, units), lambda i: (i, 0)),
-        out_shape=jax.ShapeDtypeStruct((length, units), WIDE),
-        name="hidden_grad_rows",
-    )(down_grad, *downs)
-
-
-def wide_kernel(bit_ref, left_ref, *refs):
-    pieces, (away_ref, here_ref) = refs[:-2], refs[-2:]
-
-    def write(out_ref):
-        at = 0
-        for piece in pieces:
-            n = piece.shape[1]
-            out_ref[:, at : at + n] = dot_to(left_ref[...], piece[...], ((1,), (0,))).astype(LOW)
-            at += n
-
-    by_half(pl.program_id(0), away_ref, here_ref, write)
-
-
-def wide_rows(bit, left, pieces):
-    length, depth = left.shape
+    units = relu.shape[1]
     rows = BLOCK_Q
     steps = length // rows
-    width = sum(p.shape[1] for p in pieces)
-    out_specs, out_shape = half_specs(steps, rows, width, LOW)
+    downs = [p for group in down_groups for p in group]
+    ups = [p for group in up_groups for p in group]
     return pl.pallas_call(
-        wide_kernel,
+        functools.partial(
+            ffn_kernel, tuple(len(g) for g in down_groups), tuple(len(g) for g in up_groups)
+        ),
         grid_spec=pltpu.PrefetchScalarGridSpec(
             num_scalar_prefetch=1,
             grid=(steps,),
-            in_specs=[row_spec(steps, rows, depth)] + [fixed(p) for p in pieces],
-            out_specs=out_specs,
+            in_specs=[row_spec(steps, rows, width), row_spec(steps, rows, units)]
+            + [fixed(p) for p in downs]
+            + [fixed(p) for p in ups],
+            out_specs=[
+                row_spec(steps, rows, units),
+                pl.BlockSpec((rows, width), lambda i, bit: (i, 0)),
+            ],
         ),
-        out_shape=out_shape,
+        out_shape=[
+            jax.ShapeDtypeStruct((length, units), LOW),
+            jax.ShapeDtypeStruct((length, width), LOW),
+        ],
+        name="ffn_rows",
+    )(bit, down_grad, relu, *downs, *ups)
+
+
+def wide_kernel(cuts, left_ref, *refs):
+    pieces, out_ref = refs[:-1], refs[-1]
+    for j in range(cuts[0]):
+        total, used, at = None, 0, 0
+        for n in cuts:
+            piece = pieces[used + j]
+            used += n
+            k = piece.shape[0]
+            part = dot_to(left_ref[:, at : at + k], piece[...], ((1,), (0,)))
+            total = part if total is None else total + part
+            at += k
+        m = total.shape[1]
+        out_ref[:, j * m : (j + 1) * m] = total.astype(LOW)
+
+
+def wide_rows(left, groups):
+    length, depth = left.shape
+    rows = BLOCK_Q
+    pieces = [p for group in groups for p in group]
+    width = sum(p.shape[1] for p in groups[0])
+    return pl.pallas_call(
+        functools.partial(wide_kernel, tuple(len(g) for g in groups)),
+        grid=(length // rows,),
+        in_specs=[pl.BlockSpec((rows, depth), lambda i: (i, 0))] + [fixed(p) for p in pieces],
+        out_specs=pl.BlockSpec((rows, width), lambda i: (i, 0)),
+        out_shape=jax.ShapeDtypeStruct((length, width), LOW),
         name="wide_rows",
-    )(bit, left, *pieces)
+    )(left, *pieces)
+
+
+def own_kernel(bits_ref, a_ref, b_ref, a_out, b_out):
+    width = a_ref.shape[1]
+    for mine, theirs in chunks(bits_ref, width):
+        at = slice(mine, mine + width // 8)
+        a_out[:, at] = a_ref[:, pl.ds(theirs, width // 8)].astype(WIDE)
+        b_out[:, at] = b_ref[:, pl.ds(theirs, width // 8)].astype(WIDE)
+
+
+def own_rows(bits, a, b):
+    shape = jax.ShapeDtypeStruct(a.shape, WIDE)
+    whole = pl.BlockSpec(a.shape, lambda i, bits: (0, 0))
+    return pl.pallas_call(
+        own_kernel,
+        grid_spec=pltpu.PrefetchScalarGridSpec(
+            num_scalar_prefetch=1, grid=(1,), in_specs=[whole, whole], out_specs=[whole, whole]
+        ),
+        out_shape=[shape, shape],
+        name="own_rows",
+    )(bits, a, b)
+
+
+def home_kernel(bits_ref, a_ref, out_ref):
+    width = a_ref.shape[1]
+    for mine, theirs in chunks(bits_ref, width):
+        part = a_ref[:, mine : mine + width // 8]
+        out_ref[:, pl.ds(theirs, width // 8)] = part.astype(LOW)
+
+
+def home_rows(bits, a):
+    whole = pl.BlockSpec(a.shape, lambda i, bits: (0, 0))
+    return pl.pallas_call(
+        home_kernel,
+        grid_spec=pltpu.PrefetchScalarGridSpec(
+            num_scalar_prefetch=1, grid=(1,), in_specs=[whole], out_specs=whole
+        ),
+        out_shape=jax.ShapeDtypeStruct(a.shape, LOW),
+        name="home_rows",
+    )(bits, a)
+
+
+def first_kernel(
+    bits_ref, sum_ref, router_ref, rows_ref, resid_ref, gain_ref, out_ref, sums_ref
+):
+    grad = sum_ref[...] + router_ref[...]
+    rows = rows_ref[...]
+    gain = gain_ref[...]
+    _, scaled, inverse = norm_forward(rows, gain, 0.0)
+    sums_ref[0:1, :] = jnp.sum(grad * scaled, axis=0, keepdims=True)
+    sums_ref[1:2, :] = jnp.sum(grad, axis=0, keepdims=True)
+    out = (resid_ref[...] + norm_backward(grad, scaled, inverse, gain)).astype(LOW)
+    width = out.shape[1]
+    for mine, theirs in chunks(bits_ref, width):
+        out_ref[:, pl.ds(theirs, width // 8)] = out[:, mine : mine + width // 8]
+
+
+def first_back(bits, normed_sum, router_part, rows, resid_grad, gain):
+    whole = pl.BlockSpec(rows.shape, lambda i, bits: (0, 0))
+    width = rows.shape[1]
+    return pl.pallas_call(
+        first_kernel,
+        grid_spec=pltpu.PrefetchScalarGridSpec(
+            num_scalar_prefetch=1,
+            grid=(1,),
+            in_specs=[whole] * 4 + [pl.BlockSpec((1, width), lambda i, bits: (0, 0))],
+            out_specs=[whole, pl.BlockSpec((2, width), lambda i, bits: (0, 0))],
+        ),
+        out_shape=[
+            jax.ShapeDtypeStruct(rows.shape, LOW),
+            jax.ShapeDtypeStruct((2, width), WIDE),
+        ],
+        name="first_back",
+    )(bits, normed_sum, router_part, rows, resid_grad, gain)
 
 
 def qkv_kernel(h_ref, *refs):
@@ -804,30 +924,39 @@
 
     bits = jnp.stack([zh, x]).astype(jnp.int32)
     core = c.reshape(1).astype(jnp.int32)
+    e_in = exchange(jnp.moveaxis(in_weight.reshape(block, 3, 4, heads, head_dim), 2, 0))
+    e_in = e_in.reshape(4 * block, 3 * inner)
+    token_pieces = to_batch(tokens)
+
+    def rows_of_block(value):
+        value = value.astype(WIDE).reshape(-1)
+        return jnp.pad(value, (0, -value.shape[0] % block)).reshape(-1, block)
+
     small = jnp.concatenate(
         [
-            first_gain,
-            first_shift,
-            second_gain,
-            second_shift,
-            out_bias,
-            down_bias,
-            router_weight.reshape(-1),
-            in_bias.reshape(-1),
-            up_bias.reshape(-1),
-            head_groups.astype(LOW).reshape(-1),
-            ffn_widths.astype(LOW).reshape(-1),
-        ]
-    )
-    count = small.shape[0]
-    small = jnp.pad(small, (0, 24 * 128 - count)).reshape(1, 24, 128)
-    token_pieces = to_batch(tokens)
+            rows_of_block(v)
+            for v in (
+                first_gain,
+                first_shift,
+                second_gain,
+                second_shift,
+                out_bias,
+                down_bias,
+                router_weight,
+                up_bias,
+                head_groups,
+                ffn_widths,
+                in_bias,
+            )
+        ],
+        axis=0,
+    )
+    n_small = small.shape[0]
+    small = small[None]
     small = gather_over(small, ("zh", "x"), (zh, x))
-    *token_pieces, small, in_weight = tie(*token_pieces, small, in_weight)
+    *token_pieces, small, e_in = tie(*token_pieces, small, e_in)
     tokens_own = jnp.concatenate(token_pieces, axis=0)
     tokens_all = lax.all_gather(tokens_own, GROUP, axis=0, tiled=True)
-    e_in = exchange(jnp.moveaxis(in_weight.reshape(block, 3, 4, heads, head_dim), 2, 0))
-    e_in = e_in.reshape(4 * block, 3 * inner)
 
     index = jnp.arange(length, dtype=jnp.int32).reshape(2, 2, 2, 2, 2, half)
 
@@ -837,18 +966,13 @@
         value = jnp.transpose(value, lead + tuple(at + i for i in (3, 1, 4, 0, 2, 5)))
         return value.reshape(value.shape[: value.ndim - 6] + (length,))
 
-    e_in, small, cotangent, out_weight, up_weight = tie(
-        e_in, small, cotangent, out_weight, up_weight
-    )
-
     cut = e_in.shape[0] // 2
     in_z1 = swap(e_in[:cut], "zh")
     in_z2 = swap(e_in[cut:], "zh")
     in_x = swap(e_in, "x")
     in_zx1 = swap(in_z1, "x")
-    cotangent_own = jnp.concatenate(to_batch(cotangent), axis=0)
     small = gather_over(small, ("c", "zl"), (c, zl)).reshape(2, 2, 2, 2, -1)
-    small_all = jnp.transpose(small, (3, 0, 2, 1, 4)).reshape(16, 24 * 128)
+    small_all = jnp.transpose(small, (3, 0, 2, 1, 4)).reshape(16, n_small * block)
     e_out = exchange(out_weight.reshape(4, inner, block))
     e_out = jnp.moveaxis(e_out, 0, 1).reshape(inner, 4 * block)
     positions = by_place(index) ^ (zh * (8 * tok_dev) + x * (2 * tok_dev))
@@ -861,26 +985,26 @@
     signed = jnp.where(lane < HEAD_DIM // 2, -sine, sine)
     n_vec = 6 + 2 * GROUPS
     rows_of = jnp.arange(16) ^ (zh * 8 + x * 2)
-    pick = (rows_of[:, None] == jnp.arange(16)[None, :]).astype(LOW)
-    small_own = dot_to(pick, small_all, ((1,), (0,)))
+    pick = (rows_of[:, None] == jnp.arange(16)[None, :]).astype(WIDE)
+    small_own = jnp.dot(pick, small_all, precision=HIGHEST)
     vectors_f = small_own[:, : n_vec * block].reshape(2, 2, 2, 2, n_vec, block)
     vectors_f = jnp.transpose(vectors_f, (4, 0, 2, 1, 3, 5)).reshape(n_vec, width)
     router = vectors_f[6:].astype(LOW)
     at = n_vec * block
-    size = in_bias.size
-    bias_in = small_all[:, at : at + size].reshape((16,) + in_bias.shape)
-    bias_in = jnp.moveaxis(bias_in, 0, 2).reshape(3, 4, heads, head_dim)
-    bias_in = lax.dynamic_index_in_dim(bias_in, part, 1, keepdims=False).astype(WIDE)
-    bias_in = bias_in.reshape(1, 3 * inner)
-    at += size
     size = up_bias.size
     bias_up = small_all[:, at : at + size].reshape((16,) + up_bias.shape)
     bias_up = jnp.moveaxis(bias_up, 0, 1).reshape(4, units)
-    bias_up = lax.dynamic_index_in_dim(bias_up, part, 0, keepdims=True).astype(WIDE)
+    bias_up = lax.dynamic_index_in_dim(bias_up, part, 0, keepdims=True)
     at += size
-    widths = small_own[:, at:count].reshape(16, 2, micro, tok_dev)
+    size = 2 * micro * tok_dev
+    widths = small_own[:, at : at + size].reshape(16, 2, micro, tok_dev)
     widths = lax.dynamic_index_in_dim(widths, batch, 2, keepdims=False).astype(jnp.int32)
     widths = jnp.swapaxes(widths, 0, 1).reshape(2, 2, 2, 2, 2, 2, half)
+    at += size
+    bias_in = small_all[:, at : at + in_bias.size].reshape((16,) + in_bias.shape)
+    bias_in = jnp.moveaxis(bias_in, 0, 2).reshape(3, 4, heads, head_dim)
+    bias_in = lax.dynamic_index_in_dim(bias_in, part, 1, keepdims=False)
+    bias_in = bias_in.reshape(1, 3 * inner)
     heads_row, units_row = by_place(widths)
     head_ids = (y * 4 + part) * heads + jnp.arange(heads, dtype=jnp.int32)
     head_active = (head_ids[:, None] // (HEADS // GROUPS) < heads_row[None, :]).astype(WIDE)
@@ -888,11 +1012,11 @@
     unit_group = (y * 4 + part) * units // (FF // GROUPS)
     unit_active = (unit_group < units_row).astype(WIDE)[:, None]
     (
-        tokens_all, in_x, in_z1, in_z2, in_zx1, e_out, cotangent_own, up_weight, down_weight,
+        tokens_all, in_x, in_z1, in_z2, in_zx1, e_out, cotangent, up_weight, down_weight,
         vectors_f, router, bias_in, bias_up, head_active, unit_active,
         cosine, sine, signed, span, key_place,
     ) = tie(
-        tokens_all, in_x, in_z1, in_z2, in_zx1, e_out, cotangent_own, up_weight, down_weight,
+        tokens_all, in_x, in_z1, in_z2, in_zx1, e_out, cotangent, up_weight, down_weight,
         vectors_f, router, bias_in, bias_up, head_active, unit_active,
         cosine, sine, signed, span, key_place,
     )
@@ -905,27 +1029,28 @@
     out_x = swap(e_out, "x")
     e_up = exchange(jnp.moveaxis(up_weight.reshape(block, 4, units), 1, 0))
     e_up = e_up.reshape(4 * block, units)
-    cotangent_all = lax.all_gather(cotangent_own, GROUP, axis=0, tiled=True)
+    cotangent_pieces = to_batch(cotangent)
     normed_low, logits = norm_rows(bits, tokens_all, gain_one, shift_one, router)
-    normed_low, in_zx2, out_z, out_x, e_up, down_weight, logits = tie(
-        normed_low, in_zx2, out_z, out_x, e_up, down_weight, logits
-    )
+    normed_low, in_zx2, out_z, out_x, e_up, down_weight, logits, *cotangent_pieces = tie(
+        normed_low, in_zx2, out_z, out_x, e_up, down_weight, logits, *cotangent_pieces
+    )
+    cotangent_own = jnp.concatenate(cotangent_pieces, axis=0)
 
     def mine(value):
         return lax.dynamic_slice_in_dim(value, place * own, own, 0)
 
-    up_cut = e_up.shape[0] // 2
+    cut_units = units // 2
     out_zx = swap(out_z, "x")
-    up_x1 = swap(e_up[:up_cut], "x")
-    up_z1 = swap(e_up[:up_cut], "zh")
+    up_x1 = swap(e_up[:, :cut_units], "x")
+    up_z1 = swap(e_up[:, :cut_units], "zh")
     e_down = exchange(down_weight.reshape(4, units, block))
     e_down = jnp.moveaxis(e_down, 0, 1).reshape(units, 4 * block)
     w_in = (e_in, in_x, in_z1, in_z2, in_zx1, in_zx2)
     qkv = qkv_rows(normed_low, w_in, bias_in, cosine, signed)
     mixed, lse = attend(qkv, key_place, span, head_active, heads)
     w_out = jnp.concatenate([e_out, out_x, out_z, out_zx], axis=1)
-    mixed, w_out, e_up, e_down, up_x1, up_z1, cotangent_own, tokens_own, logits, w_in = tie(
-        mixed, w_out, e_up, e_down, up_x1, up_z1, cotangent_own, tokens_own, logits, w_in
+    mixed, w_out, e_up, e_down, up_x1, up_z1, cotangent_own, tokens_own, logits = tie(
+        mixed, w_out, e_up, e_down, up_x1, up_z1, cotangent_own, tokens_own, logits
     )
 
     part_own = own // 2
@@ -953,12 +1078,13 @@
 
     attn_here, attn_away = halves(mixed)
     attn_away = dot_to(attn_away, w_out, ((1,), (0,))).astype(LOW)
+    cotangent_all = lax.all_gather(cotangent_own, GROUP, axis=0, tiled=True)
     attn_away, attn_here, tokens_own, cotangent_own, logits = tie(
         attn_away, attn_here, tokens_own, cotangent_own, logits
     )
     attn_got = swap(attn_away, "c")
-    up_x2 = swap(e_up[up_cut:], "x")
-    up_z2 = swap(e_up[up_cut:], "zh")
+    up_x2 = swap(e_up[:, cut_units:], "x")
+    up_z2 = swap(e_up[:, cut_units:], "zh")
     up_zx1 = swap(up_z1, "x")
     options = jnp.arange(GROUPS, dtype=jnp.int32)
     attn_prob = jax.nn.softmax(logits[:, :GROUPS], axis=-1)
@@ -972,12 +1098,10 @@
         attn_total, attn_gate, ffn_gate, tokens_own, cotangent_own
     )
     attn_parts = group_second(attn_total)
-    rows = to_own_order(tokens_own, zh, x).astype(WIDE)
-    upstream = to_own_order(cotangent_own, zh, x).astype(WIDE)
+    rows, upstream = own_rows(bits, tokens_own, cotangent_own)
     *attn_parts, rows, upstream, up_x2 = tie(*attn_parts, rows, upstream, up_x2)
     attn_sum = group_third(*attn_parts)
-    down_cut = e_down.shape[1] // 2
-    down_x1 = swap(e_down[:, :down_cut], "x")
+    down_x1 = swap(e_down[:cut_units], "x")
     attn_sum, cotangent_all, up_z2, up_zx1, down_x1, e_down = tie(
         attn_sum, cotangent_all, up_z2, up_zx1, down_x1, e_down
     )
@@ -988,45 +1112,38 @@
     resid = rows + attn_gate_own * attn_branch
     normed_two, scaled_two, inverse_two = norm_forward(resid, gain_two, shift_two)
     normed_two_low = normed_two.astype(LOW)
-    normed_two_low, e_down, cotangent_all, w_in, up_z2 = tie(
-        normed_two_low, e_down, cotangent_all, w_in, up_z2
+    normed_two_low, e_down, cotangent_all, up_z2 = tie(
+        normed_two_low, e_down, cotangent_all, up_z2
     )
     normed_two_low = lax.all_gather(normed_two_low, GROUP, axis=0, tiled=True)
-    down_z1 = swap(e_down[:, :down_cut], "zh")
+    down_z1 = swap(e_down[:cut_units], "zh")
     up_zx2 = swap(up_z2, "x")
-    down_x2 = swap(e_down[:, down_cut:], "x")
+    down_x2 = swap(e_down[cut_units:], "x")
     down_grad = gate_rows(bits, cotangent_all, ffn_gate)
-    w_in = jnp.concatenate(w_in, axis=0)
-    down_grad, down_z1, up_zx2, down_x2, w_in, e_down = tie(
-        down_grad, down_z1, up_zx2, down_x2, w_in, e_down
-    )
-    down_z2 = swap(e_down[:, down_cut:], "zh")
+    down_grad, down_z1, up_zx2, down_x2, e_down = tie(
+        down_grad, down_z1, up_zx2, down_x2, e_down
+    )
+    down_z2 = swap(e_down[cut_units:], "zh")
     down_zx1 = swap(down_z1, "x")
-    hidden_grad = hidden_grad_rows(down_grad, (e_down, down_x1, down_x2, down_z1))
-    w_up = jnp.concatenate([e_up, up_x1, up_x2, up_z1, up_z2, up_zx1, up_zx2], axis=0)
-    normed_two_low, hidden_grad, w_up, down_z2, down_zx1 = tie(
-        normed_two_low, hidden_grad, w_up, down_z2, down_zx1
-    )
+    normed_two_low, down_z2, down_zx1 = tie(normed_two_low, down_z2, down_zx1)
 
     def columns(value, k):
         return value[:, k * 4 * block : (k + 1) * 4 * block]
 
     down_zx2 = swap(down_z2, "x")
-    up_pre = dot_to(normed_two_low, w_up, ((1,), (0,))) + bias_up
-    relu_part = jnp.maximum(up_pre, 0.0) * unit_active
-    relu_part, down_zx2, hidden_grad, w_up = tie(relu_part, down_zx2, hidden_grad, w_up)
-    late = jnp.concatenate([down_z2, down_zx1, down_zx2], axis=1)
-    late_at = width - late.shape[1]
-    hidden_grad = hidden_grad + dot_to(down_grad[:, late_at:], late, ((1,), (1,)))
-    up_grad = (hidden_grad * 2.0 * relu_part).astype(LOW)
-    w_down = (e_down, down_x1, down_x2, down_z1, down_z2, down_zx1, down_zx2)
-    two_here, two_away = halves(up_grad)
-    two_away = dot_to(two_away, w_up, ((1,), (1,))).astype(LOW)
-    two_away, two_here, relu_part, down_grad, up_grad = tie(
-        two_away, two_here, relu_part, down_grad, up_grad
-    )
+    w_up = (
+        (e_up[:, :cut_units], up_x1, up_z1, up_zx1),
+        (e_up[:, cut_units:], up_x2, up_z2, up_zx2),
+    )
+    relu_part, hidden = hidden_rows(normed_two_low, unit_active, bias_up, w_up)
+    relu_part, hidden, down_zx2 = tie(relu_part, hidden, down_zx2)
+    w_down = (
+        (e_down[:cut_units], down_x1, down_z1, down_zx1),
+        (e_down[cut_units:], down_x2, down_z2, down_zx2),
+    )
+    up_grad, two_part = ffn_rows(core, down_grad, relu_part, w_down, w_up)
+    two_away, two_here = two_part[: length // 2], two_part[length // 2 :]
     two_got = swap(two_away, "c")
-    hidden = jnp.square(relu_part).astype(LOW)
 
     def down_piece(k):
         return dot_to(hidden, columns(down_grad, k), ((0,), (0,)))
@@ -1036,7 +1153,7 @@
 
     down_send3 = down_piece(3).astype(LOW)
     down_got3 = swap(down_send3, "x")
-    two_total = dot_to(two_here, w_up, ((1,), (1,))) + two_got.astype(WIDE)
+    two_total = two_here.astype(WIDE) + two_got.astype(WIDE)
     two_total, hidden, up_grad, down_send3 = tie(two_total, hidden, up_grad, down_send3)
     two_parts = group_second(two_total)
     up_send3 = up_piece(3).astype(LOW)
@@ -1058,60 +1175,66 @@
         gated_low, hidden, down_grad, up_grad, normed_two_grad, resid_grad, down_send2
     )
     attn_out_grad = lax.all_gather(gated_low, GROUP, axis=0, tiled=True)
-    down_far = swap(down_send2, "zh")
+    down_far1 = swap(down_send2[:cut_units], "zh")
     down_got1 = swap(down_send1, "x")
-    ffn_away, ffn_here = wide_rows(core, hidden, w_down)
-    ffn_got = swap(ffn_away, "c")
-    ffn_total = ffn_here.astype(WIDE) + ffn_got.astype(WIDE)
+    w_in = jnp.concatenate(w_in, axis=0)
+    ffn_part = wide_rows(hidden, w_down)
     grad_gain_two = jnp.sum(normed_two_grad * scaled_two, axis=0)
     grad_shift_two = jnp.sum(normed_two_grad, axis=0)
     attn_gate_grad = jnp.sum(resid_grad * attn_branch, axis=-1)
     grad_out_bias = jnp.sum(attn_gate_own * resid_grad, axis=0)
     up_send1 = up_piece(1).astype(LOW)
     up_send2 = (up_piece(2) + up_got3.astype(WIDE)).astype(LOW)
-    attn_out_grad, ffn_total, up_send1, up_send2, grad_out_bias, grad_gain_two, down_far = tie(
-        attn_out_grad, ffn_total, up_send1, up_send2, grad_out_bias, grad_gain_two, down_far
-    )
-
-    up_rows = up_send2.shape[0] // 2
-    up_far1 = swap(up_send2[:up_rows], "zh")
-    ffn_parts = group_second(ffn_total)
+    (
+        attn_out_grad, ffn_part, up_send1, up_send2, grad_out_bias, grad_gain_two, w_in,
+        down_far1, down_send2,
+    ) = tie(
+        attn_out_grad, ffn_part, up_send1, up_send2, grad_out_bias, grad_gain_two, w_in,
+        down_far1, down_send2,
+    )
+    down_far2 = swap(down_send2[cut_units:], "zh")
+
+    def out_piece(k):
+        return dot_to(mixed, columns(attn_out_grad, k), ((0,), (0,)))
+
+    ffn_sum = lax.psum_scatter(ffn_part, GROUP, scatter_dimension=0, tiled=True)
+    out_got = swap(jnp.stack([out_piece(1), out_piece(3)]).astype(LOW), "x")
     proj_grad = attend_back(
         qkv, attn_out_grad, w_out, head_active, lse, key_place, span, cosine, sine, heads
     )
-    proj_grad, *ffn_parts, attn_out_grad, down_got1, up_far1, hidden, up_send1, up_send2 = tie(
-        proj_grad, *ffn_parts, attn_out_grad, down_got1, up_far1, hidden, up_send1, up_send2
+    proj_grad, attn_out_grad, down_got1, down_far2, hidden, up_send1, up_send2, out_got = tie(
+        proj_grad, attn_out_grad, down_got1, down_far2, hidden, up_send1, up_send2, out_got
     )
 
     def in_piece(k):
         return dot_to(columns(normed_low, k), proj_grad, ((0,), (0,)))
 
-    def out_piece(k):
-        return dot_to(mixed, columns(attn_out_grad, k), ((0,), (0,)))
-
     one_here, one_away = halves(proj_grad)
     one_away = dot_to(one_away, w_in, ((1,), (1,))).astype(LOW)
-    one_away, one_here, proj_grad, attn_out_grad, *ffn_parts, hidden = tie(
-        one_away, one_here, proj_grad, attn_out_grad, *ffn_parts, hidden
+    one_away, one_here, proj_grad, hidden, out_got, up_send2 = tie(
+        one_away, one_here, proj_grad, hidden, out_got, up_send2
     )
     one_got = swap(one_away, "c")
-    up_far2 = swap(up_send2[up_rows:], "zh")
+    up_far = swap(up_send2, "zh")
     in_send3 = in_piece(3).astype(LOW)
     in_got3 = swap(in_send3, "x")
-    ffn_sum = group_third(*ffn_parts)
     one_total = dot_to(one_here, w_in, ((1,), (1,))) + one_got.astype(WIDE)
-    one_total, proj_grad, attn_out_grad, ffn_sum, in_send3 = tie(
-        one_total, proj_grad, attn_out_grad, ffn_sum, in_send3
+    one_total, proj_grad, in_send3, out_got, up_send1, hidden = tie(
+        one_total, proj_grad, in_send3, out_got, up_send1, hidden
     )
     one_parts = group_second(one_total)
     in_send1 = in_piece(1).astype(LOW)
-    out_send = jnp.stack([out_piece(1), out_piece(3)]).astype(LOW)
-    ffn_branch = ffn_sum + bias_down
-    block_out = (resid + ffn_gate_own * ffn_branch).astype(LOW)
+    out_send2 = (out_piece(2) + out_got[1].astype(WIDE)).astype(LOW)
+    *one_parts, in_send1, out_send2, in_got3, ffn_sum, up_send1, hidden = tie(
+        *one_parts, in_send1, out_send2, in_got3, ffn_sum, up_send1, hidden
+    )
+    normed_sum = group_third(*one_parts)
+    in_got1 = swap(in_send1, "x")
+    up_got1 = swap(up_send1, "x")
+    out_far = swap(out_send2, "zh")
+    in_send2 = (in_piece(2) + in_got3.astype(WIDE)).astype(LOW)
+    ffn_branch = ffn_sum.astype(WIDE) + bias_down
     ffn_gate_grad = jnp.sum(upstream * ffn_branch, axis=-1)
-    grad_down_bias = jnp.sum(ffn_gate_own * upstream, axis=0)
-    grad_up_bias = jnp.sum(up_grad.astype(WIDE), axis=0)
-    grad_in_bias = jnp.sum(proj_grad.astype(WIDE), axis=0).reshape(3, heads, head_dim)
     logit_grad = jnp.concatenate(
         [
             gate_logit_grad(mine(attn_prob), mine(attn_pick), attn_gate_grad),
@@ -1119,8 +1242,6 @@
         ],
         axis=-1,
     )
-    normed_own = mine(normed_low)
-    grad_router = jnp.dot(logit_grad.T, normed_own.astype(WIDE), precision=HIGHEST)
     router_part = jnp.dot(logit_grad, vectors_f[6:], precision=HIGHEST)
 
     def both_halves(value, other):
@@ -1139,8 +1260,25 @@
         rows = from_own_order(rows, zh, x)
         return jnp.swapaxes(rows.reshape(cut, 16, block), 0, 1).reshape(16, cut * block)
 
+    normed_sum, in_send2, router_part, ffn_branch, logit_grad, up_far, hidden = tie(
+        normed_sum, in_send2, router_part, ffn_branch, logit_grad, up_far, hidden
+    )
+
+    in_far = swap(in_send2, "zh")
+    tokens_low, last = first_back(bits, normed_sum, router_part, rows, resid_grad, gain_one)
+    tokens_low = tokens_low.reshape(4, half, width)
+    tokens_low, last, ffn_branch, logit_grad, up_grad, out_far, up_far, hidden = tie(
+        tokens_low, last, ffn_branch, logit_grad, up_grad, out_far, up_far, hidden
+    )
+    tokens_pieces = across([tokens_low[k] for k in range(4)])
+    block_low = home_rows(bits, resid + ffn_gate_own * ffn_branch).reshape(4, half, width)
+    normed_own = mine(normed_low)
+    grad_router = jnp.dot(logit_grad.T, normed_own.astype(WIDE), precision=HIGHEST)
+    grad_down_bias = jnp.sum(ffn_gate_own * upstream, axis=0)
+    grad_up_bias = jnp.sum(up_grad.astype(WIDE), axis=0)
+    grad_in_bias = jnp.sum(proj_grad.astype(WIDE), axis=0).reshape(3, heads, head_dim)
     sums = jnp.stack([grad_out_bias, grad_gain_two, grad_shift_two, grad_down_bias])
-    sums = spread(jnp.concatenate([sums, grad_router], axis=0), n_vec - 2)
+    sums = spread(jnp.concatenate([last, sums, grad_router], axis=0), n_vec)
     chosen = (jnp.arange(4) == part).astype(WIDE)
     spread_in = (grad_in_bias[:, None] * chosen[None, :, None, None]).reshape(
         3, tp_heads, 16, head_dim // 16
@@ -1148,57 +1286,27 @@
     spread_in = jnp.moveaxis(spread_in, 2, 0).reshape(16, -1)
     spread_up = (grad_up_bias[None, :] * chosen[:, None]).reshape(up_bias.shape[0], 16, block)
     spread_up = jnp.moveaxis(spread_up, 1, 0).reshape(16, -1)
-    early = jnp.concatenate([sums, spread_in, spread_up], axis=1)
-    _, scaled_one, inverse_one = norm_forward(rows, gain_one, shift_one)
-    block_low = from_own_order(block_out, zh, x).reshape(4, half, width)
-    (
-        *one_parts, in_send1, out_send, block_low, early, router_part, scaled_one, inverse_one,
-        in_got3,
-    ) = tie(
-        *one_parts, in_send1, out_send, block_low, early, router_part, scaled_one, inverse_one,
-        in_got3,
-    )
-    normed_sum = group_third(*one_parts)
-    in_got1 = swap(in_send1, "x")
-    up_got1 = swap(up_send1, "x")
-    in_send2 = (in_piece(2) + in_got3.astype(WIDE)).astype(LOW)
+    total = jnp.concatenate([sums, spread_in, spread_up], axis=1)
+    down_far = jnp.concatenate([down_far1, down_far2], axis=0)
     down_home = (down_piece(0) + down_got1.astype(WIDE) + down_far.astype(WIDE)).astype(LOW)
-    normed_sum, in_send2, block_low, early, out_send, up_grad, up_far2, in_got1, down_home = tie(
-        normed_sum, in_send2, block_low, early, out_send, up_grad, up_far2, in_got1, down_home
-    )
-
-    in_far = swap(in_send2, "zh")
     down_home = exchange(jnp.moveaxis(down_home.reshape(units, 4, block), 1, 0))
-    normed_grad = normed_sum + router_part
-    tokens_grad = resid_grad + norm_backward(normed_grad, scaled_one, inverse_one, gain_one)
-    tokens_low = from_own_order(tokens_grad.astype(LOW), zh, x).reshape(4, half, width)
-    tokens_low, normed_grad, block_low, out_send, up_grad, early = tie(
-        tokens_low, normed_grad, block_low, out_send, up_grad, early
-    )
-    tokens_pieces = across([tokens_low[k] for k in range(4)])
-    grad_gain_one = jnp.sum(normed_grad * scaled_one, axis=0)
-    grad_shift_one = jnp.sum(normed_grad, axis=0)
-    last = spread(jnp.stack([grad_gain_one, grad_shift_one]), 2)
-    up_far = jnp.concatenate([up_far1, up_far2], axis=0)
     up_home = (up_piece(0) + up_got1.astype(WIDE) + up_far.astype(WIDE)).astype(LOW)
-    out_got = swap(out_send, "x")
-    *tokens_pieces, last, early, block_low, out_got, in_far, up_home, down_home = tie(
-        *tokens_pieces, last, early, block_low, out_got, in_far, up_home, down_home
-    )
+    up_home = exchange(up_home.reshape(4, block, units))
+    out_home = (out_piece(0) + out_got[0].astype(WIDE) + out_far.astype(WIDE)).astype(LOW)
+    *tokens_pieces, total, block_low, up_home, out_home, in_got1, down_home, in_far = tie(
+        *tokens_pieces, total, block_low, up_home, out_home, in_got1, down_home, in_far
+    )
+    total = reduce_rows(total, zh, zl, x, c)
     tokens_grad = jnp.stack(tokens_pieces)
     tokens_other = swap(tokens_grad, "y")
+    block_out = jnp.stack(across([block_low[k] for k in range(4)]))
+    out_home = exchange(jnp.moveaxis(out_home.reshape(inner, 4, block), 1, 0))
     in_home = (in_piece(0) + in_got1.astype(WIDE) + in_far.astype(WIDE)).astype(LOW)
-    out_far = swap((out_piece(2) + out_got[1].astype(WIDE)).astype(LOW), "zh")
-    block_out = jnp.stack(across([block_low[k] for k in range(4)]))
-    total = reduce_rows(jnp.concatenate([last, early], axis=1), zh, zl, x, c)
-    up_home = exchange(up_home.reshape(4, block, units))
-    tokens_other, block_out, out_far, in_home, up_home, total = tie(
-        tokens_other, block_out, out_far, in_home, up_home, total
+    tokens_other, block_out, in_home, out_home, total = tie(
+        tokens_other, block_out, in_home, out_home, total
     )
     block_other = swap(block_out, "y")
     in_home = exchange(in_home.reshape(4, block, 3 * inner)).reshape(4, block, 3, heads, head_dim)
-    out_home = (out_piece(0) + out_got[0].astype(WIDE) + out_far.astype(WIDE)).astype(LOW)
-    out_home = exchange(jnp.moveaxis(out_home.reshape(inner, 4, block), 1, 0))
     at = n_vec * block
     shared = total[:at]
     shared = (shared + swap(shared, "y")).reshape(n_vec, block)

time: 713 us -> 666 us (0.934)
  local copies, waits for them, and re-layouts: 110 us -> 76.6 us
  Pallas kernels: 70.1 us -> 98 us
  starting transfers between devices: 126 us -> 103 us
  other arithmetic: 64.4 us -> 51.6 us
  matrix products: 74.6 us -> 64.4 us
    ppermute x71 -> x66, waiting for transfers between devices: 187 us -> 232 us  [swap(): return lax.ppermute(value, axis, [(0, 1), (1, 0)])]
    pallas_call x2 -> x6, Pallas kernels: 16.3 us -> 44.1 us  [the longest x1 15.3 us: ffn_rows(): pl.pallas_call(functools.partial(ffn_kernel, tuple((len(g) for g in down_...]
    all_to_all x8, waiting for transfers between devices: 31.8 us -> 4.78 us  [exchange(): return lax.all_to_all(value, ('zl', 'c'), 0, 0, tiled=True)]
    ppermute x71 -> x66, starting transfers between devices: 81.3 us -> 66.4 us  [swap(): return lax.ppermute(value, axis, [(0, 1), (1, 0)])]
    dot_general x25 -> x20, matrix products: 72.3 us -> 60.8 us  [dot_to(): lax.dot_general(left, right, (dims, ((), ())), preferred_element_type=WIDE)]
    ppermute x4, waiting for transfers between devices: 21.2 us -> 9.7 us  [across(): lax.ppermute(pieces[3], PARTS, [(i, i ^ 3) for i in range(4)])]
    all_gather x1, starting transfers between devices: 10.3 us -> 0.51 us  [grouped(): normed_two_low = lax.all_gather(normed_two_low, GROUP, axis=0, tiled=True)]
    convert_element_type x4 -> x0, local copies, waits for them, and re-layouts: 8.74 us -> none  [the longest x2 4.9 us: grouped(): upstream = to_own_order(cotangent_own, zh, x).astype(WIDE)]
  transfers between devices with their start and end apart: 87 -> 83, of which waited for: 38 -> 37; matrix products, arithmetic and copies ran while one was open for 29% -> 25% of each run, Pallas kernels for 10% -> 13%
where the time goes in v3:
time: 666 us; the launch traced here: 656 us
  waiting for transfers between devices  246 us (37%)
  starting transfers between devices  103 us (15%)
  Pallas kernels  98 us (15%)
  local copies, waits for them, and re-layouts  76.6 us (12%)
  matrix products  64.4 us (10%)
  other arithmetic  51.6 us (8%)
  between operations  16 us (2%)
    ppermute x66, waiting for transfers between devices, swap(): return lax.ppermute(value, axis, [(0, 1), (1, 0)])  232 us
    ppermute x66, starting transfers between devices, swap(): return lax.ppermute(value, axis, [(0, 1), (1, 0)])  66.4 us
    dot_general x20, matrix products, dot_to(): lax.dot_general(left, right, (dims, ((), ())), preferred_element_type=WIDE)  60.8 us
    all_to_all x8, starting transfers between devices, exchange(): return lax.all_to_all(value, ('zl', 'c'), 0, 0, tiled=True)  28.9 us
    pallas_call x1, Pallas kernels, attend_back(): pl.pallas_call(attend_back_kernel, grid=(heads, length // BLOCK_Q), in_sp...  21 us
    unnamed x212, local copies, waits for them, and re-layouts  18.8 us
    pallas_call x1, Pallas kernels, ffn_rows(): pl.pallas_call(functools.partial(ffn_kernel, tuple((len(g) for g in down_...  15.3 us
  transfers between devices with their start and end apart: 83, of which 37 were waited for; matrix products, arithmetic and copies ran while one was open for 25% of the time, Pallas kernels for 13%

profile of v3, /device:TPU:0, one launch (start us, length us, event | category | flops | bytes accessed | tf_op | source)
XLA Modules:
  0.0 655.9 jit_solution(17210439256683414694)
XLA Ops:
  10.0 4.3 all-to-all-start
  18.2 5.9 collective-permute-done.3
  36.0 5.5 collective-permute-done.1
  42.4 3.4 all-to-all-start.1
  63.6 28.6 %collective-permute-done.6.refs_2_ = bf16[256,768]{1,0:T(8,128)(2,1)S(1)} collective-permute-done((bf16[256,768]{1,0:T(8,128)(2,1)}, bf16[256,768]{1,0:T(8,128)(2,1)S(1)}, u32[]{:S(2)}, u32[]{:S(2)}) %collective-permute-start.6) | collective-permute-done | bytes 393248 | tf_op jit(solution)/shard_map/ppermute | solution.py:366
  98.5 3.6 collective-permute-done.8.refs_4_
  104.8 3.5 all-to-all-start.2
  115.7 8.0 %collective-permute-done.16 = bf16[32,2048]{1,0:T(8,128)(2,1)S(1)} collective-permute-done((bf16[32,2048]{1,0:T(8,128)(2,1)S(1)}, bf16[32,2048]{1,0:T(8,128)(2,1)S(1)}, u32[]{:S(2)}, u32[]{:S(2)}) %collective-permute-start.16) | collective-permute-done | bytes 131104 | tf_op jit(solution)/shard_map/ppermute | solution.py:916
  124.7 7.8 %norm_rows.1 = (bf16[1024,2048]{1,0:T(8,128)(2,1)}, f32[1024,8]{1,0:T(8,128)}) custom-call(s32[2]{0:T(128)} %pad_add_fusion.1.bits_ref, bf16[1024,2048]{1,0:T(8,128)(2,1)} %all-gather.5.cloned.1.call-done.x_ref, f32[1,2048]{1,0:T(1,128)} %get-tuple-element.458.gain_ref, f32[1,2048]{1,0:T(1,128)} %get-tuple-element.457.shift_ref, bf16[8,2048]{1,0:T(8,128)(2,1)} %bitcast.334), custom_call_target="tpu_custom_call" | custom-call | tf_op jit(solution)/shard_map/norm_rows/pallas_call | solution.py:451
  132.5 3.5 collective-permute-done.15
  136.7 3.5 all-to-all-start.3
  145.4 7.8 %qkv_rows.1.q_ref.k_ref.v_ref = bf16[1024,768]{1,0:T(8,128)(2,1)} custom-call(bf16[1024,2048]{1,0:T(8,128)(2,1)} %get-tuple-element.219.h_ref, bf16[512,768]{1,0:T(8,128)(2,1)} %copy-done.7, bf16[512,768]{1,0:T(8,128)(2,1)} %copy-done.24, bf16[256,768]{1,0:T(8,128)(2,1)} %copy-done.38, bf16[256,768]{1,0:T(8,128)(2,1)} %copy-done.36, ...), custom_call_target="tpu_custom_call" | custom-call | tf_op jit(solution)/shard_map/qkv_rows/pallas_call | solution.py:739
  153.2 11.2 %attend.1 = (bf16[1024,256]{1,0:T(8,128)(2,1)}, f32[2,1,1024]{2,1,0:T(1,128)}) custom-call(bf16[1024,768]{1,0:T(8,128)(2,1)} %qkv_rows.1.q_ref.k_ref.v_ref, bf16[1024,768]{1,0:T(8,128)(2,1)} %qkv_rows.1.q_ref.k_ref.v_ref, bf16[1024,768]{1,0:T(8,128)(2,1)} %qkv_rows.1.q_ref.k_ref.v_ref, s32[1024,1]{1,0:T(8,128)} %copy.207.key_ref, ...), custom_call_target="tpu_custom_call" | custom-call | tf_op jit(solution)/shard_map/attend/pallas_call | solution.py:817
  166.4 3.9 collective-permute-done.19.refs_2_.refs_10_
  192.4 3.4 own_rows.1
  199.9 19.4 %collective-permute-done.21 = bf16[2,64,2048]{2,1,0:T(8,128)(2,1)S(1)} collective-permute-done((bf16[2,64,2048]{2,1,0:T(8,128)(2,1)S(1)}, bf16[2,64,2048]{2,1,0:T(8,128)(2,1)S(1)}, u32[]{:S(2)}, u32[]{:S(2)}) %collective-permute-start.21) | collective-permute-done | bytes 524320 | tf_op jit(solution)/shard_map/ppermute | solution.py:366
  221.8 5.9 collective-permute-done.24
  238.2 6.0 gate_rows.1.dz_ref
  244.2 4.1 collective-permute-done.30.refs_7_.refs_15_
  248.3 8.9 %collective-permute-done.31.refs_5_ = bf16[512,512]{1,0:T(8,128)(2,1)S(1)} collective-permute-done((bf16[512,512]{1,0:T(8,128)(2,1)}, bf16[512,512]{1,0:T(8,128)(2,1)S(1)}, u32[]{:S(2)}, u32[]{:S(2)}) %collective-permute-start.31) | collective-permute-done | bytes 524320 | tf_op jit(solution)/shard_map/ppermute | solution.py:366
  263.0 24.0 %collective-permute-done.32.refs_6_ = bf16[512,512]{1,0:T(8,128)(2,1)S(1)} collective-permute-done((bf16[512,512]{1,0:T(8,128)(2,1)S(1)}, bf16[512,512]{1,0:T(8,128)(2,1)S(1)}, u32[]{:S(2)}, u32[]{:S(2)}) %collective-permute-start.32) | collective-permute-done | bytes 524320 | tf_op jit(solution)/shard_map/ppermute | solution.py:366
  289.3 9.5 %hidden_rows.1 = (f32[1024,1024]{1,0:T(8,128)}, bf16[1024,1024]{1,0:T(8,128)(2,1)}) custom-call(bf16[1024,2048]{1,0:T(8,128)(2,1)} %all-gather.9.cloned.1.call-done.h_ref, f32[1024,1]{1,0:T(8,128)} %copy.212.active_ref, f32[1,1024]{1,0:T(1,128)} %constant_dynamic-slice_fusion.8.bias_ref, bf16[512,512]{1,0:T(8,128)(2,1)} %get-tuple-element.421.refs_0_.refs_8_, ...), custom_call_target="tpu_custom_call" | custom-call | tf_op jit(solution)/shard_map/hidden_rows/pallas_call | solution.py:539
  300.8 15.3 %ffn_rows.1 = (bf16[1024,1024]{1,0:T(8,128)(2,1)}, bf16[1024,2048]{1,0:T(8,128)(2,1)}) custom-call(s32[1]{0:T(128)} %bitcast.52.bit_ref, bf16[1024,2048]{1,0:T(8,128)(2,1)} %gate_rows.1.dz_ref, f32[1024,1024]{1,0:T(8,128)} %get-tuple-element.287.relu_ref, bf16[512,512]{1,0:T(8,128)(2,1)} %get-tuple-element.419.refs_0_, ...), custom_call_target="tpu_custom_call" | custom-call | tf_op jit(solution)/shard_map/ffn_rows/pallas_call | solution.py:595
  325.1 3.6 convolution_convert_fusion.3
  332.6 12.4 %collective-permute-done.38 = bf16[1024,512]{1,0:T(8,128)(2,1)S(1)} collective-permute-done((bf16[1024,512]{1,0:T(8,128)(2,1)S(1)}, bf16[1024,512]{1,0:T(8,128)(2,1)S(1)}, u32[]{:S(2)}, u32[]{:S(2)}) %collective-permute-start.38) | collective-permute-done | bytes 1048608 | tf_op jit(solution)/shard_map/ppermute | solution.py:366
  348.0 4.2 collective-permute-done.39
  363.5 8.7 %wide_rows.1 = bf16[1024,2048]{1,0:T(8,128)(2,1)} custom-call(bf16[1024,1024]{1,0:T(8,128)(2,1)} %get-tuple-element.369.left_ref, bf16[512,512]{1,0:T(8,128)(2,1)} %get-tuple-element.419.refs_0_, bf16[512,512]{1,0:T(8,128)(2,1)} %collective-permute-done.28.refs_1_, bf16[512,512]{1,0:T(8,128)(2,1)} %copy-done.31, bf16[512,512]{1,0:T(8,128)(2,1)} %copy-done.33, ...), custom_call_target="tpu_custom_call" | custom-call | tf_op jit(solution)/shard_map/wide_rows/pallas_call | solution.py:638
  376.6 3.6 convolution_convert_fusion.2
  383.1 3.8 add_convert_fusion.2
  387.0 9.8 %collective-permute-done.42 = bf16[512,512]{1,0:T(8,128)(2,1)} collective-permute-done((bf16[512,512]{1,0:T(8,128)(2,1)S(1)}, bf16[512,512]{1,0:T(8,128)(2,1)}, u32[]{:S(2)}, u32[]{:S(2)}) %collective-permute-start.42) | collective-permute-done | bytes 524320 | tf_op jit(solution)/shard_map/ppermute | solution.py:366
  405.2 21.0 %attend_back.1 = bf16[1024,768]{1,0:T(8,128)(2,1)} custom-call(bf16[1024,768]{1,0:T(8,128)(2,1)} %qkv_rows.1.q_ref.k_ref.v_ref, bf16[1024,768]{1,0:T(8,128)(2,1)} %qkv_rows.1.q_ref.k_ref.v_ref, bf16[1024,768]{1,0:T(8,128)(2,1)} %qkv_rows.1.q_ref.k_ref.v_ref, bf16[1024,2048]{1,0:T(8,128)(2,1)} %all-gather.11.cloned.1.call-done.da_ref, ...), custom_call_target="tpu_custom_call" | custom-call | tf_op jit(solution)/shard_map/attend_back/pallas_call | solution.py:844
  426.2 4.7 collective-permute-done.45
  433.0 5.3 convolution_convert_fusion.1
  444.0 3.7 convolution_convert_fusion.7
  451.8 6.5 convert_add_fusion
  473.8 29.5 %collective-permute-done.47 = bf16[2,64,2048]{2,1,0:T(8,128)(2,1)} collective-permute-done((bf16[2,64,2048]{2,1,0:T(8,128)(2,1)S(1)}, bf16[2,64,2048]{2,1,0:T(8,128)(2,1)}, u32[]{:S(2)}, u32[]{:S(2)}) %collective-permute-start.47) | collective-permute-done | bytes 524320 | tf_op jit(solution)/shard_map/ppermute | solution.py:366
  506.0 3.4 add_convert_fusion.5
  516.7 8.0 %collective-permute-done.51 = bf16[64,2048]{1,0:T(8,128)(2,1)S(1)} collective-permute-done((bf16[64,2048]{1,0:T(8,128)(2,1)S(1)}, bf16[64,2048]{1,0:T(8,128)(2,1)S(1)}, u32[]{:S(2)}, u32[]{:S(2)}) %collective-permute-start.51) | collective-permute-done | bytes 262176 | tf_op jit(solution)/shard_map/ppermute | solution.py:366
  525.8 4.6 first_back.1
  530.4 4.1 fusion.5
  538.3 3.7 all-to-all-start.5
  545.6 3.4 collective-permute-start.55
  560.8 3.5 all-to-all-start.4
  572.7 6.4 collective-permute-done.55
  579.0 16.3 %collective-permute-done.59 = bf16[512,768]{1,0:T(8,128)(2,1)S(1)} collective-permute-done((bf16[512,768]{1,0:T(8,128)(2,1)}, bf16[512,768]{1,0:T(8,128)(2,1)S(1)}, u32[]{:S(2)}, u32[]{:S(2)}) %collective-permute-start.59) | collective-permute-done | bytes 786464 | tf_op jit(solution)/shard_map/ppermute | solution.py:366
  599.3 3.4 all-to-all-start.6
  625.4 3.6 all-to-all-start.7
  635.5 8.5 %collective-permute-done.68 = bf16[4,32,2048]{2,1,0:T(8,128)(2,1)} collective-permute-done((bf16[4,32,2048]{2,1,0:T(8,128)(2,1)S(1)}, bf16[4,32,2048]{2,1,0:T(8,128)(2,1)}, u32[]{:S(2)}, u32[]{:S(2)}) %collective-permute-start.68) | collective-permute-done | bytes 524320 | tf_op jit(solution)/shard_map/ppermute | solution.py:366
  (591 shorter events, 256.9 us)
Async XLA Ops:
  10.0 21.3 %all-to-all-start = ((bf16[4,128,3,2,128]{4,3,2,1,0:T(2,128)(2,1)}), bf16[4,128,3,2,128]{4,3,2,1,0:T(2,128)(2,1)S(1)}, u32[]{:S(2)}, u32[]{:S(2)}) async-start(bf16[4,128,3,2,128]{4,3,2,1,0:T(2,128)(2,1)} %bitcast.297), calls=%async_computation | async-start | bytes 1572864 | tf_op jit(solution)/shard_map/all_to_all | solution.py:903
  14.3 87.9 %all-gather.5.cloned.1.call-start = ((), (), s32[]{:S(2)}) async-start(), calls=%async_computation.9 | async-start | bytes 4718592 | tf_op jit(solution)/shard_map/all_gather | solution.py:959
  54.5 47.6 %collective-permute-start.5 = (bf16[512,768]{1,0:T(8,128)(2,1)S(1)}, bf16[512,768]{1,0:T(8,128)(2,1)S(1)}, u32[]{:S(2)}, u32[]{:S(2)}) collective-permute-start(bf16[512,768]{1,0:T(8,128)(2,1)S(1)} %reshape.872.refs_0_), channel_id=1, source_target_pairs={{0,4},{4,0},{1,5},{5,1},{2,6},{6,2},{3,7},{7,3},{8,12},{12,8},{9,1... | collective-permute-start | bytes 2359304 | tf_op jit(solution)/shard_map/ppermute | solution.py:366
  55.2 43.2 %collective-permute-start.7 = (bf16[256,768]{1,0:T(8,128)(2,1)}, bf16[256,768]{1,0:T(8,128)(2,1)S(1)}, u32[]{:S(2)}, u32[]{:S(2)}) collective-permute-start(bf16[256,768]{1,0:T(8,128)(2,1)} %get-tuple-element.433), channel_id=1, source_target_pairs={{0,16},{16,0},{1,17},{17,1},{2,18},{18,2},{3,19},{19,3},{4,20},{20... | collective-permute-start | bytes 1179656 | tf_op jit(solution)/shard_map/ppermute | solution.py:366
  57.2 35.0 %collective-permute-start.6 = (bf16[256,768]{1,0:T(8,128)(2,1)}, bf16[256,768]{1,0:T(8,128)(2,1)S(1)}, u32[]{:S(2)}, u32[]{:S(2)}) collective-permute-start(bf16[256,768]{1,0:T(8,128)(2,1)} %get-tuple-element.434), channel_id=1, source_target_pairs={{0,16},{16,0},{1,17},{17,1},{2,18},{18,2},{3,19},{19,3},{4,20},{20... | collective-permute-start | bytes 1179656 | tf_op jit(solution)/shard_map/ppermute | solution.py:366
  104.8 31.1 %all-to-all-start.2 = ((bf16[4,128,1024]{2,1,0:T(8,128)(2,1)}), bf16[4,128,1024]{2,1,0:T(8,128)(2,1)S(1)}, u32[]{:S(2)}, u32[]{:S(2)}) async-start(bf16[4,128,1024]{2,1,0:T(8,128)(2,1)} %bitcast.296), calls=%async_computation.2 | async-start | bytes 2097152 | tf_op jit(solution)/shard_map/all_to_all | solution.py:903
  110.8 25.2 %collective-permute-start.13 = (bf16[256,512]{1,0:T(8,128)(2,1)S(1)}, bf16[256,512]{1,0:T(8,128)(2,1)S(1)}, u32[]{:S(2)}, u32[]{:S(2)}) collective-permute-start(bf16[256,512]{1,0:T(8,128)(2,1)S(1)} %copy_bitcast_fusion.2), channel_id=1, source_target_pairs={{0,4},{4,0},{1,5},{5,1},{2,6},{6,2},{3,7},{7,3},{8,12},{12,8},{9,1... | collective-permute-start | bytes 786440 | tf_op jit(solution)/shard_map/ppermute | solution.py:366
  111.8 24.2 %collective-permute-start.12 = (bf16[256,512]{1,0:T(8,128)(2,1)S(1)}, bf16[256,512]{1,0:T(8,128)(2,1)S(1)}, u32[]{:S(2)}, u32[]{:S(2)}) collective-permute-start(bf16[256,512]{1,0:T(8,128)(2,1)S(1)} %copy_bitcast_fusion.2), channel_id=1, source_target_pairs={{0,16},{16,0},{1,17},{17,1},{2,18},{18,2},{3,19},{19,3},{4,20},{20... | collective-permute-start | bytes 786440 | tf_op jit(solution)/shard_map/ppermute | solution.py:366
  114.7 21.2 %collective-permute-start.11 = (bf16[256,768]{1,0:T(8,128)(2,1)S(1)}, bf16[256,768]{1,0:T(8,128)(2,1)S(1)}, u32[]{:S(2)}, u32[]{:S(2)}) collective-permute-start(bf16[256,768]{1,0:T(8,128)(2,1)S(1)} %collective-permute-done.7.refs_3_), channel_id=1, source_target_pairs={{0,4},{4,0},{1,5},{5,1},{2,6},{6,2},{3,7},{7,3},{8,12},{12,8},{9,1... | collective-permute-start | bytes 1179656 | tf_op jit(solution)/shard_map/ppermute | solution.py:366
  136.7 29.6 %all-to-all-start.3 = ((bf16[4,1024,128]{2,1,0:T(8,128)(2,1)}), bf16[4,1024,128]{2,1,0:T(8,128)(2,1)S(1)}, u32[]{:S(2)}, u32[]{:S(2)}) async-start(bf16[4,1024,128]{2,1,0:T(8,128)(2,1)} %bitcast.317), calls=%async_computation.3 | async-start | bytes 2097152 | tf_op jit(solution)/shard_map/all_to_all | solution.py:903
  140.2 89.4 %all-gather.7.cloned.1.call-start = ((), (), s32[]{:S(2)}) async-start(), calls=%async_computation.10 | async-start | bytes 4718592 | tf_op jit(solution)/shard_map/all_gather | solution.py:1081
  140.2 25.9 %collective-permute-start.17 = (bf16[256,512]{1,0:T(8,128)(2,1)S(1)}, bf16[256,512]{1,0:T(8,128)(2,1)S(1)}, u32[]{:S(2)}, u32[]{:S(2)}) collective-permute-start(bf16[256,512]{1,0:T(8,128)(2,1)S(1)} %collective-permute-done.12), channel_id=1, source_target_pairs={{0,4},{4,0},{1,5},{5,1},{2,6},{6,2},{3,7},{7,3},{8,12},{12,8},{9,1... | collective-permute-start | bytes 786440 | tf_op jit(solution)/shard_map/ppermute | solution.py:366
  143.9 26.4 %collective-permute-start.19 = (bf16[512,512]{1,0:T(8,128)(2,1)}, bf16[512,512]{1,0:T(8,128)(2,1)}, u32[]{:S(2)}, u32[]{:S(2)}) collective-permute-start(bf16[512,512]{1,0:T(8,128)(2,1)} %slice.255), channel_id=1, source_target_pairs={{0,16},{16,0},{1,17},{17,1},{2,18},{18,2},{3,19},{19,3},{4,20},{20... | collective-permute-start | bytes 1572872 | tf_op jit(solution)/shard_map/ppermute | solution.py:366
  143.9 26.4 %collective-permute-start.18 = (bf16[512,512]{1,0:T(8,128)(2,1)}, bf16[512,512]{1,0:T(8,128)(2,1)}, u32[]{:S(2)}, u32[]{:S(2)}) collective-permute-start(bf16[512,512]{1,0:T(8,128)(2,1)} %slice.255), channel_id=1, source_target_pairs={{0,4},{4,0},{1,5},{5,1},{2,6},{6,2},{3,7},{7,3},{8,12},{12,8},{9,1... | collective-permute-start | bytes 1572872 | tf_op jit(solution)/shard_map/ppermute | solution.py:366
  170.3 116.7 %all-gather.9.cloned.1.call-start = ((), (), s32[]{:S(2)}) async-start(), calls=%async_computation.11 | async-start | bytes 4718592 | tf_op jit(solution)/shard_map/all_gather | solution.py:1118
  177.3 52.3 %collective-permute-start.26 = (bf16[512,512]{1,0:T(8,128)(2,1)}, bf16[512,512]{1,0:T(8,128)(2,1)}, u32[]{:S(2)}, u32[]{:S(2)}) collective-permute-start(bf16[512,512]{1,0:T(8,128)(2,1)} %get-tuple-element.422.refs_4_.refs_12_), channel_id=1, source_target_pairs={{0,16},{16,0},{1,17},{17,1},{2,18},{18,2},{3,19},{19,3},{4,20},{20... | collective-permute-start | bytes 1572872 | tf_op jit(solution)/shard_map/ppermute | solution.py:366
  178.4 51.2 %collective-permute-start.28 = (bf16[512,512]{1,0:T(8,128)(2,1)}, bf16[512,512]{1,0:T(8,128)(2,1)}, u32[]{:S(2)}, u32[]{:S(2)}) collective-permute-start(bf16[512,512]{1,0:T(8,128)(2,1)} %slice.261), channel_id=1, source_target_pairs={{0,4},{4,0},{1,5},{5,1},{2,6},{6,2},{3,7},{7,3},{8,12},{12,8},{9,1... | collective-permute-start | bytes 1572872 | tf_op jit(solution)/shard_map/ppermute | solution.py:366
  188.0 31.3 %collective-permute-start.21 = (bf16[2,64,2048]{2,1,0:T(8,128)(2,1)S(1)}, bf16[2,64,2048]{2,1,0:T(8,128)(2,1)S(1)}, u32[]{:S(2)}, u32[]{:S(2)}) collective-permute-start(bf16[2,64,2048]{2,1,0:T(8,128)(2,1)S(1)} %fusion.29), channel_id=1, source_target_pairs={{0,8},{8,0},{1,9},{9,1},{2,10},{10,2},{3,11},{11,3},{4,12},{12,4},... | collective-permute-start | bytes 1572872 | tf_op jit(solution)/shard_map/ppermute | solution.py:366
  190.8 28.5 %collective-permute-start.22 = (bf16[2,64,2048]{2,1,0:T(8,128)(2,1)}, bf16[2,64,2048]{2,1,0:T(8,128)(2,1)S(1)}, u32[]{:S(2)}, u32[]{:S(2)}) collective-permute-start(bf16[2,64,2048]{2,1,0:T(8,128)(2,1)} %fusion.32), channel_id=1, source_target_pairs={{0,1},{1,0},{2,3},{3,2},{4,5},{5,4},{6,7},{7,6},{8,9},{9,8},{10,11... | collective-permute-start | bytes 1572872 | tf_op jit(solution)/shard_map/ppermute | solution.py:366
  198.5 31.1 %collective-permute-start.27 = (bf16[512,512]{1,0:T(8,128)(2,1)}, bf16[512,512]{1,0:T(8,128)(2,1)}, u32[]{:S(2)}, u32[]{:S(2)}) collective-permute-start(bf16[512,512]{1,0:T(8,128)(2,1)} %collective-permute-done.19.refs_2_.refs_10_), channel_id=1, source_target_pairs={{0,4},{4,0},{1,5},{5,1},{2,6},{6,2},{3,7},{7,3},{8,12},{12,8},{9,1... | collective-permute-start | bytes 1572872 | tf_op jit(solution)/shard_map/ppermute | solution.py:366
  232.9 163.9 %all-gather.11.cloned.1.call-start = ((), (), s32[]{:S(2)}) async-start(), calls=%async_computation.12 | async-start | bytes 4718592 | tf_op jit(solution)/shard_map/all_gather | solution.py:1177
  235.6 21.6 %collective-permute-start.31 = (bf16[512,512]{1,0:T(8,128)(2,1)}, bf16[512,512]{1,0:T(8,128)(2,1)S(1)}, u32[]{:S(2)}, u32[]{:S(2)}) collective-permute-start(bf16[512,512]{1,0:T(8,128)(2,1)} %get-tuple-element.423), channel_id=1, source_target_pairs={{0,4},{4,0},{1,5},{5,1},{2,6},{6,2},{3,7},{7,3},{8,12},{12,8},{9,1... | collective-permute-start | bytes 1572872 | tf_op jit(solution)/shard_map/ppermute | solution.py:366
  236.2 24.5 %collective-permute-start.29 = (bf16[512,512]{1,0:T(8,128)(2,1)}, bf16[512,512]{1,0:T(8,128)(2,1)S(1)}, u32[]{:S(2)}, u32[]{:S(2)}) collective-permute-start(bf16[512,512]{1,0:T(8,128)(2,1)} %get-tuple-element.424), channel_id=1, source_target_pairs={{0,16},{16,0},{1,17},{17,1},{2,18},{18,2},{3,19},{19,3},{4,20},{20... | collective-permute-start | bytes 1572872 | tf_op jit(solution)/shard_map/ppermute | solution.py:366
  261.6 25.5 %collective-permute-start.32 = (bf16[512,512]{1,0:T(8,128)(2,1)S(1)}, bf16[512,512]{1,0:T(8,128)(2,1)S(1)}, u32[]{:S(2)}, u32[]{:S(2)}) collective-permute-start(bf16[512,512]{1,0:T(8,128)(2,1)S(1)} %get-tuple-element.420.refs_4_), channel_id=1, source_target_pairs={{0,16},{16,0},{1,17},{17,1},{2,18},{18,2},{3,19},{19,3},{4,20},{20... | collective-permute-start | bytes 1572872 | tf_op jit(solution)/shard_map/ppermute | solution.py:366
  261.6 25.5 %collective-permute-start.33 = (bf16[512,512]{1,0:T(8,128)(2,1)S(1)}, bf16[512,512]{1,0:T(8,128)(2,1)S(1)}, u32[]{:S(2)}, u32[]{:S(2)}) collective-permute-start(bf16[512,512]{1,0:T(8,128)(2,1)S(1)} %collective-permute-done.29.refs_2_), channel_id=1, source_target_pairs={{0,4},{4,0},{1,5},{5,1},{2,6},{6,2},{3,7},{7,3},{8,12},{12,8},{9,1... | collective-permute-start | bytes 1572872 | tf_op jit(solution)/shard_map/ppermute | solution.py:366
  320.2 24.8 %collective-permute-start.38 = (bf16[1024,512]{1,0:T(8,128)(2,1)S(1)}, bf16[1024,512]{1,0:T(8,128)(2,1)S(1)}, u32[]{:S(2)}, u32[]{:S(2)}) collective-permute-start(bf16[1024,512]{1,0:T(8,128)(2,1)S(1)} %convolution_convert_fusion.5), channel_id=1, source_target_pairs={{0,4},{4,0},{1,5},{5,1},{2,6},{6,2},{3,7},{7,3},{8,12},{12,8},{9,1... | collective-permute-start | bytes 3145736 | tf_op jit(solution)/shard_map/ppermute | solution.py:366
  323.8 21.2 %collective-permute-start.36 = (bf16[2,64,2048]{2,1,0:T(8,128)(2,1)S(1)}, bf16[2,64,2048]{2,1,0:T(8,128)(2,1)S(1)}, u32[]{:S(2)}, u32[]{:S(2)}) collective-permute-start(bf16[2,64,2048]{2,1,0:T(8,128)(2,1)S(1)} %fusion.30), channel_id=1, source_target_pairs={{0,8},{8,0},{1,9},{9,1},{2,10},{10,2},{3,11},{11,3},{4,12},{12,4},... | collective-permute-start | bytes 1572872 | tf_op jit(solution)/shard_map/ppermute | solution.py:366
  355.8 147.4 %reduce-scatter.2.cloned.1.call-start = ((), (), s32[]{:S(2)}) async-start(), calls=%async_computation.13 | async-start | bytes 4718592 | tf_op jit(solution)/shard_map/reduce_scatter | solution.py:1200
  360.1 23.0 %collective-permute-start.41 = (bf16[512,1024]{1,0:T(8,128)(2,1)}, bf16[512,1024]{1,0:T(8,128)(2,1)}, u32[]{:S(2)}, u32[]{:S(2)}) collective-permute-start(bf16[512,1024]{1,0:T(8,128)(2,1)} %convolution_convert_fusion.3), channel_id=1, source_target_pairs={{0,4},{4,0},{1,5},{5,1},{2,6},{6,2},{3,7},{7,3},{8,12},{12,8},{9,1... | collective-permute-start | bytes 3145736 | tf_op jit(solution)/shard_map/ppermute | solution.py:366
  373.3 23.5 %collective-permute-start.42 = (bf16[512,512]{1,0:T(8,128)(2,1)S(1)}, bf16[512,512]{1,0:T(8,128)(2,1)}, u32[]{:S(2)}, u32[]{:S(2)}) collective-permute-start(bf16[512,512]{1,0:T(8,128)(2,1)S(1)} %slice.280), channel_id=1, source_target_pairs={{0,16},{16,0},{1,17},{17,1},{2,18},{18,2},{3,19},{19,3},{4,20},{20... | collective-permute-start | bytes 1572872 | tf_op jit(solution)/shard_map/ppermute | solution.py:366
  396.8 29.4 %collective-permute-start.43 = (bf16[1024,512]{1,0:T(8,128)(2,1)}, bf16[1024,512]{1,0:T(8,128)(2,1)}, u32[]{:S(2)}, u32[]{:S(2)}) collective-permute-start(bf16[1024,512]{1,0:T(8,128)(2,1)} %convolution_convert_fusion.4), channel_id=1, source_target_pairs={{0,4},{4,0},{1,5},{5,1},{2,6},{6,2},{3,7},{7,3},{8,12},{12,8},{9,1... | collective-permute-start | bytes 3145736 | tf_op jit(solution)/shard_map/ppermute | solution.py:366
  404.3 26.6 %collective-permute-start.45 = (bf16[2,256,512]{2,1,0:T(8,128)(2,1)}, bf16[2,256,512]{2,1,0:T(8,128)(2,1)}, u32[]{:S(2)}, u32[]{:S(2)}) collective-permute-start(bf16[2,256,512]{2,1,0:T(8,128)(2,1)} %pad_maximum_fusion.6), channel_id=1, source_target_pairs={{0,4},{4,0},{1,5},{5,1},{2,6},{6,2},{3,7},{7,3},{8,12},{12,8},{9,1... | collective-permute-start | bytes 1572872 | tf_op jit(solution)/shard_map/ppermute | solution.py:366
  405.2 25.8 %collective-permute-start.44 = (bf16[512,512]{1,0:T(8,128)(2,1)}, bf16[512,512]{1,0:T(8,128)(2,1)}, u32[]{:S(2)}, u32[]{:S(2)}) collective-permute-start(bf16[512,512]{1,0:T(8,128)(2,1)} %slice.281), channel_id=1, source_target_pairs={{0,16},{16,0},{1,17},{17,1},{2,18},{18,2},{3,19},{19,3},{4,20},{20... | collective-permute-start | bytes 1572872 | tf_op jit(solution)/shard_map/ppermute | solution.py:366
  447.8 26.0 %collective-permute-start.49 = (bf16[512,768]{1,0:T(8,128)(2,1)}, bf16[512,768]{1,0:T(8,128)(2,1)}, u32[]{:S(2)}, u32[]{:S(2)}) collective-permute-start(bf16[512,768]{1,0:T(8,128)(2,1)} %convolution_convert_fusion.7), channel_id=1, source_target_pairs={{0,4},{4,0},{1,5},{5,1},{2,6},{6,2},{3,7},{7,3},{8,12},{12,8},{9,1... | collective-permute-start | bytes 2359304 | tf_op jit(solution)/shard_map/ppermute | solution.py:366
  449.5 76.2 %collective-permute-start.52 = (bf16[512,1024]{1,0:T(8,128)(2,1)}, bf16[512,1024]{1,0:T(8,128)(2,1)}, u32[]{:S(2)}, u32[]{:S(2)}) collective-permute-start(bf16[512,1024]{1,0:T(8,128)(2,1)} %add_convert_fusion.2), channel_id=1, source_target_pairs={{0,16},{16,0},{1,17},{17,1},{2,18},{18,2},{3,19},{19,3},{4,20},{20... | collective-permute-start | bytes 3145736 | tf_op jit(solution)/shard_map/ppermute | solution.py:366
  463.0 40.2 %collective-permute-start.47 = (bf16[2,64,2048]{2,1,0:T(8,128)(2,1)S(1)}, bf16[2,64,2048]{2,1,0:T(8,128)(2,1)}, u32[]{:S(2)}, u32[]{:S(2)}) collective-permute-start(bf16[2,64,2048]{2,1,0:T(8,128)(2,1)S(1)} %fusion.31), channel_id=1, source_target_pairs={{0,8},{8,0},{1,9},{9,1},{2,10},{10,2},{3,11},{11,3},{4,12},{12,4},... | collective-permute-start | bytes 1572872 | tf_op jit(solution)/shard_map/ppermute | solution.py:366
  463.8 39.4 %collective-permute-start.48 = (bf16[2,64,2048]{2,1,0:T(8,128)(2,1)S(1)}, bf16[2,64,2048]{2,1,0:T(8,128)(2,1)}, u32[]{:S(2)}, u32[]{:S(2)}) collective-permute-start(bf16[2,64,2048]{2,1,0:T(8,128)(2,1)S(1)} %fusion.34), channel_id=1, source_target_pairs={{0,1},{1,0},{2,3},{3,2},{4,5},{5,4},{6,7},{7,6},{8,9},{9,8},{10,11... | collective-permute-start | bytes 1572872 | tf_op jit(solution)/shard_map/ppermute | solution.py:366
  506.0 24.4 %collective-permute-start.53 = (bf16[256,512]{1,0:T(8,128)(2,1)}, bf16[256,512]{1,0:T(8,128)(2,1)S(1)}, u32[]{:S(2)}, u32[]{:S(2)}) collective-permute-start(bf16[256,512]{1,0:T(8,128)(2,1)} %fusion.1), channel_id=1, source_target_pairs={{0,16},{16,0},{1,17},{17,1},{2,18},{18,2},{3,19},{19,3},{4,20},{20... | collective-permute-start | bytes 786440 | tf_op jit(solution)/shard_map/ppermute | solution.py:366
  509.5 69.6 %collective-permute-start.58 = (bf16[512,768]{1,0:T(8,128)(2,1)}, bf16[512,768]{1,0:T(8,128)(2,1)}, u32[]{:S(2)}, u32[]{:S(2)}) collective-permute-start(bf16[512,768]{1,0:T(8,128)(2,1)} %convolution_convert_fusion.6), channel_id=1, source_target_pairs={{0,4},{4,0},{1,5},{5,1},{2,6},{6,2},{3,7},{7,3},{8,12},{12,8},{9,1... | collective-permute-start | bytes 2359304 | tf_op jit(solution)/shard_map/ppermute | solution.py:366
  515.5 39.4 %collective-permute-start.57 = (bf16[512,1024]{1,0:T(8,128)(2,1)}, bf16[512,1024]{1,0:T(8,128)(2,1)}, u32[]{:S(2)}, u32[]{:S(2)}) collective-permute-start(bf16[512,1024]{1,0:T(8,128)(2,1)} %convolution_convert_fusion.2), channel_id=1, source_target_pairs={{0,4},{4,0},{1,5},{5,1},{2,6},{6,2},{3,7},{7,3},{8,12},{12,8},{9,1... | collective-permute-start | bytes 3145736 | tf_op jit(solution)/shard_map/ppermute | solution.py:366
  538.3 22.4 %all-to-all-start.5 = ((bf16[4,1024,128]{2,1,0:T(8,128)(2,1)}), bf16[4,1024,128]{2,1,0:T(8,128)(2,1)S(1)}, u32[]{:S(2)}, u32[]{:S(2)}) async-start(bf16[4,1024,128]{2,1,0:T(8,128)(2,1)} %bitcast.305), calls=%async_computation.6 | async-start | bytes 2097152 | tf_op jit(solution)/shard_map/all_to_all | solution.py:903
  545.5 27.2 %collective-permute-start.56 = (bf16[32,2048]{1,0:T(8,128)(2,1)}, bf16[32,2048]{1,0:T(8,128)(2,1)}, u32[]{:S(2)}, u32[]{:S(2)}) collective-permute-start(bf16[32,2048]{1,0:T(8,128)(2,1)} %get-tuple-element.444), channel_id=1, source_target_pairs={{0,20},{4,16},{16,4},{20,0},{1,21},{5,17},{17,5},{21,1},{2,22},{6,... | collective-permute-start | bytes 393224 | tf_op jit(solution)/shard_map/ppermute | solution.py:916
  545.6 33.4 %collective-permute-start.55 = (bf16[32,2048]{1,0:T(8,128)(2,1)}, bf16[32,2048]{1,0:T(8,128)(2,1)}, u32[]{:S(2)}, u32[]{:S(2)}) collective-permute-start(bf16[32,2048]{1,0:T(8,128)(2,1)} %get-tuple-element.445), channel_id=1, source_target_pairs={{0,16},{16,0},{1,17},{17,1},{2,18},{18,2},{3,19},{19,3},{4,20},{20... | collective-permute-start | bytes 393224 | tf_op jit(solution)/shard_map/ppermute | solution.py:366
  549.0 30.0 %collective-permute-start.54 = (bf16[32,2048]{1,0:T(8,128)(2,1)}, bf16[32,2048]{1,0:T(8,128)(2,1)}, u32[]{:S(2)}, u32[]{:S(2)}) collective-permute-start(bf16[32,2048]{1,0:T(8,128)(2,1)} %get-tuple-element.446), channel_id=1, source_target_pairs={{0,4},{4,0},{1,5},{5,1},{2,6},{6,2},{3,7},{7,3},{8,12},{12,8},{9,1... | collective-permute-start | bytes 393224 | tf_op jit(solution)/shard_map/ppermute | solution.py:366
  554.8 40.5 %collective-permute-start.59 = (bf16[512,768]{1,0:T(8,128)(2,1)}, bf16[512,768]{1,0:T(8,128)(2,1)S(1)}, u32[]{:S(2)}, u32[]{:S(2)}) collective-permute-start(bf16[512,768]{1,0:T(8,128)(2,1)} %add_convert_fusion.5), channel_id=1, source_target_pairs={{0,16},{16,0},{1,17},{17,1},{2,18},{18,2},{3,19},{19,3},{4,20},{20... | collective-permute-start | bytes 2359304 | tf_op jit(solution)/shard_map/ppermute | solution.py:366
  560.8 36.1 %all-to-all-start.4 = ((bf16[4,128,1024]{2,1,0:T(8,128)(2,1)}), bf16[4,128,1024]{2,1,0:T(8,128)(2,1)S(1)}, u32[]{:S(2)}, u32[]{:S(2)}) async-start(bf16[4,128,1024]{2,1,0:T(8,128)(2,1)} %bitcast.97), calls=%async_computation.5 | async-start | bytes 2097152 | tf_op jit(solution)/shard_map/all_to_all | solution.py:903
  599.3 23.2 %all-to-all-start.6 = ((bf16[4,256,128]{2,1,0:T(8,128)(2,1)}), bf16[4,256,128]{2,1,0:T(8,128)(2,1)S(1)}, u32[]{:S(2)}, u32[]{:S(2)}) async-start(bf16[4,256,128]{2,1,0:T(8,128)(2,1)} %bitcast_bitcast_fusion.2), calls=%async_computation.7 | async-start | bytes 524288 | tf_op jit(solution)/shard_map/all_to_all | solution.py:903
  625.4 21.3 %all-to-all-start.7 = ((bf16[4,128,768]{2,1,0:T(8,128)(2,1)}), bf16[4,128,768]{2,1,0:T(8,128)(2,1)S(1)}, u32[]{:S(2)}, u32[]{:S(2)}) async-start(bf16[4,128,768]{2,1,0:T(8,128)(2,1)} %bitcast.126), calls=%async_computation.8 | async-start | bytes 1572864 | tf_op jit(solution)/shard_map/all_to_all | solution.py:903
  (134 other events, 1655.5 us)
Sparse Core Ops, SparseCore 0:
  42.5 46.2 all-gather.4
  170.4 49.8 all-gather.6
  233.0 41.0 all-gather.8
  356.0 37.7 all-gather.10
  396.9 104.0 reduce-scatter.1

commit v4 on v3

--- a/solution.py
+++ b/solution.py
@@ -409,7 +409,7 @@
 
 def reduce_rows(value, zh, zl, x, c):
     value = value.reshape(2, 2, 2, 2, -1)
-    for axis, at, bit in (("zh", 0, zh), ("zl", 0, zl), ("x", 0, x), ("c", 0, c)):
+    for axis, at, bit in (("c", 3, c), ("zl", 1, zl), ("x", 1, x), ("zh", 0, zh)):
         keep = lax.dynamic_index_in_dim(value, bit, at, keepdims=False)
         send = lax.dynamic_index_in_dim(value, 1 - bit, at, keepdims=False)
         value = keep + swap(send, axis)
@@ -417,6 +417,7 @@
 
 
 BLOCK_Q = 256
+BLOCK_A = 512
 NEVER = -1e30
 
 
@@ -798,7 +799,7 @@
     dv_sum[...] += dot_to(probs.astype(LOW), grad, ((1,), (0,)))
     dk_sum[...] += dot_to(score_grad, query, ((1,), (0,)))
     dq = dot_to(score_grad, key, ((0,), (0,)))
-    at = pl.ds(pl.multiple_of(step * BLOCK_Q, BLOCK_Q), BLOCK_Q)
+    at = pl.ds(pl.multiple_of(step * BLOCK_A, BLOCK_A), BLOCK_A)
     col = pl.multiple_of(head * HEAD_DIM, HEAD_DIM)
     dq = turn_back(dq, cos_ref[at, :], sin_ref[at, :])
     out_ref[at, pl.ds(col, HEAD_DIM)] = dq.astype(LOW)
@@ -816,18 +817,18 @@
     n = heads
     return pl.pallas_call(
         attend_kernel,
-        grid=(heads, length // BLOCK_Q),
+        grid=(heads, length // BLOCK_A),
         in_specs=[
-            pl.BlockSpec((BLOCK_Q, d), lambda h, i: (i, h)),
+            pl.BlockSpec((BLOCK_A, d), lambda h, i: (i, h)),
             pl.BlockSpec((length, d), lambda h, i: (0, n + h)),
             pl.BlockSpec((length, d), lambda h, i: (0, 2 * n + h)),
             pl.BlockSpec((length, 1), lambda h, i: (0, 0)),
-            pl.BlockSpec((2, BLOCK_Q), lambda h, i: (0, i)),
-            pl.BlockSpec((1, BLOCK_Q, 1), lambda h, i: (h, i, 0)),
+            pl.BlockSpec((2, BLOCK_A), lambda h, i: (0, i)),
+            pl.BlockSpec((1, BLOCK_A, 1), lambda h, i: (h, i, 0)),
         ],
         out_specs=[
-            pl.BlockSpec((BLOCK_Q, d), lambda h, i: (i, h)),
-            pl.BlockSpec((1, 1, BLOCK_Q), lambda h, i: (h, 0, i)),
+            pl.BlockSpec((BLOCK_A, d), lambda h, i: (i, h)),
+            pl.BlockSpec((1, 1, BLOCK_A), lambda h, i: (h, 0, i)),
         ],
         out_shape=[
             jax.ShapeDtypeStruct((length, heads * d), LOW),
@@ -843,17 +844,17 @@
     n = heads
     return pl.pallas_call(
         attend_back_kernel,
-        grid=(heads, length // BLOCK_Q),
+        grid=(heads, length // BLOCK_A),
         in_specs=[
-            pl.BlockSpec((BLOCK_Q, d), lambda h, i: (i, h)),
+            pl.BlockSpec((BLOCK_A, d), lambda h, i: (i, h)),
             pl.BlockSpec((length, d), lambda h, i: (0, n + h)),
             pl.BlockSpec((length, d), lambda h, i: (0, 2 * n + h)),
-            pl.BlockSpec((BLOCK_Q, width), lambda h, i: (i, 0)),
+            pl.BlockSpec((BLOCK_A, width), lambda h, i: (i, 0)),
             pl.BlockSpec((d, width), lambda h, i: (h, 0)),
-            pl.BlockSpec((1, BLOCK_Q, 1), lambda h, i: (h, i, 0)),
-            pl.BlockSpec((1, 1, BLOCK_Q), lambda h, i: (h, 0, i)),
+            pl.BlockSpec((1, BLOCK_A, 1), lambda h, i: (h, i, 0)),
+            pl.BlockSpec((1, 1, BLOCK_A), lambda h, i: (h, 0, i)),
             pl.BlockSpec((length, 1), lambda h, i: (0, 0)),
-            pl.BlockSpec((2, BLOCK_Q), lambda h, i: (0, i)),
+            pl.BlockSpec((2, BLOCK_A), lambda h, i: (0, i)),
             pl.BlockSpec((length, d), lambda h, i: (0, 0)),
             pl.BlockSpec((length, d), lambda h, i: (0, 0)),
         ],
@@ -926,10 +927,9 @@
     core = c.reshape(1).astype(jnp.int32)
     e_in = exchange(jnp.moveaxis(in_weight.reshape(block, 3, 4, heads, head_dim), 2, 0))
     e_in = e_in.reshape(4 * block, 3 * inner)
-    token_pieces = to_batch(tokens)
 
     def rows_of_block(value):
-        value = value.astype(WIDE).reshape(-1)
+        value = value.astype(LOW).reshape(-1)
         return jnp.pad(value, (0, -value.shape[0] % block)).reshape(-1, block)
 
     small = jnp.concatenate(
@@ -952,11 +952,21 @@
         axis=0,
     )
     n_small = small.shape[0]
-    small = small[None]
-    small = gather_over(small, ("zh", "x"), (zh, x))
-    *token_pieces, small, e_in = tie(*token_pieces, small, e_in)
-    tokens_own = jnp.concatenate(token_pieces, axis=0)
-    tokens_all = lax.all_gather(tokens_own, GROUP, axis=0, tiled=True)
+    small_rows = -(-n_small * block // width)
+    small = jnp.pad(small.reshape(-1), (0, small_rows * width - n_small * block))
+    small = small.reshape(small_rows, width)
+    mine_of = lax.dynamic_slice_in_dim(tokens, y * half, half, 1)
+    token_pieces = across(
+        [
+            jnp.concatenate(
+                [lax.dynamic_index_in_dim(mine_of, batch ^ k, 0, keepdims=False), small], axis=0
+            )
+            for k in range(4)
+        ]
+    )
+    small = jnp.stack([p[half:].reshape(-1)[: n_small * block] for p in token_pieces])
+    small = gather_over(small[None], ("c", "zl"), (c, zl))
+    tokens_own = jnp.concatenate([p[:half] for p in token_pieces], axis=0)
 
     index = jnp.arange(length, dtype=jnp.int32).reshape(2, 2, 2, 2, 2, half)
 
@@ -966,15 +976,6 @@
         value = jnp.transpose(value, lead + tuple(at + i for i in (3, 1, 4, 0, 2, 5)))
         return value.reshape(value.shape[: value.ndim - 6] + (length,))
 
-    cut = e_in.shape[0] // 2
-    in_z1 = swap(e_in[:cut], "zh")
-    in_z2 = swap(e_in[cut:], "zh")
-    in_x = swap(e_in, "x")
-    in_zx1 = swap(in_z1, "x")
-    small = gather_over(small, ("c", "zl"), (c, zl)).reshape(2, 2, 2, 2, -1)
-    small_all = jnp.transpose(small, (3, 0, 2, 1, 4)).reshape(16, n_small * block)
-    e_out = exchange(out_weight.reshape(4, inner, block))
-    e_out = jnp.moveaxis(e_out, 0, 1).reshape(inner, 4 * block)
     positions = by_place(index) ^ (zh * (8 * tok_dev) + x * (2 * tok_dev))
     ends = jnp.cumsum(lax.dynamic_index_in_dim(doc_lengths, batch, 0, keepdims=False))
     first = jnp.max(jnp.where(ends[:, None] <= positions[None, :], ends[:, None], 0), axis=0)
@@ -983,21 +984,32 @@
     cosine, sine = rotary_tables(positions)
     lane = jnp.arange(HEAD_DIM)[None, :]
     signed = jnp.where(lane < HEAD_DIM // 2, -sine, sine)
+    tokens_own, small, e_in, cosine, sine, signed, span, key_place = tie(
+        tokens_own, small, e_in, cosine, sine, signed, span, key_place
+    )
+
+    tokens_all = lax.all_gather(tokens_own, GROUP, axis=0, tiled=True)
+    in_z = swap(e_in, "zh")
+    in_x = swap(e_in, "x")
+    e_out = exchange(out_weight.reshape(4, inner, block))
+    e_out = jnp.moveaxis(e_out, 0, 1).reshape(inner, 4 * block)
+    small_own = small.reshape(2, 2, 2, 2, n_small * block).astype(WIDE)
+    small_own = jnp.transpose(small_own, (2, 0, 3, 1, 4)).reshape(16, n_small * block)
     n_vec = 6 + 2 * GROUPS
     rows_of = jnp.arange(16) ^ (zh * 8 + x * 2)
     pick = (rows_of[:, None] == jnp.arange(16)[None, :]).astype(WIDE)
-    small_own = jnp.dot(pick, small_all, precision=HIGHEST)
+    small_all = jnp.dot(pick, small_own[:, n_vec * block :], precision=HIGHEST)
     vectors_f = small_own[:, : n_vec * block].reshape(2, 2, 2, 2, n_vec, block)
     vectors_f = jnp.transpose(vectors_f, (4, 0, 2, 1, 3, 5)).reshape(n_vec, width)
     router = vectors_f[6:].astype(LOW)
-    at = n_vec * block
     size = up_bias.size
-    bias_up = small_all[:, at : at + size].reshape((16,) + up_bias.shape)
+    bias_up = small_all[:, :size].reshape((16,) + up_bias.shape)
     bias_up = jnp.moveaxis(bias_up, 0, 1).reshape(4, units)
     bias_up = lax.dynamic_index_in_dim(bias_up, part, 0, keepdims=True)
-    at += size
+    at = size
     size = 2 * micro * tok_dev
-    widths = small_own[:, at : at + size].reshape(16, 2, micro, tok_dev)
+    widths = small_own[:, n_vec * block + at : n_vec * block + at + size]
+    widths = widths.reshape(16, 2, micro, tok_dev)
     widths = lax.dynamic_index_in_dim(widths, batch, 2, keepdims=False).astype(jnp.int32)
     widths = jnp.swapaxes(widths, 0, 1).reshape(2, 2, 2, 2, 2, 2, half)
     at += size
@@ -1012,45 +1024,43 @@
     unit_group = (y * 4 + part) * units // (FF // GROUPS)
     unit_active = (unit_group < units_row).astype(WIDE)[:, None]
     (
-        tokens_all, in_x, in_z1, in_z2, in_zx1, e_out, cotangent, up_weight, down_weight,
-        vectors_f, router, bias_in, bias_up, head_active, unit_active,
-        cosine, sine, signed, span, key_place,
+        in_z, in_x, e_out, vectors_f, router, bias_in, bias_up, head_active, unit_active,
+        cotangent, up_weight,
     ) = tie(
-        tokens_all, in_x, in_z1, in_z2, in_zx1, e_out, cotangent, up_weight, down_weight,
-        vectors_f, router, bias_in, bias_up, head_active, unit_active,
-        cosine, sine, signed, span, key_place,
+        in_z, in_x, e_out, vectors_f, router, bias_in, bias_up, head_active, unit_active,
+        cotangent, up_weight,
     )
     gain_one, shift_one, gain_two, shift_two, bias_out, bias_down = (
         vectors_f[i : i + 1] for i in range(6)
     )
 
-    in_zx2 = swap(in_z2, "x")
+    in_zx = swap(in_z, "x")
     out_z = swap(e_out, "zh")
-    out_x = swap(e_out, "x")
+    cotangent_pieces = to_batch(cotangent)
     e_up = exchange(jnp.moveaxis(up_weight.reshape(block, 4, units), 1, 0))
     e_up = e_up.reshape(4 * block, units)
-    cotangent_pieces = to_batch(cotangent)
     normed_low, logits = norm_rows(bits, tokens_all, gain_one, shift_one, router)
-    normed_low, in_zx2, out_z, out_x, e_up, down_weight, logits, *cotangent_pieces = tie(
-        normed_low, in_zx2, out_z, out_x, e_up, down_weight, logits, *cotangent_pieces
+    normed_low, in_zx, out_z, e_up, down_weight, logits, e_out, *cotangent_pieces = tie(
+        normed_low, in_zx, out_z, e_up, down_weight, logits, e_out, *cotangent_pieces
     )
     cotangent_own = jnp.concatenate(cotangent_pieces, axis=0)
-
+    cotangent_all = lax.all_gather(cotangent_own, GROUP, axis=0, tiled=True)
     def mine(value):
         return lax.dynamic_slice_in_dim(value, place * own, own, 0)
 
     cut_units = units // 2
     out_zx = swap(out_z, "x")
+    out_x = swap(e_out, "x")
     up_x1 = swap(e_up[:, :cut_units], "x")
     up_z1 = swap(e_up[:, :cut_units], "zh")
     e_down = exchange(down_weight.reshape(4, units, block))
     e_down = jnp.moveaxis(e_down, 0, 1).reshape(units, 4 * block)
-    w_in = (e_in, in_x, in_z1, in_z2, in_zx1, in_zx2)
+    w_in = (e_in, in_x, in_z, in_zx)
     qkv = qkv_rows(normed_low, w_in, bias_in, cosine, signed)
     mixed, lse = attend(qkv, key_place, span, head_active, heads)
     w_out = jnp.concatenate([e_out, out_x, out_z, out_zx], axis=1)
-    mixed, w_out, e_up, e_down, up_x1, up_z1, cotangent_own, tokens_own, logits = tie(
-        mixed, w_out, e_up, e_down, up_x1, up_z1, cotangent_own, tokens_own, logits
+    mixed, w_out, e_up, up_x1, up_z1, tokens_own, logits = tie(
+        mixed, w_out, e_up, up_x1, up_z1, tokens_own, logits
     )
 
     part_own = own // 2
@@ -1078,7 +1088,6 @@
 
     attn_here, attn_away = halves(mixed)
     attn_away = dot_to(attn_away, w_out, ((1,), (0,))).astype(LOW)
-    cotangent_all = lax.all_gather(cotangent_own, GROUP, axis=0, tiled=True)
     attn_away, attn_here, tokens_own, cotangent_own, logits = tie(
         attn_away, attn_here, tokens_own, cotangent_own, logits
     )
@@ -1094,17 +1103,20 @@
     attn_gate = GROUPS * jnp.sum(attn_prob * attn_pick, axis=-1, keepdims=True)
     ffn_gate = GROUPS * jnp.sum(ffn_prob * ffn_pick, axis=-1, keepdims=True)
     attn_total = dot_to(attn_here, w_out, ((1,), (0,))) + attn_got.astype(WIDE)
-    attn_total, attn_gate, ffn_gate, tokens_own, cotangent_own = tie(
-        attn_total, attn_gate, ffn_gate, tokens_own, cotangent_own
-    )
-    attn_parts = group_second(attn_total)
+    attn_total, attn_gate, ffn_gate, tokens_own, cotangent_own, e_down = tie(
+        attn_total, attn_gate, ffn_gate, tokens_own, cotangent_own, e_down
+    )
+    attn_total = attn_total.reshape(2, 2, own, width)
+    attn_keep, attn_send = keep_and_send(attn_total, y, 1)
+    attn_got = swap(attn_send.astype(LOW), "y")
     rows, upstream = own_rows(bits, tokens_own, cotangent_own)
-    *attn_parts, rows, upstream, up_x2 = tie(*attn_parts, rows, upstream, up_x2)
-    attn_sum = group_third(*attn_parts)
+    attn_keep, attn_got, rows, upstream, up_x2, up_z2, cotangent_all = tie(
+        attn_keep, attn_got, rows, upstream, up_x2, up_z2, cotangent_all
+    )
+    attn_keep, attn_send = keep_and_send(attn_keep + attn_got.astype(WIDE), zl, 0)
+    attn_sum = attn_keep + swap(attn_send.astype(LOW), "zl").astype(WIDE)
     down_x1 = swap(e_down[:cut_units], "x")
-    attn_sum, cotangent_all, up_z2, up_zx1, down_x1, e_down = tie(
-        attn_sum, cotangent_all, up_z2, up_zx1, down_x1, e_down
-    )
+    attn_sum, down_x1, e_down = tie(attn_sum, down_x1, e_down)
 
     attn_branch = attn_sum + bias_out
     attn_gate_own = mine(attn_gate)
@@ -1125,7 +1137,7 @@
     )
     down_z2 = swap(e_down[cut_units:], "zh")
     down_zx1 = swap(down_z1, "x")
-    normed_two_low, down_z2, down_zx1 = tie(normed_two_low, down_z2, down_zx1)
+    normed_two_low, down_z2, down_zx1, up_zx1 = tie(normed_two_low, down_z2, down_zx1, up_zx1)
 
     def columns(value, k):
         return value[:, k * 4 * block : (k + 1) * 4 * block]
@@ -1136,6 +1148,10 @@
         (e_up[:, cut_units:], up_x2, up_z2, up_zx2),
     )
     relu_part, hidden = hidden_rows(normed_two_low, unit_active, bias_up, w_up)
+
+    def down_piece(k):
+        return dot_to(hidden, columns(down_grad, k), ((0,), (0,)))
+
     relu_part, hidden, down_zx2 = tie(relu_part, hidden, down_zx2)
     w_down = (
         (e_down[:cut_units], down_x1, down_z1, down_zx1),
@@ -1145,28 +1161,22 @@
     two_away, two_here = two_part[: length // 2], two_part[length // 2 :]
     two_got = swap(two_away, "c")
 
-    def down_piece(k):
-        return dot_to(hidden, columns(down_grad, k), ((0,), (0,)))
-
     def up_piece(k):
         return dot_to(columns(normed_two_low, k), up_grad, ((0,), (0,)))
 
-    down_send3 = down_piece(3).astype(LOW)
-    down_got3 = swap(down_send3, "x")
+    down_got3 = swap(down_piece(3).astype(LOW), "x")
     two_total = two_here.astype(WIDE) + two_got.astype(WIDE)
-    two_total, hidden, up_grad, down_send3 = tie(two_total, hidden, up_grad, down_send3)
+    two_total, hidden, up_grad = tie(two_total, hidden, up_grad)
     two_parts = group_second(two_total)
     up_send3 = up_piece(3).astype(LOW)
     down_send1 = down_piece(1).astype(LOW)
-    *two_parts, down_got3, down_send1, up_send3, up_grad = tie(
-        *two_parts, down_got3, down_send1, up_send3, up_grad
-    )
+    *two_parts, down_send1, up_send3, up_grad = tie(*two_parts, down_send1, up_send3, up_grad)
     normed_two_grad = group_third(*two_parts)
     up_got3 = swap(up_send3, "x")
+    normed_two_grad, hidden, down_grad, up_grad, down_got3 = tie(
+        normed_two_grad, hidden, down_grad, up_grad, down_got3
+    )
     down_send2 = (down_piece(2) + down_got3.astype(WIDE)).astype(LOW)
-    normed_two_grad, down_send2, hidden, down_grad, up_grad = tie(
-        normed_two_grad, down_send2, hidden, down_grad, up_grad
-    )
 
     resid_grad = upstream + norm_backward(normed_two_grad, scaled_two, inverse_two, gain_two)
     gated_attn = attn_gate_own * resid_grad

time: 666 us -> 663 us (level)
  waiting for transfers between devices: 246 us -> 222 us
  starting transfers between devices: 103 us -> 118 us
  local copies, waits for them, and re-layouts: 76.6 us -> 85.4 us
    ppermute x66 -> x60, waiting for transfers between devices: 232 us -> 197 us  [swap(): return lax.ppermute(value, axis, [(0, 1), (1, 0)])]
    all_gather x1, starting transfers between devices: 0.51 us -> 11.4 us  [grouped(): normed_two_low = lax.all_gather(normed_two_low, GROUP, axis=0, tiled=True)]
    ppermute x66 -> x60, starting transfers between devices: 66.4 us -> 72 us  [swap(): return lax.ppermute(value, axis, [(0, 1), (1, 0)])]
    unnamed x212 -> x170, local copies, waits for them, and re-layouts: 18.8 us -> 14.4 us
  transfers between devices with their start and end apart: 83 -> 77, of which waited for: 37 -> 34; matrix products, arithmetic and copies ran while one was open for 25% -> 26% of each run, Pallas kernels for 13% -> 12%
where the time goes in v4:
time: 663 us; the launch traced here: 653 us
  waiting for transfers between devices  222 us (33%)
  starting transfers between devices  118 us (18%)
  Pallas kernels  92.3 us (14%)
  local copies, waits for them, and re-layouts  85.4 us (13%)
  matrix products  61.9 us (9%)
  other arithmetic  58 us (9%)
  between operations  15.7 us (2%)
    ppermute x60, waiting for transfers between devices, swap(): return lax.ppermute(value, axis, [(0, 1), (1, 0)])  197 us
    ppermute x60, starting transfers between devices, swap(): return lax.ppermute(value, axis, [(0, 1), (1, 0)])  72 us
    dot_general x20, matrix products, dot_to(): lax.dot_general(left, right, (dims, ((), ())), preferred_element_type=WIDE)  57.7 us
    all_to_all x8, starting transfers between devices, exchange(): return lax.all_to_all(value, ('zl', 'c'), 0, 0, tiled=True)  30.5 us
    pallas_call x1, Pallas kernels, attend_back(): pl.pallas_call(attend_back_kernel, grid=(heads, length // BLOCK_A), in_sp...  17.3 us
    pallas_call x1, Pallas kernels, ffn_rows(): pl.pallas_call(functools.partial(ffn_kernel, tuple((len(g) for g in down_...  15.3 us
    unnamed x170, local copies, waits for them, and re-layouts  14.4 us
  transfers between devices with their start and end apart: 77, of which 34 were waited for; matrix products, arithmetic and copies ran while one was open for 26% of the time, Pallas kernels for 12%

profile of v4, /device:TPU:0, one launch (start us, length us, event | category | flops | bytes accessed | tf_op | source)
XLA Modules:
  0.0 652.7 jit_solution(12910466690010867274)
XLA Ops:
  20.3 3.5 all-to-all-start
  27.6 3.5 collective-permute-done.1
  36.6 5.7 collective-permute-done.4
  42.8 3.4 all-to-all-start.1
  46.8 5.4 all-to-all-done.1
  81.0 9.4 %collective-permute-done.5.refs_2_ = bf16[512,768]{1,0:T(8,128)(2,1)S(1)} collective-permute-done((bf16[512,768]{1,0:T(8,128)(2,1)S(1)}, bf16[512,768]{1,0:T(8,128)(2,1)S(1)}, u32[]{:S(2)}, u32[]{:S(2)}) %collective-permute-start.5) | collective-permute-done | bytes 786464 | tf_op jit(solution)/shard_map/ppermute | solution.py:366
  91.8 3.5 all-to-all-start.2
  103.7 7.8 %norm_rows.1 = (bf16[1024,2048]{1,0:T(8,128)(2,1)}, f32[1024,8]{1,0:T(8,128)}) custom-call(s32[2]{0:T(128)} %pad_add_fusion.1.bits_ref, bf16[1024,2048]{1,0:T(8,128)(2,1)} %all-gather.5.cloned.1.call-done.x_ref, f32[1,2048]{1,0:T(1,128)} %get-tuple-element.434.gain_ref, f32[1,2048]{1,0:T(1,128)} %get-tuple-element.433.shift_ref, bf16[8,2048]{1,0:T(8,128)(2,1)} %bitcast.335), custom_call_target="tpu_custom_call" | custom-call | tf_op jit(solution)/shard_map/norm_rows/pallas_call | solution.py:452
  111.5 10.1 %collective-permute-done.11 = bf16[32,2048]{1,0:T(8,128)(2,1)S(1)} collective-permute-done((bf16[32,2048]{1,0:T(8,128)(2,1)S(1)}, bf16[32,2048]{1,0:T(8,128)(2,1)S(1)}, u32[]{:S(2)}, u32[]{:S(2)}) %collective-permute-start.11) | collective-permute-done | bytes 131104 | tf_op jit(solution)/shard_map/ppermute | solution.py:917
  129.7 8.1 %qkv_rows.1.q_ref.k_ref.v_ref = bf16[1024,768]{1,0:T(8,128)(2,1)} custom-call(bf16[1024,2048]{1,0:T(8,128)(2,1)} %get-tuple-element.203.h_ref, bf16[512,768]{1,0:T(8,128)(2,1)} %copy-done.14, bf16[512,768]{1,0:T(8,128)(2,1)} %copy-done.27, bf16[512,768]{1,0:T(8,128)(2,1)} %copy-done.28, bf16[512,768]{1,0:T(8,128)(2,1)} %copy-done.29, f32[1,768]{1,0:T(1,128)} %bitcast.361, ...), custom_call_target="tpu_custom_call" | custom-call | tf_op jit(solution)/shard_map/qkv_rows/pallas_call | solution.py:740
  137.7 9.3 %attend.1 = (bf16[1024,256]{1,0:T(8,128)(2,1)}, f32[2,1,1024]{2,1,0:T(1,128)}) custom-call(bf16[1024,768]{1,0:T(8,128)(2,1)} %qkv_rows.1.q_ref.k_ref.v_ref, bf16[1024,768]{1,0:T(8,128)(2,1)} %qkv_rows.1.q_ref.k_ref.v_ref, bf16[1024,768]{1,0:T(8,128)(2,1)} %qkv_rows.1.q_ref.k_ref.v_ref, s32[1024,1]{1,0:T(8,128)} %copy.206.key_ref, ...), custom_call_target="tpu_custom_call" | custom-call | tf_op jit(solution)/shard_map/attend/pallas_call | solution.py:818
  154.4 4.3 all-to-all-start.3
  158.7 11.4 %all-gather.9.cloned.1.call-start = ((), (), s32[]{:S(2)}) async-start(), calls=%async_computation.11 | async-start | bytes 4718592 | tf_op jit(solution)/shard_map/all_gather | solution.py:1130
  184.7 3.4 own_rows.1
  191.2 16.4 %collective-permute-done.19.refs_6_.refs_14_ = bf16[512,512]{1,0:T(8,128)(2,1)} collective-permute-done((bf16[512,512]{1,0:T(8,128)(2,1)S(1)}, bf16[512,512]{1,0:T(8,128)(2,1)}, u32[]{:S(2)}, u32[]{:S(2)}) %collective-permute-start.19) | collective-permute-done | bytes 524320 | tf_op jit(solution)/shard_map/ppermute | solution.py:366
  212.7 11.9 %collective-permute-done.20 = bf16[128,2048]{1,0:T(8,128)(2,1)S(1)} collective-permute-done((bf16[128,2048]{1,0:T(8,128)(2,1)S(1)}, bf16[128,2048]{1,0:T(8,128)(2,1)S(1)}, u32[]{:S(2)}, u32[]{:S(2)}) %collective-permute-start.20) | collective-permute-done | bytes 524320 | tf_op jit(solution)/shard_map/ppermute | solution.py:366
  236.5 5.8 gate_rows.1.dz_ref
  243.9 11.1 %collective-permute-done.24.refs_5_ = bf16[512,512]{1,0:T(8,128)(2,1)S(1)} collective-permute-done((bf16[512,512]{1,0:T(8,128)(2,1)}, bf16[512,512]{1,0:T(8,128)(2,1)S(1)}, u32[]{:S(2)}, u32[]{:S(2)}) %collective-permute-start.24) | collective-permute-done | bytes 524320 | tf_op jit(solution)/shard_map/ppermute | solution.py:366
  260.4 6.0 collective-permute-done.27.refs_3_.refs_11_
  266.4 16.5 %collective-permute-done.25.refs_6_ = bf16[512,512]{1,0:T(8,128)(2,1)S(1)} collective-permute-done((bf16[512,512]{1,0:T(8,128)(2,1)S(1)}, bf16[512,512]{1,0:T(8,128)(2,1)S(1)}, u32[]{:S(2)}, u32[]{:S(2)}) %collective-permute-start.25) | collective-permute-done | bytes 524320 | tf_op jit(solution)/shard_map/ppermute | solution.py:366
  284.7 9.5 %hidden_rows.1 = (f32[1024,1024]{1,0:T(8,128)}, bf16[1024,1024]{1,0:T(8,128)(2,1)}) custom-call(bf16[1024,2048]{1,0:T(8,128)(2,1)} %all-gather.9.cloned.1.call-done.h_ref, f32[1024,1]{1,0:T(8,128)} %copy.211.active_ref, f32[1,1024]{1,0:T(1,128)} %constant_dynamic-slice_fusion.11.bias_ref, bf16[512,512]{1,0:T(8,128)(2,1)} %get-tuple-element.397.refs_0_.refs_8_, ...), custom_call_target="tpu_custom_call" | custom-call | tf_op jit(solution)/shard_map/hidden_rows/pallas_call | solution.py:540
  295.8 15.3 %ffn_rows.1 = (bf16[1024,1024]{1,0:T(8,128)(2,1)}, bf16[1024,2048]{1,0:T(8,128)(2,1)}) custom-call(s32[1]{0:T(128)} %bitcast.49.bit_ref, bf16[1024,2048]{1,0:T(8,128)(2,1)} %gate_rows.1.dz_ref, f32[1024,1024]{1,0:T(8,128)} %get-tuple-element.266.relu_ref, bf16[512,512]{1,0:T(8,128)(2,1)} %get-tuple-element.395.refs_0_, bf16[512,512]{1,0:T(8,128)(2,1)} %copy-done.37, ...), custom_call_target="tpu_custom_call" | custom-call | tf_op jit(solution)/shard_map/ffn_rows/pallas_call | solution.py:596
  320.7 3.5 convolution_convert_fusion.4
  328.1 4.8 collective-permute-done.30
  335.6 5.4 collective-permute-done.32
  350.2 8.6 %wide_rows.1 = bf16[1024,2048]{1,0:T(8,128)(2,1)} custom-call(bf16[1024,1024]{1,0:T(8,128)(2,1)} %get-tuple-element.347.left_ref, bf16[512,512]{1,0:T(8,128)(2,1)} %get-tuple-element.395.refs_0_, bf16[512,512]{1,0:T(8,128)(2,1)} %copy-done.37, bf16[512,512]{1,0:T(8,128)(2,1)} %collective-permute-done.22.refs_2_, bf16[512,512]{1,0:T(8,128)(2,1)} %copy-done.41, ...), custom_call_target="tpu_custom_call" | custom-call | tf_op jit(solution)/shard_map/wide_rows/pallas_call | solution.py:639
  359.9 3.5 collective-permute-start.36
  365.5 3.7 convolution_convert_fusion.2
  370.0 3.8 add_convert_fusion.2
  373.8 9.2 %collective-permute-done.36 = bf16[512,512]{1,0:T(8,128)(2,1)} collective-permute-done((bf16[512,512]{1,0:T(8,128)(2,1)S(1)}, bf16[512,512]{1,0:T(8,128)(2,1)}, u32[]{:S(2)}, u32[]{:S(2)}) %collective-permute-start.36) | collective-permute-done | bytes 524320 | tf_op jit(solution)/shard_map/ppermute | solution.py:366
  383.0 3.5 all-gather.11.cloned.1.call-done.da_ref
  397.4 17.3 %attend_back.1 = bf16[1024,768]{1,0:T(8,128)(2,1)} custom-call(bf16[1024,768]{1,0:T(8,128)(2,1)} %qkv_rows.1.q_ref.k_ref.v_ref, bf16[1024,768]{1,0:T(8,128)(2,1)} %qkv_rows.1.q_ref.k_ref.v_ref, bf16[1024,768]{1,0:T(8,128)(2,1)} %qkv_rows.1.q_ref.k_ref.v_ref, bf16[1024,2048]{1,0:T(8,128)(2,1)} %all-gather.11.cloned.1.call-done.da_ref, ...), custom_call_target="tpu_custom_call" | custom-call | tf_op jit(solution)/shard_map/attend_back/pallas_call | solution.py:845
  414.6 8.9 %collective-permute-done.39 = bf16[2,256,512]{2,1,0:T(8,128)(2,1)} collective-permute-done((bf16[2,256,512]{2,1,0:T(8,128)(2,1)}, bf16[2,256,512]{2,1,0:T(8,128)(2,1)}, u32[]{:S(2)}, u32[]{:S(2)}) %collective-permute-start.39) | collective-permute-done | bytes 524320 | tf_op jit(solution)/shard_map/ppermute | solution.py:366
  425.6 5.3 convolution_convert_fusion.1
  435.0 3.8 convolution_convert_fusion.7
  442.7 5.5 convert_add_fusion
  463.3 31.5 %collective-permute-done.41 = bf16[2,64,2048]{2,1,0:T(8,128)(2,1)} collective-permute-done((bf16[2,64,2048]{2,1,0:T(8,128)(2,1)S(1)}, bf16[2,64,2048]{2,1,0:T(8,128)(2,1)}, u32[]{:S(2)}, u32[]{:S(2)}) %collective-permute-start.41) | collective-permute-done | bytes 524320 | tf_op jit(solution)/shard_map/ppermute | solution.py:366
  497.9 3.4 add_convert_fusion.5
  508.8 7.3 %collective-permute-done.45 = bf16[64,2048]{1,0:T(8,128)(2,1)S(1)} collective-permute-done((bf16[64,2048]{1,0:T(8,128)(2,1)S(1)}, bf16[64,2048]{1,0:T(8,128)(2,1)S(1)}, u32[]{:S(2)}, u32[]{:S(2)}) %collective-permute-start.45) | collective-permute-done | bytes 262176 | tf_op jit(solution)/shard_map/ppermute | solution.py:366
  517.2 4.6 first_back.1
  521.8 4.0 fusion.5
  529.6 3.5 all-to-all-start.5
  537.2 4.0 collective-permute-start.49
  552.9 3.5 all-to-all-start.4
  559.9 11.3 %collective-permute-done.49 = bf16[32,2048]{1,0:T(8,128)(2,1)} collective-permute-done((bf16[32,2048]{1,0:T(8,128)(2,1)}, bf16[32,2048]{1,0:T(8,128)(2,1)}, u32[]{:S(2)}, u32[]{:S(2)}) %collective-permute-start.49) | collective-permute-done | bytes 131104 | tf_op jit(solution)/shard_map/ppermute | solution.py:366
  571.3 16.3 %collective-permute-done.53 = bf16[512,768]{1,0:T(8,128)(2,1)S(1)} collective-permute-done((bf16[512,768]{1,0:T(8,128)(2,1)}, bf16[512,768]{1,0:T(8,128)(2,1)S(1)}, u32[]{:S(2)}, u32[]{:S(2)}) %collective-permute-start.53) | collective-permute-done | bytes 786464 | tf_op jit(solution)/shard_map/ppermute | solution.py:366
  620.8 5.4 all-to-all-start.7
  632.7 8.1 %collective-permute-done.62 = bf16[4,32,2048]{2,1,0:T(8,128)(2,1)} collective-permute-done((bf16[4,32,2048]{2,1,0:T(8,128)(2,1)S(1)}, bf16[4,32,2048]{2,1,0:T(8,128)(2,1)}, u32[]{:S(2)}, u32[]{:S(2)}) %collective-permute-start.62) | collective-permute-done | bytes 524320 | tf_op jit(solution)/shard_map/ppermute | solution.py:366
  (533 shorter events, 265.9 us)
Async XLA Ops:
  20.3 22.1 %all-to-all-start = ((bf16[4,128,3,2,128]{4,3,2,1,0:T(2,128)(2,1)}), bf16[4,128,3,2,128]{4,3,2,1,0:T(2,128)(2,1)S(1)}, u32[]{:S(2)}, u32[]{:S(2)}) async-start(bf16[4,128,3,2,128]{4,3,2,1,0:T(2,128)(2,1)} %bitcast.294), calls=%async_computation | async-start | bytes 1572864 | tf_op jit(solution)/shard_map/all_to_all | solution.py:904
  23.8 79.9 %all-gather.5.cloned.1.call-start = ((), (), s32[]{:S(2)}) async-start(), calls=%async_computation.9 | async-start | bytes 4718592 | tf_op jit(solution)/shard_map/all_gather | solution.py:991
  52.9 28.1 %collective-permute-start.6 = (bf16[512,768]{1,0:T(8,128)(2,1)S(1)}, bf16[512,768]{1,0:T(8,128)(2,1)S(1)}, u32[]{:S(2)}, u32[]{:S(2)}) collective-permute-start(bf16[512,768]{1,0:T(8,128)(2,1)S(1)} %reshape.863.refs_0_), channel_id=1, source_target_pairs={{0,4},{4,0},{1,5},{5,1},{2,6},{6,2},{3,7},{7,3},{8,12},{12,8},{9,1... | collective-permute-start | bytes 2359304 | tf_op jit(solution)/shard_map/ppermute | solution.py:366
  53.9 36.6 %collective-permute-start.5 = (bf16[512,768]{1,0:T(8,128)(2,1)S(1)}, bf16[512,768]{1,0:T(8,128)(2,1)S(1)}, u32[]{:S(2)}, u32[]{:S(2)}) collective-permute-start(bf16[512,768]{1,0:T(8,128)(2,1)S(1)} %reshape.863.refs_0_), channel_id=1, source_target_pairs={{0,16},{16,0},{1,17},{17,1},{2,18},{18,2},{3,19},{19,3},{4,20},{20... | collective-permute-start | bytes 2359304 | tf_op jit(solution)/shard_map/ppermute | solution.py:366
  91.8 31.4 %all-to-all-start.2 = ((bf16[4,128,1024]{2,1,0:T(8,128)(2,1)}), bf16[4,128,1024]{2,1,0:T(8,128)(2,1)S(1)}, u32[]{:S(2)}, u32[]{:S(2)}) async-start(bf16[4,128,1024]{2,1,0:T(8,128)(2,1)} %bitcast.293), calls=%async_computation.2 | async-start | bytes 2097152 | tf_op jit(solution)/shard_map/all_to_all | solution.py:904
  95.3 112.3 %all-gather.7.cloned.1.call-start = ((), (), s32[]{:S(2)}) async-start(), calls=%async_computation.10 | async-start | bytes 4718592 | tf_op jit(solution)/shard_map/all_gather | solution.py:1047
  95.3 27.8 %collective-permute-start.7 = (bf16[512,768]{1,0:T(8,128)(2,1)}, bf16[512,768]{1,0:T(8,128)(2,1)S(1)}, u32[]{:S(2)}, u32[]{:S(2)}) collective-permute-start(bf16[512,768]{1,0:T(8,128)(2,1)} %copy-done.28), channel_id=1, source_target_pairs={{0,4},{4,0},{1,5},{5,1},{2,6},{6,2},{3,7},{7,3},{8,12},{12,8},{9,1... | collective-permute-start | bytes 2359304 | tf_op jit(solution)/shard_map/ppermute | solution.py:366
  97.1 26.1 %collective-permute-start.8 = (bf16[256,512]{1,0:T(8,128)(2,1)S(1)}, bf16[256,512]{1,0:T(8,128)(2,1)S(1)}, u32[]{:S(2)}, u32[]{:S(2)}) collective-permute-start(bf16[256,512]{1,0:T(8,128)(2,1)S(1)} %copy-done.47), channel_id=1, source_target_pairs={{0,16},{16,0},{1,17},{17,1},{2,18},{18,2},{3,19},{19,3},{4,20},{20... | collective-permute-start | bytes 786440 | tf_op jit(solution)/shard_map/ppermute | solution.py:366
  98.6 23.0 %collective-permute-start.11 = (bf16[32,2048]{1,0:T(8,128)(2,1)S(1)}, bf16[32,2048]{1,0:T(8,128)(2,1)S(1)}, u32[]{:S(2)}, u32[]{:S(2)}) collective-permute-start(bf16[32,2048]{1,0:T(8,128)(2,1)S(1)} %get-tuple-element.401), channel_id=1, source_target_pairs={{0,20},{4,16},{16,4},{20,0},{1,21},{5,17},{17,5},{21,1},{2,22},{6,... | collective-permute-start | bytes 393224 | tf_op jit(solution)/shard_map/ppermute | solution.py:917
  101.8 21.4 %collective-permute-start.10 = (bf16[32,2048]{1,0:T(8,128)(2,1)S(1)}, bf16[32,2048]{1,0:T(8,128)(2,1)S(1)}, u32[]{:S(2)}, u32[]{:S(2)}) collective-permute-start(bf16[32,2048]{1,0:T(8,128)(2,1)S(1)} %get-tuple-element.402), channel_id=1, source_target_pairs={{0,16},{16,0},{1,17},{17,1},{2,18},{18,2},{3,19},{19,3},{4,20},{20... | collective-permute-start | bytes 393224 | tf_op jit(solution)/shard_map/ppermute | solution.py:366
  102.0 21.1 %collective-permute-start.9 = (bf16[32,2048]{1,0:T(8,128)(2,1)S(1)}, bf16[32,2048]{1,0:T(8,128)(2,1)S(1)}, u32[]{:S(2)}, u32[]{:S(2)}) collective-permute-start(bf16[32,2048]{1,0:T(8,128)(2,1)S(1)} %get-tuple-element.403), channel_id=1, source_target_pairs={{0,4},{4,0},{1,5},{5,1},{2,6},{6,2},{3,7},{7,3},{8,12},{12,8},{9,1... | collective-permute-start | bytes 393224 | tf_op jit(solution)/shard_map/ppermute | solution.py:366
  125.6 25.8 %collective-permute-start.15 = (bf16[512,512]{1,0:T(8,128)(2,1)}, bf16[512,512]{1,0:T(8,128)(2,1)S(1)}, u32[]{:S(2)}, u32[]{:S(2)}) collective-permute-start(bf16[512,512]{1,0:T(8,128)(2,1)} %slice.282), channel_id=1, source_target_pairs={{0,16},{16,0},{1,17},{17,1},{2,18},{18,2},{3,19},{19,3},{4,20},{20... | collective-permute-start | bytes 1572872 | tf_op jit(solution)/shard_map/ppermute | solution.py:366
  125.6 25.9 %collective-permute-start.14 = (bf16[512,512]{1,0:T(8,128)(2,1)}, bf16[512,512]{1,0:T(8,128)(2,1)S(1)}, u32[]{:S(2)}, u32[]{:S(2)}) collective-permute-start(bf16[512,512]{1,0:T(8,128)(2,1)} %slice.282), channel_id=1, source_target_pairs={{0,4},{4,0},{1,5},{5,1},{2,6},{6,2},{3,7},{7,3},{8,12},{12,8},{9,1... | collective-permute-start | bytes 1572872 | tf_op jit(solution)/shard_map/ppermute | solution.py:366
  127.6 22.6 %collective-permute-start.13 = (bf16[256,512]{1,0:T(8,128)(2,1)}, bf16[256,512]{1,0:T(8,128)(2,1)}, u32[]{:S(2)}, u32[]{:S(2)}) collective-permute-start(bf16[256,512]{1,0:T(8,128)(2,1)} %copy-done.61), channel_id=1, source_target_pairs={{0,4},{4,0},{1,5},{5,1},{2,6},{6,2},{3,7},{7,3},{8,12},{12,8},{9,1... | collective-permute-start | bytes 786440 | tf_op jit(solution)/shard_map/ppermute | solution.py:366
  154.4 20.6 %collective-permute-start.16 = (bf16[512,2048]{1,0:T(8,128)(2,1)}, bf16[512,2048]{1,0:T(8,128)(2,1)}, u32[]{:S(2)}, u32[]{:S(2)}) collective-permute-start(bf16[512,2048]{1,0:T(8,128)(2,1)} %convolution_convert_fusion), channel_id=1, source_target_pairs={{0,2},{2,0},{1,3},{3,1},{4,6},{6,4},{5,7},{7,5},{8,10},{10,8},{9,1... | collective-permute-start | bytes 6291464 | tf_op jit(solution)/shard_map/ppermute | solution.py:366
  158.7 124.2 %all-gather.9.cloned.1.call-start = ((), (), s32[]{:S(2)}) async-start(), calls=%async_computation.11 | async-start | bytes 4718592 | tf_op jit(solution)/shard_map/all_gather | solution.py:1130
  178.6 29.0 %collective-permute-start.17 = (bf16[2,128,2048]{2,1,0:T(8,128)(2,1)}, bf16[2,128,2048]{2,1,0:T(8,128)(2,1)}, u32[]{:S(2)}, u32[]{:S(2)}) collective-permute-start(bf16[2,128,2048]{2,1,0:T(8,128)(2,1)} %fusion.6), channel_id=1, source_target_pairs={{0,1},{1,0},{2,3},{3,2},{4,5},{5,4},{6,7},{7,6},{8,9},{9,8},{10,11... | collective-permute-start | bytes 3145736 | tf_op jit(solution)/shard_map/ppermute | solution.py:366
  181.3 26.3 %collective-permute-start.19 = (bf16[512,512]{1,0:T(8,128)(2,1)S(1)}, bf16[512,512]{1,0:T(8,128)(2,1)}, u32[]{:S(2)}, u32[]{:S(2)}) collective-permute-start(bf16[512,512]{1,0:T(8,128)(2,1)S(1)} %get-tuple-element.398.refs_4_.refs_12_), channel_id=1, source_target_pairs={{0,16},{16,0},{1,17},{17,1},{2,18},{18,2},{3,19},{19,3},{4,20},{20... | collective-permute-start | bytes 1572872 | tf_op jit(solution)/shard_map/ppermute | solution.py:366
  183.9 23.6 %collective-permute-start.18 = (bf16[512,512]{1,0:T(8,128)(2,1)S(1)}, bf16[512,512]{1,0:T(8,128)(2,1)S(1)}, u32[]{:S(2)}, u32[]{:S(2)}) collective-permute-start(bf16[512,512]{1,0:T(8,128)(2,1)S(1)} %get-tuple-element.398.refs_4_.refs_12_), channel_id=1, source_target_pairs={{0,4},{4,0},{1,5},{5,1},{2,6},{6,2},{3,7},{7,3},{8,12},{12,8},{9,1... | collective-permute-start | bytes 1572872 | tf_op jit(solution)/shard_map/ppermute | solution.py:366
  228.6 158.0 %all-gather.11.cloned.1.call-start = ((), (), s32[]{:S(2)}) async-start(), calls=%async_computation.12 | async-start | bytes 4718592 | tf_op jit(solution)/shard_map/all_gather | solution.py:1187
  230.3 24.8 %collective-permute-start.24 = (bf16[512,512]{1,0:T(8,128)(2,1)}, bf16[512,512]{1,0:T(8,128)(2,1)S(1)}, u32[]{:S(2)}, u32[]{:S(2)}) collective-permute-start(bf16[512,512]{1,0:T(8,128)(2,1)} %get-tuple-element.399), channel_id=1, source_target_pairs={{0,4},{4,0},{1,5},{5,1},{2,6},{6,2},{3,7},{7,3},{8,12},{12,8},{9,1... | collective-permute-start | bytes 1572872 | tf_op jit(solution)/shard_map/ppermute | solution.py:366
  231.8 25.2 %collective-permute-start.22 = (bf16[512,512]{1,0:T(8,128)(2,1)}, bf16[512,512]{1,0:T(8,128)(2,1)}, u32[]{:S(2)}, u32[]{:S(2)}) collective-permute-start(bf16[512,512]{1,0:T(8,128)(2,1)} %get-tuple-element.400), channel_id=1, source_target_pairs={{0,16},{16,0},{1,17},{17,1},{2,18},{18,2},{3,19},{19,3},{4,20},{20... | collective-permute-start | bytes 1572872 | tf_op jit(solution)/shard_map/ppermute | solution.py:366
  234.8 31.6 %collective-permute-start.27 = (bf16[512,512]{1,0:T(8,128)(2,1)S(1)}, bf16[512,512]{1,0:T(8,128)(2,1)}, u32[]{:S(2)}, u32[]{:S(2)}) collective-permute-start(bf16[512,512]{1,0:T(8,128)(2,1)S(1)} %copy-done.35), channel_id=1, source_target_pairs={{0,4},{4,0},{1,5},{5,1},{2,6},{6,2},{3,7},{7,3},{8,12},{12,8},{9,1... | collective-permute-start | bytes 1572872 | tf_op jit(solution)/shard_map/ppermute | solution.py:366
  257.8 25.0 %collective-permute-start.25 = (bf16[512,512]{1,0:T(8,128)(2,1)S(1)}, bf16[512,512]{1,0:T(8,128)(2,1)S(1)}, u32[]{:S(2)}, u32[]{:S(2)}) collective-permute-start(bf16[512,512]{1,0:T(8,128)(2,1)S(1)} %get-tuple-element.396.refs_4_), channel_id=1, source_target_pairs={{0,16},{16,0},{1,17},{17,1},{2,18},{18,2},{3,19},{19,3},{4,20},{20... | collective-permute-start | bytes 1572872 | tf_op jit(solution)/shard_map/ppermute | solution.py:366
  259.7 23.2 %collective-permute-start.26 = (bf16[512,512]{1,0:T(8,128)(2,1)}, bf16[512,512]{1,0:T(8,128)(2,1)S(1)}, u32[]{:S(2)}, u32[]{:S(2)}) collective-permute-start(bf16[512,512]{1,0:T(8,128)(2,1)} %collective-permute-done.22.refs_2_), channel_id=1, source_target_pairs={{0,4},{4,0},{1,5},{5,1},{2,6},{6,2},{3,7},{7,3},{8,12},{12,8},{9,1... | collective-permute-start | bytes 1572872 | tf_op jit(solution)/shard_map/ppermute | solution.py:366
  315.2 26.7 %collective-permute-start.34 = (bf16[1024,512]{1,0:T(8,128)(2,1)S(1)}, bf16[1024,512]{1,0:T(8,128)(2,1)S(1)}, u32[]{:S(2)}, u32[]{:S(2)}) collective-permute-start(bf16[1024,512]{1,0:T(8,128)(2,1)S(1)} %convolution_convert_fusion.3), channel_id=1, source_target_pairs={{0,4},{4,0},{1,5},{5,1},{2,6},{6,2},{3,7},{7,3},{8,12},{12,8},{9,1... | collective-permute-start | bytes 3145736 | tf_op jit(solution)/shard_map/ppermute | solution.py:366
  346.3 148.5 %reduce-scatter.2.cloned.1.call-start = ((), (), s32[]{:S(2)}) async-start(), calls=%async_computation.13 | async-start | bytes 4718592 | tf_op jit(solution)/shard_map/reduce_scatter | solution.py:1210
  346.6 23.4 %collective-permute-start.35 = (bf16[512,1024]{1,0:T(8,128)(2,1)}, bf16[512,1024]{1,0:T(8,128)(2,1)}, u32[]{:S(2)}, u32[]{:S(2)}) collective-permute-start(bf16[512,1024]{1,0:T(8,128)(2,1)} %convolution_convert_fusion.4), channel_id=1, source_target_pairs={{0,4},{4,0},{1,5},{5,1},{2,6},{6,2},{3,7},{7,3},{8,12},{12,8},{9,1... | collective-permute-start | bytes 3145736 | tf_op jit(solution)/shard_map/ppermute | solution.py:366
  359.9 23.1 %collective-permute-start.36 = (bf16[512,512]{1,0:T(8,128)(2,1)S(1)}, bf16[512,512]{1,0:T(8,128)(2,1)}, u32[]{:S(2)}, u32[]{:S(2)}) collective-permute-start(bf16[512,512]{1,0:T(8,128)(2,1)S(1)} %slice.305), channel_id=1, source_target_pairs={{0,16},{16,0},{1,17},{17,1},{2,18},{18,2},{3,19},{19,3},{4,20},{20... | collective-permute-start | bytes 1572872 | tf_op jit(solution)/shard_map/ppermute | solution.py:366
  386.6 28.0 %collective-permute-start.37 = (bf16[1024,512]{1,0:T(8,128)(2,1)}, bf16[1024,512]{1,0:T(8,128)(2,1)}, u32[]{:S(2)}, u32[]{:S(2)}) collective-permute-start(bf16[1024,512]{1,0:T(8,128)(2,1)} %convolution_convert_fusion.5), channel_id=1, source_target_pairs={{0,4},{4,0},{1,5},{5,1},{2,6},{6,2},{3,7},{7,3},{8,12},{12,8},{9,1... | collective-permute-start | bytes 3145736 | tf_op jit(solution)/shard_map/ppermute | solution.py:366
  394.4 29.1 %collective-permute-start.39 = (bf16[2,256,512]{2,1,0:T(8,128)(2,1)}, bf16[2,256,512]{2,1,0:T(8,128)(2,1)}, u32[]{:S(2)}, u32[]{:S(2)}) collective-permute-start(bf16[2,256,512]{2,1,0:T(8,128)(2,1)} %pad_maximum_fusion.6), channel_id=1, source_target_pairs={{0,4},{4,0},{1,5},{5,1},{2,6},{6,2},{3,7},{7,3},{8,12},{12,8},{9,1... | collective-permute-start | bytes 1572872 | tf_op jit(solution)/shard_map/ppermute | solution.py:366
  394.9 28.6 %collective-permute-start.38 = (bf16[512,512]{1,0:T(8,128)(2,1)}, bf16[512,512]{1,0:T(8,128)(2,1)}, u32[]{:S(2)}, u32[]{:S(2)}) collective-permute-start(bf16[512,512]{1,0:T(8,128)(2,1)} %slice.306), channel_id=1, source_target_pairs={{0,16},{16,0},{1,17},{17,1},{2,18},{18,2},{3,19},{19,3},{4,20},{20... | collective-permute-start | bytes 1572872 | tf_op jit(solution)/shard_map/ppermute | solution.py:366
  438.9 24.4 %collective-permute-start.43 = (bf16[512,768]{1,0:T(8,128)(2,1)}, bf16[512,768]{1,0:T(8,128)(2,1)}, u32[]{:S(2)}, u32[]{:S(2)}) collective-permute-start(bf16[512,768]{1,0:T(8,128)(2,1)} %convolution_convert_fusion.7), channel_id=1, source_target_pairs={{0,4},{4,0},{1,5},{5,1},{2,6},{6,2},{3,7},{7,3},{8,12},{12,8},{9,1... | collective-permute-start | bytes 2359304 | tf_op jit(solution)/shard_map/ppermute | solution.py:366
  440.4 76.8 %collective-permute-start.46 = (bf16[512,1024]{1,0:T(8,128)(2,1)}, bf16[512,1024]{1,0:T(8,128)(2,1)}, u32[]{:S(2)}, u32[]{:S(2)}) collective-permute-start(bf16[512,1024]{1,0:T(8,128)(2,1)} %add_convert_fusion.2), channel_id=1, source_target_pairs={{0,16},{16,0},{1,17},{17,1},{2,18},{18,2},{3,19},{19,3},{4,20},{20... | collective-permute-start | bytes 3145736 | tf_op jit(solution)/shard_map/ppermute | solution.py:366
  452.4 42.5 %collective-permute-start.41 = (bf16[2,64,2048]{2,1,0:T(8,128)(2,1)S(1)}, bf16[2,64,2048]{2,1,0:T(8,128)(2,1)}, u32[]{:S(2)}, u32[]{:S(2)}) collective-permute-start(bf16[2,64,2048]{2,1,0:T(8,128)(2,1)S(1)} %fusion.32), channel_id=1, source_target_pairs={{0,8},{8,0},{1,9},{9,1},{2,10},{10,2},{3,11},{11,3},{4,12},{12,4},... | collective-permute-start | bytes 1572872 | tf_op jit(solution)/shard_map/ppermute | solution.py:366
  453.3 41.6 %collective-permute-start.42 = (bf16[2,64,2048]{2,1,0:T(8,128)(2,1)S(1)}, bf16[2,64,2048]{2,1,0:T(8,128)(2,1)}, u32[]{:S(2)}, u32[]{:S(2)}) collective-permute-start(bf16[2,64,2048]{2,1,0:T(8,128)(2,1)S(1)} %fusion.34), channel_id=1, source_target_pairs={{0,1},{1,0},{2,3},{3,2},{4,5},{5,4},{6,7},{7,6},{8,9},{9,8},{10,11... | collective-permute-start | bytes 1572872 | tf_op jit(solution)/shard_map/ppermute | solution.py:366
  497.9 23.9 %collective-permute-start.47 = (bf16[256,512]{1,0:T(8,128)(2,1)}, bf16[256,512]{1,0:T(8,128)(2,1)}, u32[]{:S(2)}, u32[]{:S(2)}) collective-permute-start(bf16[256,512]{1,0:T(8,128)(2,1)} %fusion.1), channel_id=1, source_target_pairs={{0,16},{16,0},{1,17},{17,1},{2,18},{18,2},{3,19},{19,3},{4,20},{20... | collective-permute-start | bytes 786440 | tf_op jit(solution)/shard_map/ppermute | solution.py:366
  501.3 69.9 %collective-permute-start.52 = (bf16[512,768]{1,0:T(8,128)(2,1)}, bf16[512,768]{1,0:T(8,128)(2,1)}, u32[]{:S(2)}, u32[]{:S(2)}) collective-permute-start(bf16[512,768]{1,0:T(8,128)(2,1)} %convolution_convert_fusion.6), channel_id=1, source_target_pairs={{0,4},{4,0},{1,5},{5,1},{2,6},{6,2},{3,7},{7,3},{8,12},{12,8},{9,1... | collective-permute-start | bytes 2359304 | tf_op jit(solution)/shard_map/ppermute | solution.py:366
  508.6 37.9 %collective-permute-start.51 = (bf16[512,1024]{1,0:T(8,128)(2,1)}, bf16[512,1024]{1,0:T(8,128)(2,1)}, u32[]{:S(2)}, u32[]{:S(2)}) collective-permute-start(bf16[512,1024]{1,0:T(8,128)(2,1)} %convolution_convert_fusion.2), channel_id=1, source_target_pairs={{0,4},{4,0},{1,5},{5,1},{2,6},{6,2},{3,7},{7,3},{8,12},{12,8},{9,1... | collective-permute-start | bytes 3145736 | tf_op jit(solution)/shard_map/ppermute | solution.py:366
  529.6 22.3 %all-to-all-start.5 = ((bf16[4,1024,128]{2,1,0:T(8,128)(2,1)}), bf16[4,1024,128]{2,1,0:T(8,128)(2,1)S(1)}, u32[]{:S(2)}, u32[]{:S(2)}) async-start(bf16[4,1024,128]{2,1,0:T(8,128)(2,1)} %bitcast.306), calls=%async_computation.6 | async-start | bytes 2097152 | tf_op jit(solution)/shard_map/all_to_all | solution.py:904
  537.2 22.7 %collective-permute-start.50 = (bf16[32,2048]{1,0:T(8,128)(2,1)}, bf16[32,2048]{1,0:T(8,128)(2,1)S(1)}, u32[]{:S(2)}, u32[]{:S(2)}) collective-permute-start(bf16[32,2048]{1,0:T(8,128)(2,1)} %get-tuple-element.418), channel_id=1, source_target_pairs={{0,20},{4,16},{16,4},{20,0},{1,21},{5,17},{17,5},{21,1},{2,22},{6,... | collective-permute-start | bytes 393224 | tf_op jit(solution)/shard_map/ppermute | solution.py:917
  537.2 34.0 %collective-permute-start.49 = (bf16[32,2048]{1,0:T(8,128)(2,1)}, bf16[32,2048]{1,0:T(8,128)(2,1)}, u32[]{:S(2)}, u32[]{:S(2)}) collective-permute-start(bf16[32,2048]{1,0:T(8,128)(2,1)} %get-tuple-element.419), channel_id=1, source_target_pairs={{0,16},{16,0},{1,17},{17,1},{2,18},{18,2},{3,19},{19,3},{4,20},{20... | collective-permute-start | bytes 393224 | tf_op jit(solution)/shard_map/ppermute | solution.py:366
  541.2 30.0 %collective-permute-start.48 = (bf16[32,2048]{1,0:T(8,128)(2,1)}, bf16[32,2048]{1,0:T(8,128)(2,1)}, u32[]{:S(2)}, u32[]{:S(2)}) collective-permute-start(bf16[32,2048]{1,0:T(8,128)(2,1)} %get-tuple-element.420), channel_id=1, source_target_pairs={{0,4},{4,0},{1,5},{5,1},{2,6},{6,2},{3,7},{7,3},{8,12},{12,8},{9,1... | collective-permute-start | bytes 393224 | tf_op jit(solution)/shard_map/ppermute | solution.py:366
  546.5 41.0 %collective-permute-start.53 = (bf16[512,768]{1,0:T(8,128)(2,1)}, bf16[512,768]{1,0:T(8,128)(2,1)S(1)}, u32[]{:S(2)}, u32[]{:S(2)}) collective-permute-start(bf16[512,768]{1,0:T(8,128)(2,1)} %add_convert_fusion.5), channel_id=1, source_target_pairs={{0,16},{16,0},{1,17},{17,1},{2,18},{18,2},{3,19},{19,3},{4,20},{20... | collective-permute-start | bytes 2359304 | tf_op jit(solution)/shard_map/ppermute | solution.py:366
  552.9 36.1 %all-to-all-start.4 = ((bf16[4,128,1024]{2,1,0:T(8,128)(2,1)}), bf16[4,128,1024]{2,1,0:T(8,128)(2,1)S(1)}, u32[]{:S(2)}, u32[]{:S(2)}) async-start(bf16[4,128,1024]{2,1,0:T(8,128)(2,1)} %bitcast.94), calls=%async_computation.5 | async-start | bytes 2097152 | tf_op jit(solution)/shard_map/all_to_all | solution.py:904
  591.3 26.7 %all-to-all-start.6 = ((bf16[4,256,128]{2,1,0:T(8,128)(2,1)}), bf16[4,256,128]{2,1,0:T(8,128)(2,1)S(1)}, u32[]{:S(2)}, u32[]{:S(2)}) async-start(bf16[4,256,128]{2,1,0:T(8,128)(2,1)} %bitcast_bitcast_fusion.2), calls=%async_computation.7 | async-start | bytes 524288 | tf_op jit(solution)/shard_map/all_to_all | solution.py:904
  595.8 22.2 %collective-permute-start.54 = (bf16[4,32,2048]{2,1,0:T(8,128)(2,1)S(1)}, bf16[4,32,2048]{2,1,0:T(8,128)(2,1)}, u32[]{:S(2)}, u32[]{:S(2)}) collective-permute-start(bf16[4,32,2048]{2,1,0:T(8,128)(2,1)S(1)} %pad_maximum_fusion.7), channel_id=1, source_target_pairs={{0,1},{1,0},{2,3},{3,2},{4,5},{5,4},{6,7},{7,6},{8,9},{9,8},{10,11... | collective-permute-start | bytes 1572872 | tf_op jit(solution)/shard_map/ppermute | solution.py:366
  620.8 22.7 %all-to-all-start.7 = ((bf16[4,128,768]{2,1,0:T(8,128)(2,1)}), bf16[4,128,768]{2,1,0:T(8,128)(2,1)S(1)}, u32[]{:S(2)}, u32[]{:S(2)}) async-start(bf16[4,128,768]{2,1,0:T(8,128)(2,1)} %bitcast.119), calls=%async_computation.8 | async-start | bytes 1572864 | tf_op jit(solution)/shard_map/all_to_all | solution.py:904
  (105 other events, 949.9 us)
Sparse Core Ops, SparseCore 0:
  42.9 43.8 all-gather.4
  124.9 38.7 all-gather.6
  228.7 43.5 all-gather.8
  346.4 40.1 all-gather.10
  388.7 104.4 reduce-scatter.1

commit v5 on v4

--- a/solution.py
+++ b/solution.py
@@ -1103,15 +1103,15 @@
     attn_gate = GROUPS * jnp.sum(attn_prob * attn_pick, axis=-1, keepdims=True)
     ffn_gate = GROUPS * jnp.sum(ffn_prob * ffn_pick, axis=-1, keepdims=True)
     attn_total = dot_to(attn_here, w_out, ((1,), (0,))) + attn_got.astype(WIDE)
-    attn_total, attn_gate, ffn_gate, tokens_own, cotangent_own, e_down = tie(
-        attn_total, attn_gate, ffn_gate, tokens_own, cotangent_own, e_down
+    attn_total, attn_gate, ffn_gate, tokens_own, cotangent_own = tie(
+        attn_total, attn_gate, ffn_gate, tokens_own, cotangent_own
     )
     attn_total = attn_total.reshape(2, 2, own, width)
     attn_keep, attn_send = keep_and_send(attn_total, y, 1)
     attn_got = swap(attn_send.astype(LOW), "y")
     rows, upstream = own_rows(bits, tokens_own, cotangent_own)
-    attn_keep, attn_got, rows, upstream, up_x2, up_z2, cotangent_all = tie(
-        attn_keep, attn_got, rows, upstream, up_x2, up_z2, cotangent_all
+    attn_keep, attn_got, rows, upstream, up_x2, up_z2, cotangent_all, e_down = tie(
+        attn_keep, attn_got, rows, upstream, up_x2, up_z2, cotangent_all, e_down
     )
     attn_keep, attn_send = keep_and_send(attn_keep + attn_got.astype(WIDE), zl, 0)
     attn_sum = attn_keep + swap(attn_send.astype(LOW), "zl").astype(WIDE)

time: 663 us -> 661 us (level)
    unnamed x170 -> x172, local copies, waits for them, and re-layouts: 14.4 us -> 18 us
  transfers between devices with their start and end apart: 77 -> 77, of which waited for: 34 -> 33; matrix products, arithmetic and copies ran while one was open for 26% -> 26% of each run, Pallas kernels for 12% -> 12%
where the time goes in v5:
time: 661 us; the launch traced here: 654 us
  waiting for transfers between devices  221 us (33%)
  starting transfers between devices  116 us (18%)
  Pallas kernels  92.3 us (14%)
  local copies, waits for them, and re-layouts  89.4 us (14%)
  matrix products  61.9 us (9%)
  other arithmetic  57.8 us (9%)
  between operations  15.6 us (2%)
    ppermute x60, waiting for transfers between devices, swap(): return lax.ppermute(value, axis, [(0, 1), (1, 0)])  196 us
    ppermute x60, starting transfers between devices, swap(): return lax.ppermute(value, axis, [(0, 1), (1, 0)])  71.5 us
    dot_general x20, matrix products, dot_to(): lax.dot_general(left, right, (dims, ((), ())), preferred_element_type=WIDE)  57.7 us
    all_to_all x8, starting transfers between devices, exchange(): return lax.all_to_all(value, ('zl', 'c'), 0, 0, tiled=True)  29.7 us
    unnamed x172, local copies, waits for them, and re-layouts  18 us
    pallas_call x1, Pallas kernels, attend_back(): pl.pallas_call(attend_back_kernel, grid=(heads, length // BLOCK_A), in_sp...  17.3 us
    pallas_call x1, Pallas kernels, ffn_rows(): pl.pallas_call(functools.partial(ffn_kernel, tuple((len(g) for g in down_...  15.3 us
  transfers between devices with their start and end apart: 77, of which 33 were waited for; matrix products, arithmetic and copies ran while one was open for 26% of the time, Pallas kernels for 12%

profile of v5, /device:TPU:0, one launch (start us, length us, event | category | flops | bytes accessed | tf_op | source)
XLA Modules:
  0.0 654.0 jit_solution(7813760062246575903)
XLA Ops:
  20.3 3.5 all-to-all-start
  27.7 3.5 collective-permute-done.1
  36.6 5.7 collective-permute-done.4
  42.8 3.4 all-to-all-start.1
  46.8 5.4 all-to-all-done.1
  81.1 9.4 %collective-permute-done.5.refs_2_ = bf16[512,768]{1,0:T(8,128)(2,1)S(1)} collective-permute-done((bf16[512,768]{1,0:T(8,128)(2,1)S(1)}, bf16[512,768]{1,0:T(8,128)(2,1)S(1)}, u32[]{:S(2)}, u32[]{:S(2)}) %collective-permute-start.5) | collective-permute-done | bytes 786464 | tf_op jit(solution)/shard_map/ppermute | solution.py:366
  91.6 3.5 all-to-all-start.2
  104.2 7.8 %norm_rows.1 = (bf16[1024,2048]{1,0:T(8,128)(2,1)}, f32[1024,8]{1,0:T(8,128)}) custom-call(s32[2]{0:T(128)} %pad_add_fusion.1.bits_ref, bf16[1024,2048]{1,0:T(8,128)(2,1)} %all-gather.5.cloned.1.call-done.x_ref, f32[1,2048]{1,0:T(1,128)} %get-tuple-element.434.gain_ref, f32[1,2048]{1,0:T(1,128)} %get-tuple-element.433.shift_ref, bf16[8,2048]{1,0:T(8,128)(2,1)} %bitcast.335), custom_call_target="tpu_custom_call" | custom-call | tf_op jit(solution)/shard_map/norm_rows/pallas_call | solution.py:452
  112.0 9.7 %collective-permute-done.11 = bf16[32,2048]{1,0:T(8,128)(2,1)S(1)} collective-permute-done((bf16[32,2048]{1,0:T(8,128)(2,1)}, bf16[32,2048]{1,0:T(8,128)(2,1)S(1)}, u32[]{:S(2)}, u32[]{:S(2)}) %collective-permute-start.11) | collective-permute-done | bytes 131104 | tf_op jit(solution)/shard_map/ppermute | solution.py:917
  131.5 8.1 %qkv_rows.1.q_ref.k_ref.v_ref = bf16[1024,768]{1,0:T(8,128)(2,1)} custom-call(bf16[1024,2048]{1,0:T(8,128)(2,1)} %get-tuple-element.203.h_ref, bf16[512,768]{1,0:T(8,128)(2,1)} %copy-done.14, bf16[512,768]{1,0:T(8,128)(2,1)} %copy-done.27, bf16[512,768]{1,0:T(8,128)(2,1)} %copy-done.28, bf16[512,768]{1,0:T(8,128)(2,1)} %copy-done.29, f32[1,768]{1,0:T(1,128)} %bitcast.361, ...), custom_call_target="tpu_custom_call" | custom-call | tf_op jit(solution)/shard_map/qkv_rows/pallas_call | solution.py:740
  139.5 9.3 %attend.1 = (bf16[1024,256]{1,0:T(8,128)(2,1)}, f32[2,1,1024]{2,1,0:T(1,128)}) custom-call(bf16[1024,768]{1,0:T(8,128)(2,1)} %qkv_rows.1.q_ref.k_ref.v_ref, bf16[1024,768]{1,0:T(8,128)(2,1)} %qkv_rows.1.q_ref.k_ref.v_ref, bf16[1024,768]{1,0:T(8,128)(2,1)} %qkv_rows.1.q_ref.k_ref.v_ref, s32[1024,1]{1,0:T(8,128)} %copy.206.key_ref, ...), custom_call_target="tpu_custom_call" | custom-call | tf_op jit(solution)/shard_map/attend/pallas_call | solution.py:818
  156.3 4.3 all-to-all-start.3
  160.5 11.3 %all-gather.9.cloned.1.call-start = ((), (), s32[]{:S(2)}) async-start(), calls=%async_computation.11 | async-start | bytes 4718592 | tf_op jit(solution)/shard_map/all_gather | solution.py:1130
  188.2 3.4 own_rows.1
  194.7 15.1 %collective-permute-done.19.refs_6_.refs_14_ = bf16[512,512]{1,0:T(8,128)(2,1)} collective-permute-done((bf16[512,512]{1,0:T(8,128)(2,1)S(1)}, bf16[512,512]{1,0:T(8,128)(2,1)}, u32[]{:S(2)}, u32[]{:S(2)}) %collective-permute-start.19) | collective-permute-done | bytes 524320 | tf_op jit(solution)/shard_map/ppermute | solution.py:366
  214.7 12.0 %collective-permute-done.20 = bf16[128,2048]{1,0:T(8,128)(2,1)S(1)} collective-permute-done((bf16[128,2048]{1,0:T(8,128)(2,1)S(1)}, bf16[128,2048]{1,0:T(8,128)(2,1)S(1)}, u32[]{:S(2)}, u32[]{:S(2)}) %collective-permute-start.20) | collective-permute-done | bytes 524320 | tf_op jit(solution)/shard_map/ppermute | solution.py:366
  238.4 5.8 gate_rows.1.dz_ref
  245.9 11.1 %collective-permute-done.24.refs_5_ = bf16[512,512]{1,0:T(8,128)(2,1)S(1)} collective-permute-done((bf16[512,512]{1,0:T(8,128)(2,1)}, bf16[512,512]{1,0:T(8,128)(2,1)S(1)}, u32[]{:S(2)}, u32[]{:S(2)}) %collective-permute-start.24) | collective-permute-done | bytes 524320 | tf_op jit(solution)/shard_map/ppermute | solution.py:366
  262.3 6.0 collective-permute-done.27.refs_3_.refs_11_
  268.3 16.5 %collective-permute-done.25.refs_6_ = bf16[512,512]{1,0:T(8,128)(2,1)S(1)} collective-permute-done((bf16[512,512]{1,0:T(8,128)(2,1)S(1)}, bf16[512,512]{1,0:T(8,128)(2,1)S(1)}, u32[]{:S(2)}, u32[]{:S(2)}) %collective-permute-start.25) | collective-permute-done | bytes 524320 | tf_op jit(solution)/shard_map/ppermute | solution.py:366
  286.6 9.5 %hidden_rows.1 = (f32[1024,1024]{1,0:T(8,128)}, bf16[1024,1024]{1,0:T(8,128)(2,1)}) custom-call(bf16[1024,2048]{1,0:T(8,128)(2,1)} %all-gather.9.cloned.1.call-done.h_ref, f32[1024,1]{1,0:T(8,128)} %copy.211.active_ref, f32[1,1024]{1,0:T(1,128)} %constant_dynamic-slice_fusion.11.bias_ref, bf16[512,512]{1,0:T(8,128)(2,1)} %get-tuple-element.397.refs_0_.refs_8_, ...), custom_call_target="tpu_custom_call" | custom-call | tf_op jit(solution)/shard_map/hidden_rows/pallas_call | solution.py:540
  297.8 15.3 %ffn_rows.1 = (bf16[1024,1024]{1,0:T(8,128)(2,1)}, bf16[1024,2048]{1,0:T(8,128)(2,1)}) custom-call(s32[1]{0:T(128)} %bitcast.49.bit_ref, bf16[1024,2048]{1,0:T(8,128)(2,1)} %gate_rows.1.dz_ref, f32[1024,1024]{1,0:T(8,128)} %get-tuple-element.266.relu_ref, bf16[512,512]{1,0:T(8,128)(2,1)} %get-tuple-element.395.refs_0_, bf16[512,512]{1,0:T(8,128)(2,1)} %copy-done.37, ...), custom_call_target="tpu_custom_call" | custom-call | tf_op jit(solution)/shard_map/ffn_rows/pallas_call | solution.py:596
  322.2 3.5 convolution_convert_fusion.4
  329.6 5.2 collective-permute-done.30
  337.3 5.8 collective-permute-done.32
  352.3 8.6 %wide_rows.1 = bf16[1024,2048]{1,0:T(8,128)(2,1)} custom-call(bf16[1024,1024]{1,0:T(8,128)(2,1)} %get-tuple-element.347.left_ref, bf16[512,512]{1,0:T(8,128)(2,1)} %get-tuple-element.395.refs_0_, bf16[512,512]{1,0:T(8,128)(2,1)} %copy-done.37, bf16[512,512]{1,0:T(8,128)(2,1)} %collective-permute-done.22.refs_2_, bf16[512,512]{1,0:T(8,128)(2,1)} %copy-done.41, ...), custom_call_target="tpu_custom_call" | custom-call | tf_op jit(solution)/shard_map/wide_rows/pallas_call | solution.py:639
  362.0 3.5 collective-permute-start.36
  367.6 3.7 convolution_convert_fusion.2
  372.1 3.8 add_convert_fusion.2
  375.9 9.4 %collective-permute-done.36 = bf16[512,512]{1,0:T(8,128)(2,1)} collective-permute-done((bf16[512,512]{1,0:T(8,128)(2,1)S(1)}, bf16[512,512]{1,0:T(8,128)(2,1)}, u32[]{:S(2)}, u32[]{:S(2)}) %collective-permute-start.36) | collective-permute-done | bytes 524320 | tf_op jit(solution)/shard_map/ppermute | solution.py:366
  385.3 3.5 all-gather.11.cloned.1.call-done.da_ref
  399.6 17.3 %attend_back.1 = bf16[1024,768]{1,0:T(8,128)(2,1)} custom-call(bf16[1024,768]{1,0:T(8,128)(2,1)} %qkv_rows.1.q_ref.k_ref.v_ref, bf16[1024,768]{1,0:T(8,128)(2,1)} %qkv_rows.1.q_ref.k_ref.v_ref, bf16[1024,768]{1,0:T(8,128)(2,1)} %qkv_rows.1.q_ref.k_ref.v_ref, bf16[1024,2048]{1,0:T(8,128)(2,1)} %all-gather.11.cloned.1.call-done.da_ref, ...), custom_call_target="tpu_custom_call" | custom-call | tf_op jit(solution)/shard_map/attend_back/pallas_call | solution.py:845
  416.9 8.9 %collective-permute-done.39 = bf16[2,256,512]{2,1,0:T(8,128)(2,1)} collective-permute-done((bf16[2,256,512]{2,1,0:T(8,128)(2,1)}, bf16[2,256,512]{2,1,0:T(8,128)(2,1)}, u32[]{:S(2)}, u32[]{:S(2)}) %collective-permute-start.39) | collective-permute-done | bytes 524320 | tf_op jit(solution)/shard_map/ppermute | solution.py:366
  427.9 5.3 convolution_convert_fusion.1
  437.3 3.8 convolution_convert_fusion.7
  445.0 5.5 convert_add_fusion
  465.6 31.5 %collective-permute-done.41 = bf16[2,64,2048]{2,1,0:T(8,128)(2,1)} collective-permute-done((bf16[2,64,2048]{2,1,0:T(8,128)(2,1)S(1)}, bf16[2,64,2048]{2,1,0:T(8,128)(2,1)}, u32[]{:S(2)}, u32[]{:S(2)}) %collective-permute-start.41) | collective-permute-done | bytes 524320 | tf_op jit(solution)/shard_map/ppermute | solution.py:366
  510.7 7.6 %collective-permute-done.45 = bf16[64,2048]{1,0:T(8,128)(2,1)S(1)} collective-permute-done((bf16[64,2048]{1,0:T(8,128)(2,1)S(1)}, bf16[64,2048]{1,0:T(8,128)(2,1)S(1)}, u32[]{:S(2)}, u32[]{:S(2)}) %collective-permute-start.45) | collective-permute-done | bytes 262176 | tf_op jit(solution)/shard_map/ppermute | solution.py:366
  519.4 4.6 first_back.1
  524.0 4.0 fusion.5
  531.9 3.5 all-to-all-start.5
  539.5 3.6 collective-permute-start.49
  555.5 3.5 all-to-all-start.4
  562.5 10.6 %collective-permute-done.49 = bf16[32,2048]{1,0:T(8,128)(2,1)} collective-permute-done((bf16[32,2048]{1,0:T(8,128)(2,1)}, bf16[32,2048]{1,0:T(8,128)(2,1)}, u32[]{:S(2)}, u32[]{:S(2)}) %collective-permute-start.49) | collective-permute-done | bytes 131104 | tf_op jit(solution)/shard_map/ppermute | solution.py:366
  573.1 16.3 %collective-permute-done.53 = bf16[512,768]{1,0:T(8,128)(2,1)S(1)} collective-permute-done((bf16[512,768]{1,0:T(8,128)(2,1)}, bf16[512,768]{1,0:T(8,128)(2,1)S(1)}, u32[]{:S(2)}, u32[]{:S(2)}) %collective-permute-start.53) | collective-permute-done | bytes 786464 | tf_op jit(solution)/shard_map/ppermute | solution.py:366
  601.2 3.6 collective-permute-start.56
  622.6 4.6 all-to-all-start.7
  633.7 8.5 %collective-permute-done.62 = bf16[4,32,2048]{2,1,0:T(8,128)(2,1)} collective-permute-done((bf16[4,32,2048]{2,1,0:T(8,128)(2,1)S(1)}, bf16[4,32,2048]{2,1,0:T(8,128)(2,1)}, u32[]{:S(2)}, u32[]{:S(2)}) %collective-permute-start.62) | collective-permute-done | bytes 524320 | tf_op jit(solution)/shard_map/ppermute | solution.py:366
  (535 shorter events, 269.2 us)
Async XLA Ops:
  20.3 22.1 %all-to-all-start = ((bf16[4,128,3,2,128]{4,3,2,1,0:T(2,128)(2,1)}), bf16[4,128,3,2,128]{4,3,2,1,0:T(2,128)(2,1)S(1)}, u32[]{:S(2)}, u32[]{:S(2)}) async-start(bf16[4,128,3,2,128]{4,3,2,1,0:T(2,128)(2,1)} %bitcast.294), calls=%async_computation | async-start | bytes 1572864 | tf_op jit(solution)/shard_map/all_to_all | solution.py:904
  23.8 80.4 %all-gather.5.cloned.1.call-start = ((), (), s32[]{:S(2)}) async-start(), calls=%async_computation.9 | async-start | bytes 4718592 | tf_op jit(solution)/shard_map/all_gather | solution.py:991
  53.0 28.1 %collective-permute-start.6 = (bf16[512,768]{1,0:T(8,128)(2,1)S(1)}, bf16[512,768]{1,0:T(8,128)(2,1)S(1)}, u32[]{:S(2)}, u32[]{:S(2)}) collective-permute-start(bf16[512,768]{1,0:T(8,128)(2,1)S(1)} %reshape.863.refs_0_), channel_id=1, source_target_pairs={{0,4},{4,0},{1,5},{5,1},{2,6},{6,2},{3,7},{7,3},{8,12},{12,8},{9,1... | collective-permute-start | bytes 2359304 | tf_op jit(solution)/shard_map/ppermute | solution.py:366
  53.9 36.6 %collective-permute-start.5 = (bf16[512,768]{1,0:T(8,128)(2,1)S(1)}, bf16[512,768]{1,0:T(8,128)(2,1)S(1)}, u32[]{:S(2)}, u32[]{:S(2)}) collective-permute-start(bf16[512,768]{1,0:T(8,128)(2,1)S(1)} %reshape.863.refs_0_), channel_id=1, source_target_pairs={{0,16},{16,0},{1,17},{17,1},{2,18},{18,2},{3,19},{19,3},{4,20},{20... | collective-permute-start | bytes 2359304 | tf_op jit(solution)/shard_map/ppermute | solution.py:366
  91.6 31.6 %all-to-all-start.2 = ((bf16[4,128,1024]{2,1,0:T(8,128)(2,1)}), bf16[4,128,1024]{2,1,0:T(8,128)(2,1)S(1)}, u32[]{:S(2)}, u32[]{:S(2)}) async-start(bf16[4,128,1024]{2,1,0:T(8,128)(2,1)} %bitcast.293), calls=%async_computation.2 | async-start | bytes 2097152 | tf_op jit(solution)/shard_map/all_to_all | solution.py:904
  95.1 114.7 %all-gather.7.cloned.1.call-start = ((), (), s32[]{:S(2)}) async-start(), calls=%async_computation.10 | async-start | bytes 4718592 | tf_op jit(solution)/shard_map/all_gather | solution.py:1047
  95.2 28.0 %collective-permute-start.7 = (bf16[512,768]{1,0:T(8,128)(2,1)S(1)}, bf16[512,768]{1,0:T(8,128)(2,1)S(1)}, u32[]{:S(2)}, u32[]{:S(2)}) collective-permute-start(bf16[512,768]{1,0:T(8,128)(2,1)S(1)} %collective-permute-done.5.refs_2_), channel_id=1, source_target_pairs={{0,4},{4,0},{1,5},{5,1},{2,6},{6,2},{3,7},{7,3},{8,12},{12,8},{9,1... | collective-permute-start | bytes 2359304 | tf_op jit(solution)/shard_map/ppermute | solution.py:366
  96.9 26.3 %collective-permute-start.8 = (bf16[256,512]{1,0:T(8,128)(2,1)}, bf16[256,512]{1,0:T(8,128)(2,1)}, u32[]{:S(2)}, u32[]{:S(2)}) collective-permute-start(bf16[256,512]{1,0:T(8,128)(2,1)} %copy_bitcast_fusion.2), channel_id=1, source_target_pairs={{0,16},{16,0},{1,17},{17,1},{2,18},{18,2},{3,19},{19,3},{4,20},{20... | collective-permute-start | bytes 786440 | tf_op jit(solution)/shard_map/ppermute | solution.py:366
  99.2 22.5 %collective-permute-start.11 = (bf16[32,2048]{1,0:T(8,128)(2,1)}, bf16[32,2048]{1,0:T(8,128)(2,1)S(1)}, u32[]{:S(2)}, u32[]{:S(2)}) collective-permute-start(bf16[32,2048]{1,0:T(8,128)(2,1)} %get-tuple-element.401), channel_id=1, source_target_pairs={{0,20},{4,16},{16,4},{20,0},{1,21},{5,17},{17,5},{21,1},{2,22},{6,... | collective-permute-start | bytes 393224 | tf_op jit(solution)/shard_map/ppermute | solution.py:917
  102.2 21.0 %collective-permute-start.10 = (bf16[32,2048]{1,0:T(8,128)(2,1)S(1)}, bf16[32,2048]{1,0:T(8,128)(2,1)S(1)}, u32[]{:S(2)}, u32[]{:S(2)}) collective-permute-start(bf16[32,2048]{1,0:T(8,128)(2,1)S(1)} %get-tuple-element.402), channel_id=1, source_target_pairs={{0,16},{16,0},{1,17},{17,1},{2,18},{18,2},{3,19},{19,3},{4,20},{20... | collective-permute-start | bytes 393224 | tf_op jit(solution)/shard_map/ppermute | solution.py:366
  102.5 20.7 %collective-permute-start.9 = (bf16[32,2048]{1,0:T(8,128)(2,1)S(1)}, bf16[32,2048]{1,0:T(8,128)(2,1)S(1)}, u32[]{:S(2)}, u32[]{:S(2)}) collective-permute-start(bf16[32,2048]{1,0:T(8,128)(2,1)S(1)} %get-tuple-element.403), channel_id=1, source_target_pairs={{0,4},{4,0},{1,5},{5,1},{2,6},{6,2},{3,7},{7,3},{8,12},{12,8},{9,1... | collective-permute-start | bytes 393224 | tf_op jit(solution)/shard_map/ppermute | solution.py:366
  127.4 25.9 %collective-permute-start.15 = (bf16[512,512]{1,0:T(8,128)(2,1)}, bf16[512,512]{1,0:T(8,128)(2,1)S(1)}, u32[]{:S(2)}, u32[]{:S(2)}) collective-permute-start(bf16[512,512]{1,0:T(8,128)(2,1)} %slice.282), channel_id=1, source_target_pairs={{0,16},{16,0},{1,17},{17,1},{2,18},{18,2},{3,19},{19,3},{4,20},{20... | collective-permute-start | bytes 1572872 | tf_op jit(solution)/shard_map/ppermute | solution.py:366
  127.4 25.9 %collective-permute-start.14 = (bf16[512,512]{1,0:T(8,128)(2,1)}, bf16[512,512]{1,0:T(8,128)(2,1)S(1)}, u32[]{:S(2)}, u32[]{:S(2)}) collective-permute-start(bf16[512,512]{1,0:T(8,128)(2,1)} %slice.282), channel_id=1, source_target_pairs={{0,4},{4,0},{1,5},{5,1},{2,6},{6,2},{3,7},{7,3},{8,12},{12,8},{9,1... | collective-permute-start | bytes 1572872 | tf_op jit(solution)/shard_map/ppermute | solution.py:366
  129.5 22.6 %collective-permute-start.13 = (bf16[256,512]{1,0:T(8,128)(2,1)}, bf16[256,512]{1,0:T(8,128)(2,1)}, u32[]{:S(2)}, u32[]{:S(2)}) collective-permute-start(bf16[256,512]{1,0:T(8,128)(2,1)} %collective-permute-done.8), channel_id=1, source_target_pairs={{0,4},{4,0},{1,5},{5,1},{2,6},{6,2},{3,7},{7,3},{8,12},{12,8},{9,1... | collective-permute-start | bytes 786440 | tf_op jit(solution)/shard_map/ppermute | solution.py:366
  156.3 30.6 %all-to-all-start.3 = ((bf16[4,1024,128]{2,1,0:T(8,128)(2,1)}), bf16[4,1024,128]{2,1,0:T(8,128)(2,1)}, u32[]{:S(2)}, u32[]{:S(2)}) async-start(bf16[4,1024,128]{2,1,0:T(8,128)(2,1)} %bitcast.318), calls=%async_computation.3 | async-start | bytes 2097152 | tf_op jit(solution)/shard_map/all_to_all | solution.py:904
  160.5 124.3 %all-gather.9.cloned.1.call-start = ((), (), s32[]{:S(2)}) async-start(), calls=%async_computation.11 | async-start | bytes 4718592 | tf_op jit(solution)/shard_map/all_gather | solution.py:1130
  180.9 28.9 %collective-permute-start.17 = (bf16[2,128,2048]{2,1,0:T(8,128)(2,1)}, bf16[2,128,2048]{2,1,0:T(8,128)(2,1)S(1)}, u32[]{:S(2)}, u32[]{:S(2)}) collective-permute-start(bf16[2,128,2048]{2,1,0:T(8,128)(2,1)} %fusion.6), channel_id=1, source_target_pairs={{0,1},{1,0},{2,3},{3,2},{4,5},{5,4},{6,7},{7,6},{8,9},{9,8},{10,11... | collective-permute-start | bytes 3145736 | tf_op jit(solution)/shard_map/ppermute | solution.py:366
  183.5 26.3 %collective-permute-start.19 = (bf16[512,512]{1,0:T(8,128)(2,1)S(1)}, bf16[512,512]{1,0:T(8,128)(2,1)}, u32[]{:S(2)}, u32[]{:S(2)}) collective-permute-start(bf16[512,512]{1,0:T(8,128)(2,1)S(1)} %get-tuple-element.398.refs_4_.refs_12_), channel_id=1, source_target_pairs={{0,16},{16,0},{1,17},{17,1},{2,18},{18,2},{3,19},{19,3},{4,20},{20... | collective-permute-start | bytes 1572872 | tf_op jit(solution)/shard_map/ppermute | solution.py:366
  186.1 23.7 %collective-permute-start.18 = (bf16[512,512]{1,0:T(8,128)(2,1)S(1)}, bf16[512,512]{1,0:T(8,128)(2,1)S(1)}, u32[]{:S(2)}, u32[]{:S(2)}) collective-permute-start(bf16[512,512]{1,0:T(8,128)(2,1)S(1)} %get-tuple-element.398.refs_4_.refs_12_), channel_id=1, source_target_pairs={{0,4},{4,0},{1,5},{5,1},{2,6},{6,2},{3,7},{7,3},{8,12},{12,8},{9,1... | collective-permute-start | bytes 1572872 | tf_op jit(solution)/shard_map/ppermute | solution.py:366
  230.6 158.2 %all-gather.11.cloned.1.call-start = ((), (), s32[]{:S(2)}) async-start(), calls=%async_computation.12 | async-start | bytes 4718592 | tf_op jit(solution)/shard_map/all_gather | solution.py:1187
  232.5 24.5 %collective-permute-start.24 = (bf16[512,512]{1,0:T(8,128)(2,1)}, bf16[512,512]{1,0:T(8,128)(2,1)S(1)}, u32[]{:S(2)}, u32[]{:S(2)}) collective-permute-start(bf16[512,512]{1,0:T(8,128)(2,1)} %get-tuple-element.399), channel_id=1, source_target_pairs={{0,4},{4,0},{1,5},{5,1},{2,6},{6,2},{3,7},{7,3},{8,12},{12,8},{9,1... | collective-permute-start | bytes 1572872 | tf_op jit(solution)/shard_map/ppermute | solution.py:366
  233.8 25.1 %collective-permute-start.22 = (bf16[512,512]{1,0:T(8,128)(2,1)}, bf16[512,512]{1,0:T(8,128)(2,1)}, u32[]{:S(2)}, u32[]{:S(2)}) collective-permute-start(bf16[512,512]{1,0:T(8,128)(2,1)} %get-tuple-element.400), channel_id=1, source_target_pairs={{0,16},{16,0},{1,17},{17,1},{2,18},{18,2},{3,19},{19,3},{4,20},{20... | collective-permute-start | bytes 1572872 | tf_op jit(solution)/shard_map/ppermute | solution.py:366
  236.7 31.6 %collective-permute-start.27 = (bf16[512,512]{1,0:T(8,128)(2,1)S(1)}, bf16[512,512]{1,0:T(8,128)(2,1)}, u32[]{:S(2)}, u32[]{:S(2)}) collective-permute-start(bf16[512,512]{1,0:T(8,128)(2,1)S(1)} %copy-done.35), channel_id=1, source_target_pairs={{0,4},{4,0},{1,5},{5,1},{2,6},{6,2},{3,7},{7,3},{8,12},{12,8},{9,1... | collective-permute-start | bytes 1572872 | tf_op jit(solution)/shard_map/ppermute | solution.py:366
  259.8 25.0 %collective-permute-start.25 = (bf16[512,512]{1,0:T(8,128)(2,1)S(1)}, bf16[512,512]{1,0:T(8,128)(2,1)S(1)}, u32[]{:S(2)}, u32[]{:S(2)}) collective-permute-start(bf16[512,512]{1,0:T(8,128)(2,1)S(1)} %get-tuple-element.396.refs_4_), channel_id=1, source_target_pairs={{0,16},{16,0},{1,17},{17,1},{2,18},{18,2},{3,19},{19,3},{4,20},{20... | collective-permute-start | bytes 1572872 | tf_op jit(solution)/shard_map/ppermute | solution.py:366
  261.6 23.2 %collective-permute-start.26 = (bf16[512,512]{1,0:T(8,128)(2,1)}, bf16[512,512]{1,0:T(8,128)(2,1)S(1)}, u32[]{:S(2)}, u32[]{:S(2)}) collective-permute-start(bf16[512,512]{1,0:T(8,128)(2,1)} %collective-permute-done.22.refs_2_), channel_id=1, source_target_pairs={{0,4},{4,0},{1,5},{5,1},{2,6},{6,2},{3,7},{7,3},{8,12},{12,8},{9,1... | collective-permute-start | bytes 1572872 | tf_op jit(solution)/shard_map/ppermute | solution.py:366
  317.1 26.4 %collective-permute-start.34 = (bf16[1024,512]{1,0:T(8,128)(2,1)S(1)}, bf16[1024,512]{1,0:T(8,128)(2,1)S(1)}, u32[]{:S(2)}, u32[]{:S(2)}) collective-permute-start(bf16[1024,512]{1,0:T(8,128)(2,1)S(1)} %convolution_convert_fusion.3), channel_id=1, source_target_pairs={{0,4},{4,0},{1,5},{5,1},{2,6},{6,2},{3,7},{7,3},{8,12},{12,8},{9,1... | collective-permute-start | bytes 3145736 | tf_op jit(solution)/shard_map/ppermute | solution.py:366
  347.9 149.1 %reduce-scatter.2.cloned.1.call-start = ((), (), s32[]{:S(2)}) async-start(), calls=%async_computation.13 | async-start | bytes 4718592 | tf_op jit(solution)/shard_map/reduce_scatter | solution.py:1210
  348.2 23.9 %collective-permute-start.35 = (bf16[512,1024]{1,0:T(8,128)(2,1)}, bf16[512,1024]{1,0:T(8,128)(2,1)}, u32[]{:S(2)}, u32[]{:S(2)}) collective-permute-start(bf16[512,1024]{1,0:T(8,128)(2,1)} %convolution_convert_fusion.4), channel_id=1, source_target_pairs={{0,4},{4,0},{1,5},{5,1},{2,6},{6,2},{3,7},{7,3},{8,12},{12,8},{9,1... | collective-permute-start | bytes 3145736 | tf_op jit(solution)/shard_map/ppermute | solution.py:366
  362.0 23.3 %collective-permute-start.36 = (bf16[512,512]{1,0:T(8,128)(2,1)S(1)}, bf16[512,512]{1,0:T(8,128)(2,1)}, u32[]{:S(2)}, u32[]{:S(2)}) collective-permute-start(bf16[512,512]{1,0:T(8,128)(2,1)S(1)} %slice.305), channel_id=1, source_target_pairs={{0,16},{16,0},{1,17},{17,1},{2,18},{18,2},{3,19},{19,3},{4,20},{20... | collective-permute-start | bytes 1572872 | tf_op jit(solution)/shard_map/ppermute | solution.py:366
  388.9 28.0 %collective-permute-start.37 = (bf16[1024,512]{1,0:T(8,128)(2,1)}, bf16[1024,512]{1,0:T(8,128)(2,1)}, u32[]{:S(2)}, u32[]{:S(2)}) collective-permute-start(bf16[1024,512]{1,0:T(8,128)(2,1)} %convolution_convert_fusion.5), channel_id=1, source_target_pairs={{0,4},{4,0},{1,5},{5,1},{2,6},{6,2},{3,7},{7,3},{8,12},{12,8},{9,1... | collective-permute-start | bytes 3145736 | tf_op jit(solution)/shard_map/ppermute | solution.py:366
  396.6 29.1 %collective-permute-start.39 = (bf16[2,256,512]{2,1,0:T(8,128)(2,1)}, bf16[2,256,512]{2,1,0:T(8,128)(2,1)}, u32[]{:S(2)}, u32[]{:S(2)}) collective-permute-start(bf16[2,256,512]{2,1,0:T(8,128)(2,1)} %pad_maximum_fusion.6), channel_id=1, source_target_pairs={{0,4},{4,0},{1,5},{5,1},{2,6},{6,2},{3,7},{7,3},{8,12},{12,8},{9,1... | collective-permute-start | bytes 1572872 | tf_op jit(solution)/shard_map/ppermute | solution.py:366
  397.2 28.6 %collective-permute-start.38 = (bf16[512,512]{1,0:T(8,128)(2,1)}, bf16[512,512]{1,0:T(8,128)(2,1)}, u32[]{:S(2)}, u32[]{:S(2)}) collective-permute-start(bf16[512,512]{1,0:T(8,128)(2,1)} %slice.306), channel_id=1, source_target_pairs={{0,16},{16,0},{1,17},{17,1},{2,18},{18,2},{3,19},{19,3},{4,20},{20... | collective-permute-start | bytes 1572872 | tf_op jit(solution)/shard_map/ppermute | solution.py:366
  441.1 24.4 %collective-permute-start.43 = (bf16[512,768]{1,0:T(8,128)(2,1)}, bf16[512,768]{1,0:T(8,128)(2,1)}, u32[]{:S(2)}, u32[]{:S(2)}) collective-permute-start(bf16[512,768]{1,0:T(8,128)(2,1)} %convolution_convert_fusion.7), channel_id=1, source_target_pairs={{0,4},{4,0},{1,5},{5,1},{2,6},{6,2},{3,7},{7,3},{8,12},{12,8},{9,1... | collective-permute-start | bytes 2359304 | tf_op jit(solution)/shard_map/ppermute | solution.py:366
  442.7 76.7 %collective-permute-start.46 = (bf16[512,1024]{1,0:T(8,128)(2,1)}, bf16[512,1024]{1,0:T(8,128)(2,1)}, u32[]{:S(2)}, u32[]{:S(2)}) collective-permute-start(bf16[512,1024]{1,0:T(8,128)(2,1)} %add_convert_fusion.2), channel_id=1, source_target_pairs={{0,16},{16,0},{1,17},{17,1},{2,18},{18,2},{3,19},{19,3},{4,20},{20... | collective-permute-start | bytes 3145736 | tf_op jit(solution)/shard_map/ppermute | solution.py:366
  454.6 42.4 %collective-permute-start.41 = (bf16[2,64,2048]{2,1,0:T(8,128)(2,1)S(1)}, bf16[2,64,2048]{2,1,0:T(8,128)(2,1)}, u32[]{:S(2)}, u32[]{:S(2)}) collective-permute-start(bf16[2,64,2048]{2,1,0:T(8,128)(2,1)S(1)} %fusion.32), channel_id=1, source_target_pairs={{0,8},{8,0},{1,9},{9,1},{2,10},{10,2},{3,11},{11,3},{4,12},{12,4},... | collective-permute-start | bytes 1572872 | tf_op jit(solution)/shard_map/ppermute | solution.py:366
  455.5 41.6 %collective-permute-start.42 = (bf16[2,64,2048]{2,1,0:T(8,128)(2,1)S(1)}, bf16[2,64,2048]{2,1,0:T(8,128)(2,1)}, u32[]{:S(2)}, u32[]{:S(2)}) collective-permute-start(bf16[2,64,2048]{2,1,0:T(8,128)(2,1)S(1)} %fusion.34), channel_id=1, source_target_pairs={{0,1},{1,0},{2,3},{3,2},{4,5},{5,4},{6,7},{7,6},{8,9},{9,8},{10,11... | collective-permute-start | bytes 1572872 | tf_op jit(solution)/shard_map/ppermute | solution.py:366
  500.1 23.9 %collective-permute-start.47 = (bf16[256,512]{1,0:T(8,128)(2,1)}, bf16[256,512]{1,0:T(8,128)(2,1)}, u32[]{:S(2)}, u32[]{:S(2)}) collective-permute-start(bf16[256,512]{1,0:T(8,128)(2,1)} %fusion.1), channel_id=1, source_target_pairs={{0,16},{16,0},{1,17},{17,1},{2,18},{18,2},{3,19},{19,3},{4,20},{20... | collective-permute-start | bytes 786440 | tf_op jit(solution)/shard_map/ppermute | solution.py:366
  503.5 69.6 %collective-permute-start.52 = (bf16[512,768]{1,0:T(8,128)(2,1)}, bf16[512,768]{1,0:T(8,128)(2,1)}, u32[]{:S(2)}, u32[]{:S(2)}) collective-permute-start(bf16[512,768]{1,0:T(8,128)(2,1)} %convolution_convert_fusion.6), channel_id=1, source_target_pairs={{0,4},{4,0},{1,5},{5,1},{2,6},{6,2},{3,7},{7,3},{8,12},{12,8},{9,1... | collective-permute-start | bytes 2359304 | tf_op jit(solution)/shard_map/ppermute | solution.py:366
  510.2 38.4 %collective-permute-start.51 = (bf16[512,1024]{1,0:T(8,128)(2,1)}, bf16[512,1024]{1,0:T(8,128)(2,1)}, u32[]{:S(2)}, u32[]{:S(2)}) collective-permute-start(bf16[512,1024]{1,0:T(8,128)(2,1)} %convolution_convert_fusion.2), channel_id=1, source_target_pairs={{0,4},{4,0},{1,5},{5,1},{2,6},{6,2},{3,7},{7,3},{8,12},{12,8},{9,1... | collective-permute-start | bytes 3145736 | tf_op jit(solution)/shard_map/ppermute | solution.py:366
  531.9 22.7 %all-to-all-start.5 = ((bf16[4,1024,128]{2,1,0:T(8,128)(2,1)}), bf16[4,1024,128]{2,1,0:T(8,128)(2,1)S(1)}, u32[]{:S(2)}, u32[]{:S(2)}) async-start(bf16[4,1024,128]{2,1,0:T(8,128)(2,1)} %bitcast.306), calls=%async_computation.6 | async-start | bytes 2097152 | tf_op jit(solution)/shard_map/all_to_all | solution.py:904
  539.5 23.1 %collective-permute-start.50 = (bf16[32,2048]{1,0:T(8,128)(2,1)}, bf16[32,2048]{1,0:T(8,128)(2,1)S(1)}, u32[]{:S(2)}, u32[]{:S(2)}) collective-permute-start(bf16[32,2048]{1,0:T(8,128)(2,1)} %get-tuple-element.418), channel_id=1, source_target_pairs={{0,20},{4,16},{16,4},{20,0},{1,21},{5,17},{17,5},{21,1},{2,22},{6,... | collective-permute-start | bytes 393224 | tf_op jit(solution)/shard_map/ppermute | solution.py:917
  539.5 33.6 %collective-permute-start.49 = (bf16[32,2048]{1,0:T(8,128)(2,1)}, bf16[32,2048]{1,0:T(8,128)(2,1)}, u32[]{:S(2)}, u32[]{:S(2)}) collective-permute-start(bf16[32,2048]{1,0:T(8,128)(2,1)} %get-tuple-element.419), channel_id=1, source_target_pairs={{0,16},{16,0},{1,17},{17,1},{2,18},{18,2},{3,19},{19,3},{4,20},{20... | collective-permute-start | bytes 393224 | tf_op jit(solution)/shard_map/ppermute | solution.py:366
  543.1 30.0 %collective-permute-start.48 = (bf16[32,2048]{1,0:T(8,128)(2,1)}, bf16[32,2048]{1,0:T(8,128)(2,1)}, u32[]{:S(2)}, u32[]{:S(2)}) collective-permute-start(bf16[32,2048]{1,0:T(8,128)(2,1)} %get-tuple-element.420), channel_id=1, source_target_pairs={{0,4},{4,0},{1,5},{5,1},{2,6},{6,2},{3,7},{7,3},{8,12},{12,8},{9,1... | collective-permute-start | bytes 393224 | tf_op jit(solution)/shard_map/ppermute | solution.py:366
  548.5 40.9 %collective-permute-start.53 = (bf16[512,768]{1,0:T(8,128)(2,1)}, bf16[512,768]{1,0:T(8,128)(2,1)S(1)}, u32[]{:S(2)}, u32[]{:S(2)}) collective-permute-start(bf16[512,768]{1,0:T(8,128)(2,1)} %add_convert_fusion.5), channel_id=1, source_target_pairs={{0,16},{16,0},{1,17},{17,1},{2,18},{18,2},{3,19},{19,3},{4,20},{20... | collective-permute-start | bytes 2359304 | tf_op jit(solution)/shard_map/ppermute | solution.py:366
  555.5 35.7 %all-to-all-start.4 = ((bf16[4,128,1024]{2,1,0:T(8,128)(2,1)}), bf16[4,128,1024]{2,1,0:T(8,128)(2,1)S(1)}, u32[]{:S(2)}, u32[]{:S(2)}) async-start(bf16[4,128,1024]{2,1,0:T(8,128)(2,1)} %bitcast.94), calls=%async_computation.5 | async-start | bytes 2097152 | tf_op jit(solution)/shard_map/all_to_all | solution.py:904
  593.5 26.3 %all-to-all-start.6 = ((bf16[4,256,128]{2,1,0:T(8,128)(2,1)}), bf16[4,256,128]{2,1,0:T(8,128)(2,1)S(1)}, u32[]{:S(2)}, u32[]{:S(2)}) async-start(bf16[4,256,128]{2,1,0:T(8,128)(2,1)} %bitcast_bitcast_fusion.2), calls=%async_computation.7 | async-start | bytes 524288 | tf_op jit(solution)/shard_map/all_to_all | solution.py:904
  598.0 21.7 %collective-permute-start.54 = (bf16[4,32,2048]{2,1,0:T(8,128)(2,1)S(1)}, bf16[4,32,2048]{2,1,0:T(8,128)(2,1)}, u32[]{:S(2)}, u32[]{:S(2)}) collective-permute-start(bf16[4,32,2048]{2,1,0:T(8,128)(2,1)S(1)} %pad_maximum_fusion.7), channel_id=1, source_target_pairs={{0,1},{1,0},{2,3},{3,2},{4,5},{5,4},{6,7},{7,6},{8,9},{9,8},{10,11... | collective-permute-start | bytes 1572872 | tf_op jit(solution)/shard_map/ppermute | solution.py:366
  622.6 22.3 %all-to-all-start.7 = ((bf16[4,128,768]{2,1,0:T(8,128)(2,1)}), bf16[4,128,768]{2,1,0:T(8,128)(2,1)S(1)}, u32[]{:S(2)}, u32[]{:S(2)}) async-start(bf16[4,128,768]{2,1,0:T(8,128)(2,1)} %bitcast.119), calls=%async_computation.8 | async-start | bytes 1572864 | tf_op jit(solution)/shard_map/all_to_all | solution.py:904
  (106 other events, 943.9 us)
Sparse Core Ops, SparseCore 0:
  42.9 43.8 all-gather.4
  126.7 38.7 all-gather.6
  230.7 43.4 all-gather.8
  348.1 40.7 all-gather.10
  391.0 104.4 reduce-scatter.1
